TPU v7x, 256 devices: a whole 4x4x8 slice. The times are simulated.
256 devices in a mesh: space: 8 (over y, core), tm: 32 (over x, z).
Axes of the slice: x: 4, y: 4, z: 8, core: 2. Of those that a mesh axis runs over, the one named last changes fastest.
Arguments:
- snapshots: bfloat16 [8192, 32768], P('space', 'tm'), may hold values from -6 to 6
- basis: bfloat16 [8192, 64], P('space'), may hold values from -0.0625 to 0.0625
- lengths: int32 [16], replicated, may hold values from 1540 to 2048
Outputs:
- gram_matrix: float32 [2144, 2144], P('space')
- right_sides: float32 [2144, 64], P('space')
Inputs may be any that keep to these rules, and one draw needn't show every extreme that they name: lengths[k] snapshots of trajectory k are recorded; later positions of its slot of 2048 are padding.
All inputs are finite; a program needn't handle non-finite values.
Results may differ from a plain program's by a relative error of at most 0.0003.
Values sent between devices are 32-bit elements; how exact they have to be, the bound alone decides.
No kernel may reach another device: no remote copies, remote signals or barrier semaphores. Data moves between devices by JAX's collectives and lax.ppermute only.
A program may use at most 64 MiB of HBM per device.

v0:
```python
import jax
import jax.numpy as jnp
import numpy as np
from jax import lax
from jax.sharding import PartitionSpec as P

FEAT = 2144


EXACT = lax.Precision.HIGHEST


def extended(cells, sides, width):
    for axis, dim in sides:
        count = lax.axis_size(axis)
        ends = count - 1
        head = lax.slice_in_dim(cells, 0, width, axis=dim)
        tail = lax.slice_in_dim(cells, cells.shape[dim] - width, cells.shape[dim], axis=dim)
        cells = jnp.concatenate(
            [
                lax.ppermute(tail, axis, [(i, (i + 1) % count) for i in range(ends)]),
                cells,
                lax.ppermute(head, axis, [((i + 1) % count, i) for i in range(ends)]),
            ],
            axis=dim,
        )
    return cells


def selectors(modes_count):
    firsts, seconds = np.triu_indices(modes_count)
    modes = np.arange(modes_count)[:, None]
    pick_first = jnp.asarray((modes == firsts[None, :]).astype(np.float32))
    pick_second = jnp.asarray((modes == seconds[None, :]).astype(np.float32))
    return (pick_first, pick_second)


def features(block_rows):
    pick_first, pick_second = selectors(block_rows.shape[1])
    first = jnp.dot(block_rows, pick_first, precision=EXACT, preferred_element_type=jnp.float32)
    second = jnp.dot(block_rows, pick_second, precision=EXACT, preferred_element_type=jnp.float32)
    return jnp.concatenate([block_rows, first * second], axis=1)


def outer_rows(left_part, right_part):
    return jnp.einsum(
        "tf,tg->fg", left_part, right_part, precision=EXACT, preferred_element_type=jnp.float32
    )


def energy_sum(energy_part):
    return lax.psum(energy_part, ("space", "tm"))


def stencil(padded, width):
    return (
        padded[:, :width]
        - 8.0 * padded[:, 1 : width + 1]
        + 8.0 * padded[:, 3 : width + 3]
        - padded[:, 4:]
    ) / 12.0


def shards(snapshots, basis, lengths):
    partial_value = jnp.einsum("cr,ct->rt", basis, snapshots, preferred_element_type=jnp.float32)
    horizon = partial_value.shape[1]
    time_index = lax.axis_index("tm")
    cell_index = lax.axis_index("space")
    padded = extended(partial_value, (("tm", 1),), 2)
    change_part = stencil(padded, horizon)
    states, change = (
        lax.psum_scatter(partial_value, "space", scatter_dimension=1, tiled=True),
        lax.psum_scatter(change_part, "space", scatter_dimension=1, tiled=True),
    )
    share = states.shape[1]
    slot_width = 2 * horizon
    traj_count = lengths.shape[0]
    shifted = (
        time_index * horizon
        + cell_index * share
        + jnp.arange(share, dtype=jnp.int32)
        + horizon // 2
    )
    offsets = shifted % slot_width
    owners = shifted // slot_width % traj_count
    match = owners[:, None] == jnp.arange(traj_count, dtype=jnp.int32)[None, :]
    limits = jnp.sum(jnp.where(match, lengths[None, :], 0), axis=1)
    living = ((offsets >= 2) & (offsets <= limits - 3)).astype(jnp.float32)
    samples = jnp.sum(lengths - 4).astype(jnp.float32)
    masked = states * living[None, :]
    dmasked = change * living[None, :]
    energy_part = jnp.sum(masked * masked, axis=1)
    row_count = FEAT // lax.axis_size("space")
    scales = jnp.sqrt(energy_sum(energy_part) / samples + 1e-06)
    masked = masked / scales[:, None]
    dmasked = dmasked / scales[:, None]
    whole_states, whole_change = (
        lax.all_gather(masked, "space", axis=1, tiled=True),
        lax.all_gather(dmasked, "space", axis=1, tiled=True),
    )
    design = features(whole_states.T)
    picked = lax.dynamic_slice_in_dim(design, cell_index * row_count, row_count, 1)
    gram_part = outer_rows(picked, design)
    side_part = outer_rows(picked, whole_change.T)
    gram_part, side_part = lax.psum((gram_part, side_part), "tm")
    return (gram_part / samples, side_part / samples)


def solution(mesh):
    return jax.shard_map(
        shards,
        mesh=mesh,
        in_specs=(P("space", "tm"), P("space", None), P()),
        out_specs=(P("space", None), P("space", None)),
        check_vma=False,
    )
```

profile of v0, /device:TPU:8, one launch (start us, length us, event | category | flops | bytes accessed | tf_op | source)
XLA Modules:
  0.0 340.6 jit_solution(10435550340036665465)
XLA Ops:
  7.2 0.0 copy-start
  7.2 0.0 copy-start.2
  7.2 0.0 copy-start.4
  7.2 0.0 reduce-scatter.3.cloned.1.call-start
  7.2 1.5 copy-done
  8.8 2.1 fusion.14
  10.9 0.0 reduce-scatter.3.cloned.1.call-update
  10.9 0.0 reduce-scatter.5.cloned.1.call-start
  10.9 0.9 fusion.13
  11.8 3.8 %collective-permute-start = (f32[64,2]{1,0:T(8,128)S(1)}, f32[64,2]{1,0:T(8,128)S(1)}, u32[]{:S(2)}, u32[]{:S(2)}) collective-permute-start(f32[64,2]{1,0:T(8,128)S(1)} %get-tuple-element.4), channel_id=1, source_target_pairs={{0,1},{1,2},{2,3},{3,4},{4,5},{5,6},{6,7},{7,8},{8,9},{9,10},{10,1... | collective-permute-start | bytes 1544 | tf_op jit(solution)/shard_map/ppermute | solution.py:21
  15.6 1.3 collective-permute-start.1
  16.9 0.0 copy-done.4
  17.0 0.1 select_reduce_fusion
  17.0 0.6 add_reduce_fusion
  18.3 0.0 collective-permute-done
  18.3 3.1 collective-permute-done.1
  21.4 2.4 fusion.7
  23.8 0.0 reduce-scatter.5.cloned.1.call-update
  23.8 0.0 all-reduce.3.cloned.1.call-start
  23.9 20.7 %reduce-scatter.3.cloned.1.call-done = f32[64,128]{1,0:T(8,128)} async-done(((f32[64,1024]{1,0:T(8,128)}), f32[64,128]{1,0:T(8,128)}) %reduce-scatter.3.cloned.1.call-update) | async-done | bytes 32784 | tf_op jit(solution)/shard_map/reduce_scatter | solution.py:72
  44.5 0.9 multiply_reduce_fusion
  45.4 77.0 %psum.21 = f32[64]{0:T(128)S(1)} all-reduce(f32[64]{0:T(128)S(1)} %multiply_reduce_fusion), channel_id=1, replica_groups=mesh['space'=8,'tm'=32] {'space','tm'}, use_global_device_ids=true, to_apply=%region_3.4 | all-reduce | flops 64 | bytes 512 | tf_op jit(solution)/shard_map/psum | solution.py:52
  122.4 0.0 reduce-scatter.5.cloned.1.call-done
  122.4 0.9 multiply_divide_fusion
  123.3 12.9 %all_gather.6 = f32[64,1024]{1,0:T(8,128)S(1)} all-gather(f32[64,128]{1,0:T(8,128)S(1)} %get-tuple-element.7), channel_id=1, replica_groups=mesh['space'=8,'tm'=32] {'space'}, dimensions={1}, use_global_device_ids=true | all-gather | bytes 294912 | tf_op jit(solution)/shard_map/all_gather | solution.py:98
  136.2 0.0 copy-done.2
  136.2 0.0 copy-start.1
  136.2 7.0 %fusion.15 = f32[1024,2080]{0,1:T(8,128)S(1)} fusion(f32[64,1024]{1,0:T(8,128)S(1)} %all_gather.6, f32[64,2080]{1,0:T(8,128)S(1)} %copy-done.2), kind=kOutput, calls=%fused_computation.44 | convolution fusion | flops 1635778560 | bytes 9314304 | tf_op jit(solution)/shard_map/dot_general | solution.py:40
  143.1 0.0 copy-done.1
  143.2 7.3 %convolution_multiply_fusion = f32[1024,2080]{0,1:T(8,128)S(1)} fusion(f32[1024,2080]{0,1:T(8,128)S(1)} %fusion.15, f32[64,1024]{1,0:T(8,128)S(1)} %all_gather.6, f32[64,2080]{1,0:T(8,128)S(1)} %copy-done.1), kind=kOutput, calls=%fused_computation.5 | convolution fusion | flops 1637908480 | bytes 17833984 | tf_op jit(solution)/shard_map/dot_general | solution.py:41
  150.5 0.2 fusion.2
  150.7 9.9 %fusion = f32[268,2144]{1,0:T(8,128)} fusion(f32[1024,268]{0,1:T(8,128)S(1)} %fusion.2, f32[1024,64]{0,1:T(8,128)S(1)} %bitcast.11, f32[1024,2080]{0,1:T(8,128)S(1)} %convolution_multiply_fusion), kind=kOutput, calls=%fused_computation.2 | convolution fusion | flops 7062781952 | bytes 12177920 | tf_op jit(solution)/shard_map/tf,tg->fg/dot_general | solution.py:46
  160.6 12.9 %all_gather.7 = f32[64,1024]{1,0:T(8,128)S(1)} all-gather(f32[64,128]{1,0:T(8,128)S(1)} %get-tuple-element.6), channel_id=1, replica_groups=mesh['space'=8,'tm'=32] {'space'}, dimensions={1}, use_global_device_ids=true | all-gather | bytes 294912 | tf_op jit(solution)/shard_map/all_gather | solution.py:99
  173.5 1.9 fusion.16
  175.4 0.0 all-reduce.3.cloned.1.call-update
  175.4 154.8 %all-reduce.3.cloned.1.call-done = (f32[268,2144]{1,0:T(8,128)}, f32[268,64]{0,1:T(8,128)}) async-done(((f32[268,2144]{1,0:T(8,128)}, f32[268,64]{0,1:T(8,128)}), (f32[268,2144]{1,0:T(8,128)}, f32[268,64]{0,1:T(8,128)})) %all-reduce.3.cloned.1.call-update) | async-done | bytes 2366992 | tf_op jit(solution)/shard_map/psum | solution.py:105
  330.2 0.0 copy-start.3
  330.2 3.3 broadcast_divide_fusion
  333.5 0.0 copy-done.3
  333.5 0.7 broadcast_divide_fusion.1
  (3 shorter events, 0.0 us)
Async XLA Ops:
  7.2 1.6 copy-start
  7.2 129.0 %copy-start.2 = (f32[64,2080]{1,0:T(8,128)S(1)}, f32[64,2080]{1,0:T(8,128)}, u32[]{:S(2)}) copy-start(f32[64,2080]{1,0:T(8,128)} %constant.80.clone) | copy-start | bytes 1597444
  7.2 9.8 %copy-start.4 = (s32[16]{0:T(128)S(1)}, s32[16]{0:T(128)}, u32[]{:S(2)}) copy-start(s32[16]{0:T(128)} %param.7) | copy-start | bytes 196
  7.2 37.3 %reduce-scatter.3.cloned.1.call-start = ((), (), s32[]{:S(2)}) async-start(), calls=%async_computation.2 | async-start | bytes 294912 | tf_op jit(solution)/shard_map/reduce_scatter | solution.py:72
  10.9 111.5 %reduce-scatter.5.cloned.1.call-start = ((), (), s32[]{:S(2)}) async-start(), calls=%async_computation.3 | async-start | bytes 294912 | tf_op jit(solution)/shard_map/reduce_scatter | solution.py:73
  11.8 6.5 %collective-permute-start = (f32[64,2]{1,0:T(8,128)S(1)}, f32[64,2]{1,0:T(8,128)S(1)}, u32[]{:S(2)}, u32[]{:S(2)}) collective-permute-start(f32[64,2]{1,0:T(8,128)S(1)} %get-tuple-element.4), channel_id=1, source_target_pairs={{0,1},{1,2},{2,3},{3,4},{4,5},{5,6},{6,7},{7,8},{8,9},{9,10},{10,1... | collective-permute-start | bytes 1544 | tf_op jit(solution)/shard_map/ppermute | solution.py:21
  15.6 5.8 %collective-permute-start.1 = (f32[64,2]{1,0:T(8,128)S(1)}, f32[64,2]{1,0:T(8,128)S(1)}, u32[]{:S(2)}, u32[]{:S(2)}) collective-permute-start(f32[64,2]{1,0:T(8,128)S(1)} %get-tuple-element.5), channel_id=1, source_target_pairs={{1,0},{2,1},{3,2},{4,3},{5,4},{6,5},{7,6},{8,7},{9,8},{10,9},{11,1... | collective-permute-start | bytes 1544 | tf_op jit(solution)/shard_map/ppermute | solution.py:23
  23.8 306.4 %all-reduce.3.cloned.1.call-start = ((), (), s32[]{:S(2)}) async-start(), calls=%async_computation.4 | async-start | bytes 4931584 | tf_op jit(solution)/shard_map/psum | solution.py:105
  136.2 7.0 %copy-start.1 = (f32[64,2080]{1,0:T(8,128)S(1)}, f32[64,2080]{1,0:T(8,128)}, u32[]{:S(2)}) copy-start(f32[64,2080]{1,0:T(8,128)} %constant.81.clone) | copy-start | bytes 1597444
  330.2 3.3 copy-start.3
Sparse Core Ops, SparseCore 0:
  11.1 33.4 reduce-scatter.2
  47.0 32.4 reduce-scatter.4
  175.6 154.5 all-reduce.2
where the time goes:
time: 341 us
  waiting for transfers between devices  179 us (52%)
  blocking collectives  103 us (30%)
  matrix products  28.1 us (8%)
  between operations  14.5 us (4%)
  other arithmetic  8.98 us (3%)
  starting transfers between devices  5.23 us (2%)
    psum x1, waiting for transfers between devices, shards(): gram_part, side_part = lax.psum((gram_part, side_part), 'tm')  155 us
    psum x1, blocking collectives, energy_sum(): return lax.psum(energy_part, ('space', 'tm'))  77 us
    reduce_scatter x1, waiting for transfers between devices, shards(): lax.psum_scatter(partial_value, 'space', scatter_dimension=1, tiled=True)  20.7 us
    all_gather x1, blocking collectives, shards(): lax.all_gather(dmasked, 'space', axis=1, tiled=True)  12.9 us
    all_gather x1, blocking collectives, shards(): lax.all_gather(masked, 'space', axis=1, tiled=True)  12.9 us
    dot_general x2, matrix products, outer_rows(): jnp.einsum('tf,tg->fg', left_part, right_part, precision=EXACT, preferred...  11.8 us
    dot_general x1, matrix products, features(): jnp.dot(block_rows, pick_second, precision=EXACT, preferred_element_type=...  7.29 us
    dot_general x1, matrix products, features(): jnp.dot(block_rows, pick_first, precision=EXACT, preferred_element_type=j...  6.96 us
  transfers between devices with their start and end apart: 5, of which 3 were waited for; matrix products, arithmetic and copies ran while one was open for 1% of the time, Pallas kernels for 0%

commit v1 on v0

v1 whole, which is shorter than its diff:
```python
import functools

import jax
import jax.numpy as jnp
from jax import lax
from jax.experimental import pallas as pl
from jax.experimental.pallas import tpu as pltpu
from jax.sharding import Mesh, PartitionSpec as P

R = 64
FEAT = 2144
SLOT = 2048
TRAJ = 16
BLOCK = 1024
HALF = 512
ROWS = 268
ROWS_PAD = 272
COLS = 512
TAIL_QUADS = 96
TAIL_SIDES = 32
TAIL_ROWS = 144
PICKS = ROWS_PAD + COLS + TAIL_QUADS
TAIL_AT = 4 * ROWS_PAD
ENERGY_AT = TAIL_AT + TAIL_ROWS
PIECE = 160
TILES = 8 * PIECE
UP = 2.0**16


def swap(value):
    return lax.ppermute(value, "c", [(0, 1), (1, 0)])


def everyone(value, axis):
    count = lax.axis_size(axis)
    spread = jnp.broadcast_to(value[None], (count,) + value.shape)
    return lax.all_to_all(spread, axis, 0, 0, tiled=True)


def one_hots(first_feature, count):
    lane = lax.broadcasted_iota(jnp.int32, (count, 256), 1)
    feature = lax.broadcasted_iota(jnp.int32, (count, 256), 0) + first_feature
    mode = lane & (R - 1)
    below = lane < 3 * R
    ends = R + (mode + 1) * R - (mode + 1) * mode // 2
    passed = jnp.where((lane < R) & (feature >= ends), 1.0, 0.0)
    row = jnp.sum(passed, axis=1, keepdims=True).astype(jnp.int32)
    start = R + row * R - row * (row - 1) // 2
    linear = feature < R
    first = jnp.where(linear, feature, row)
    second = jnp.where(linear, -1, feature - start + row)
    pick_first = below & (mode == first)
    pick_second = (below & (mode == second)) | (linear & (lane == 3 * R))
    as_type = lambda pick: jnp.where(pick, 1.0, 0.0).astype(jnp.bfloat16)
    return as_type(pick_first), as_type(pick_second)


def split3(value):
    high = value.astype(jnp.bfloat16)
    rest = value - high.astype(jnp.float32)
    middle = rest.astype(jnp.bfloat16)
    low = (rest - middle.astype(jnp.float32)).astype(jnp.bfloat16)
    return high, middle, low


def split2(value):
    high = value.astype(jnp.bfloat16)
    return high, (value - high.astype(jnp.float32)).astype(jnp.bfloat16)


def dot(left, right, dims):
    return lax.dot_general(left, right, (dims, ((), ())), preferred_element_type=jnp.float32)


NT = ((1,), (1,))
NN = ((1,), (0,))


def gram_kernel(place, lengths, near, far, out, first_pick, second_pick, stack, change, rows_hi, rows_lo, cols_hi, cols_lo, acc, tail, energy):
    step = pl.program_id(0)
    last = pl.num_programs(0) - 1
    space, x, z = place[0], place[1], place[2]

    @pl.when(step == 0)
    def _():
        for at, count, feature in (
            (0, ROWS_PAD, space * ROWS),
            (ROWS_PAD, COLS, x * COLS),
            (ROWS_PAD + COLS, TAIL_QUADS, 4 * COLS),
        ):
            first, second = one_hots(feature, count)
            first_pick[at : at + count, :] = first
            second_pick[at : at + count, :] = second
        index = lax.broadcasted_iota(jnp.int32, (R, BLOCK), 0)
        stack[3 * R :, :] = jnp.where(index == 0, 1.0, 0.0).astype(jnp.bfloat16)
        acc[...] = jnp.zeros_like(acc)
        tail[...] = jnp.zeros_like(tail)
        energy[...] = jnp.zeros_like(energy)

    start = (step * 8 + z) * BLOCK
    states = jnp.concatenate([near[0, 0, :R, :], far[0, 0, :R, :]], axis=1) * UP
    ends = (near[0, 0, R:, :128] + far[0, 0, R:, :128]).T[:R, :] * UP
    lane = lax.broadcasted_iota(jnp.int32, (1, BLOCK), 1)
    position = (start + HALF) % SLOT
    one = lengths[(start + HALF) // SLOT % TRAJ]
    two = lengths[(start + 2 * HALF) // SLOT % TRAJ]
    offset = (position + lane) & (SLOT - 1)
    limit = jnp.where(lane < HALF, one, two) - 3
    living = jnp.where((offset >= 2) & (offset <= limit), 1.0, 0.0)
    wide = lax.broadcasted_iota(jnp.int32, (R, BLOCK), 1)
    before = jnp.where(wide == 0, ends[:, 1:2], pltpu.roll(states, 1, 1))
    before2 = jnp.where(wide == 0, ends[:, 0:1], jnp.where(wide == 1, ends[:, 1:2], pltpu.roll(states, 2, 1)))
    after = jnp.where(wide == BLOCK - 1, ends[:, 2:3], pltpu.roll(states, BLOCK - 1, 1))
    after2 = jnp.where(
        wide == BLOCK - 1, ends[:, 3:4], jnp.where(wide == BLOCK - 2, ends[:, 2:3], pltpu.roll(states, BLOCK - 2, 1))
    )
    change[...] = (before2 - 8.0 * before + 8.0 * after - after2) * (1.0 / 12.0) * living
    masked = states * living
    squares = masked * masked
    energy[...] += functools.reduce(lambda a, b: a + b, [squares[:, k * 128 : (k + 1) * 128] for k in range(BLOCK // 128)])
    high, middle, low = split3(masked)
    stack[:R, :] = high
    stack[R : 2 * R, :] = middle
    stack[2 * R : 3 * R, :] = low

    def features(at, count):
        first = dot(first_pick[at : at + count, :], stack[...], NN)
        second = dot(second_pick[at : at + count, :], stack[...], NN)
        return split2(first * second)

    rows_hi[...], rows_lo[...] = features(0, ROWS_PAD)
    for at in range(0, COLS, 256):
        cols_hi[at : at + 256, :], cols_lo[at : at + 256, :] = features(ROWS_PAD + at, 256)
    cols_hi[COLS : COLS + TAIL_QUADS, :], cols_lo[COLS : COLS + TAIL_QUADS, :] = features(ROWS_PAD + COLS, TAIL_QUADS)
    side = change[pl.ds(pl.multiple_of(x // 2 * TAIL_SIDES, TAIL_SIDES), TAIL_SIDES), :]
    cols_hi[COLS + TAIL_QUADS :, :], cols_lo[COLS + TAIL_QUADS :, :] = split2(side)

    for at in range(0, COLS, 256):
        left_hi, left_lo = rows_hi[...], rows_lo[...]
        right_hi, right_lo = cols_hi[at : at + 256, :], cols_lo[at : at + 256, :]
        acc[:, at : at + 256] += dot(left_hi, right_hi, NT) + (dot(left_hi, right_lo, NT) + dot(left_lo, right_hi, NT))
    part = pl.ds(pl.multiple_of(x % 2 * 128, 128), TAIL_ROWS)
    left_hi, left_lo = rows_hi[part, :], rows_lo[part, :]
    right_hi, right_lo = cols_hi[COLS:, :], cols_lo[COLS:, :]
    tail[...] += dot(left_hi, right_hi, NT) + (dot(left_hi, right_lo, NT) + dot(left_lo, right_hi, NT))

    @pl.when(step == last)
    def _():
        for k in range(COLS // 128):
            out[k * ROWS_PAD : (k + 1) * ROWS_PAD, :] = acc[:, k * 128 : (k + 1) * 128]
        out[TAIL_AT:ENERGY_AT, :] = tail[...]
        out[ENERGY_AT:, :] = jnp.zeros((TILES - ENERGY_AT, 128), jnp.float32)
        total = lax.dot_general(
            jnp.ones((8, 128), jnp.float32),
            energy[...],
            (NT, ((), ())),
            precision=lax.Precision.HIGHEST,
            preferred_element_type=jnp.float32,
        )
        out[ENERGY_AT : ENERGY_AT + 8, :R] = total


def gram(place, lengths, near, far):
    return pl.pallas_call(
        gram_kernel,
        out_shape=jax.ShapeDtypeStruct((TILES, 128), jnp.float32),
        grid_spec=pltpu.PrefetchScalarGridSpec(
            num_scalar_prefetch=2,
            grid=(4,),
            in_specs=[
                pl.BlockSpec((1, 1, R + 8, HALF), lambda i, *_: (0, i, 0, 0)),
                pl.BlockSpec((1, 1, R + 8, HALF), lambda i, *_: (0, i, 0, 0)),
            ],
            out_specs=pl.BlockSpec((TILES, 128), lambda i, *_: (0, 0)),
            scratch_shapes=[
                pltpu.VMEM((PICKS, 256), jnp.bfloat16),
                pltpu.VMEM((PICKS, 256), jnp.bfloat16),
                pltpu.VMEM((4 * R, BLOCK), jnp.bfloat16),
                pltpu.VMEM((R, BLOCK), jnp.float32),
                pltpu.VMEM((ROWS_PAD, BLOCK), jnp.bfloat16),
                pltpu.VMEM((ROWS_PAD, BLOCK), jnp.bfloat16),
                pltpu.VMEM((COLS + 128, BLOCK), jnp.bfloat16),
                pltpu.VMEM((COLS + 128, BLOCK), jnp.bfloat16),
                pltpu.VMEM((ROWS_PAD, COLS), jnp.float32),
                pltpu.VMEM((TAIL_ROWS, 128), jnp.float32),
                pltpu.VMEM((R, 128), jnp.float32),
            ],
        ),
        name="gram",
    )(place, lengths, near, far)


def scale_kernel(place, lengths, block, out):
    space, x = place[0], place[1]
    samples = lengths[0] - 4
    for k in range(1, TRAJ):
        samples += lengths[k] - 4
    samples = samples.astype(jnp.float32)
    energy = block[ENERGY_AT : ENERGY_AT + 8, :R] * (1.0 / (UP * UP))
    inverse = (1.0 / UP) / jnp.sqrt(energy / samples + 1e-06)
    high, middle, low = split3(inverse)
    fill = jnp.where(lax.broadcasted_iota(jnp.int32, (8, R), 1) == 0, 1.0, 0.0).astype(jnp.bfloat16)
    weights = jnp.concatenate([high.astype(jnp.float32), middle.astype(jnp.float32), low.astype(jnp.float32), fill.astype(jnp.float32)], axis=1)
    weights = weights.astype(jnp.bfloat16)
    tall = jnp.broadcast_to(weights[0:1, :].astype(jnp.float32), (128, 256)).astype(jnp.bfloat16)
    first, second = one_hots(space * ROWS, ROWS_PAD)
    row_weight = dot(first, tall, NT) * dot(second, tall, NT)
    by_row = row_weight / samples
    for k in range(COLS // 128):
        first, second = one_hots(x * COLS + k * 128, 128)
        column = (dot(weights, first, NT) * dot(weights, second, NT))[0:1, :]
        out[k * ROWS_PAD : (k + 1) * ROWS_PAD, :] = block[k * ROWS_PAD : (k + 1) * ROWS_PAD, :] * by_row * column
    first, second = one_hots(4 * COLS, TAIL_QUADS)
    quads = (dot(weights, first, NT) * dot(weights, second, NT))[0:1, :]
    low_sides, high_sides = inverse[0:1, :TAIL_SIDES], inverse[0:1, TAIL_SIDES:]
    sides = jnp.where(x < 2, low_sides, high_sides)
    column = jnp.concatenate([quads, sides], axis=1)
    tail_rows = jnp.where(x % 2 == 0, by_row[:TAIL_ROWS, :], by_row[128:, :])
    out[TAIL_AT:ENERGY_AT, :] = block[TAIL_AT:ENERGY_AT, :] * tail_rows * column
    out[ENERGY_AT:, :] = jnp.zeros((TILES - ENERGY_AT, 128), jnp.float32)


def scale(place, lengths, block):
    return pl.pallas_call(
        scale_kernel,
        out_shape=jax.ShapeDtypeStruct((TILES, 128), jnp.float32),
        grid_spec=pltpu.PrefetchScalarGridSpec(
            num_scalar_prefetch=2,
            grid=(1,),
            in_specs=[pl.BlockSpec((TILES, 128), lambda i, *_: (0, 0))],
            out_specs=pl.BlockSpec((TILES, 128), lambda i, *_: (0, 0)),
        ),
        name="scale",
    )(place, lengths, block)


def lay_kernel(parts, gram_out, side_out):
    for x in range(4):
        for k in range(4):
            lanes = (4 * x + k) * 128
            gram_out[:, lanes : lanes + 128] = parts[x, k * ROWS_PAD : k * ROWS_PAD + ROWS, :]
    split = 128
    for x, at, to in ((0, 0, 0), (1, 0, split)):
        count = split if x == 0 else ROWS - split
        gram_out[to : to + count, 16 * 128 :] = parts[x, TAIL_AT : TAIL_AT + count, :TAIL_QUADS]
        side_out[to : to + count, :TAIL_SIDES] = parts[x, TAIL_AT : TAIL_AT + count, TAIL_QUADS:]
        side_out[to : to + count, TAIL_SIDES:] = parts[x + 2, TAIL_AT : TAIL_AT + count, TAIL_QUADS:]


def lay(parts):
    return pl.pallas_call(
        lay_kernel,
        out_shape=(
            jax.ShapeDtypeStruct((ROWS, FEAT), jnp.float32),
            jax.ShapeDtypeStruct((ROWS, R), jnp.float32),
        ),
        name="lay",
    )(parts)


def shards(snapshots, basis, lengths):
    core, x, z = lax.axis_index("c"), lax.axis_index("x"), lax.axis_index("z")
    space = lax.axis_index("y") * 2 + core
    place = jnp.stack([space, x, z, core]).astype(jnp.int32)
    partial = jnp.einsum("cr,ct->rt", basis, snapshots, preferred_element_type=jnp.float32)
    head = partial[:, :2].T
    tail = partial[:, BLOCK - 2 :].T
    left = lax.ppermute(tail, ("x", "z"), [(i, i + 1) for i in range(31)])
    right = lax.ppermute(head, ("x", "z"), [(i + 1, i) for i in range(31)])
    mine = lax.dynamic_slice_in_dim(partial, core * HALF, HALF, 1)
    other = lax.dynamic_slice_in_dim(partial, (1 - core) * HALF, HALF, 1)
    half = mine + swap(other)
    ends = jnp.pad(jnp.concatenate([left, right], axis=0), ((0, 4), (0, HALF - R)))
    message = jnp.sum(everyone(jnp.concatenate([half, ends], axis=0), "y").reshape(4, R + 8, HALF), axis=0)
    own = everyone(message, "x").reshape(4, R + 8, HALF)
    theirs = swap(own)
    near = jnp.where(core == 0, own, theirs)[None]
    far = jnp.where(core == 0, theirs, own)[None]
    block = gram(place, lengths, near, far)
    piece = jnp.sum(lax.all_to_all(block.reshape(8, PIECE, 128), "z", 0, 0, tiled=True), axis=0)
    block = everyone(piece, "z").reshape(TILES, 128)
    block = scale(place, lengths, block)
    parts = everyone(block, "x").reshape(4, TILES, 128)
    return lay(parts)


def solution(mesh):
    grid = Mesh(mesh.devices.reshape(4, 2, 4, 8), ("y", "c", "x", "z"))
    return jax.shard_map(
        shards,
        mesh=grid,
        in_specs=(P(("y", "c"), ("x", "z")), P(("y", "c"), None), P()),
        out_specs=(P(("y", "c"), None), P(("y", "c"), None)),
        check_vma=False,
    )
```

time: 341 us -> 151 us (0.44)
  waiting for transfers between devices: 179 us -> 5.83 us
  matrix products: 28.1 us -> 1.38 us
  Pallas kernels: 0 us -> 20.4 us
  between operations: 14.5 us -> 0.76 us
  other arithmetic: 8.98 us -> 1.91 us
  blocking collectives: 103 us -> 110 us
    psum x1 -> x0, waiting for transfers between devices: 155 us -> none  [shards(): gram_part, side_part = lax.psum((gram_part, side_part), 'tm')]
    all_to_all x0 -> x5, blocking collectives: none -> 110 us  [the longest x4 83.3 us: everyone(): return lax.all_to_all(spread, axis, 0, 0, tiled=True)]
    psum x1 -> x0, blocking collectives: 77 us -> none  [energy_sum(): return lax.psum(energy_part, ('space', 'tm'))]
    dot_general x4 -> x0, matrix products: 26.1 us -> none  [the longest x2 11.8 us: outer_rows(): jnp.einsum('tf,tg->fg', left_part, right_part, precision=EXACT, preferred...]
    all_gather x2 -> x0, blocking collectives: 25.8 us -> none  [the longest x1 12.9 us: shards(): lax.all_gather(dmasked, 'space', axis=1, tiled=True)]
    reduce_scatter x2 -> x0, waiting for transfers between devices: 20.7 us -> none  [the longest x1 20.7 us: shards(): lax.psum_scatter(partial_value, 'space', scatter_dimension=1, tiled=True)]
    pallas_call x0 -> x3, Pallas kernels: none -> 20.4 us  [the longest x1 13.6 us: gram(): pl.pallas_call(gram_kernel, out_shape=jax.ShapeDtypeStruct((TILES, 128),...]
    div x4 -> x0, other arithmetic: 7.15 us -> none  [the longest x2 3.92 us: shards(): return (gram_part / samples, side_part / samples)]
  transfers between devices with their start and end apart: 5 -> 4, of which waited for: 3 -> 3; matrix products, arithmetic and copies ran while one was open for 1% -> 1% of each run, Pallas kernels for 0% -> 0%
where the time goes in v1:
time: 151 us; the launch traced here: 150 us
  blocking collectives  110 us (73%)
  Pallas kernels  20.4 us (14%)
  waiting for transfers between devices  5.83 us (4%)
  starting transfers between devices  5.2 us (3%)
  local copies, waits for them, and re-layouts  4.9 us (3%)
  other arithmetic  1.91 us (1%)
    all_to_all x4, blocking collectives, everyone(): return lax.all_to_all(spread, axis, 0, 0, tiled=True)  83.3 us
    all_to_all x1, blocking collectives, shards(): lax.all_to_all(block.reshape(8, PIECE, 128), 'z', 0, 0, tiled=True)  26.6 us
    pallas_call x1, Pallas kernels, gram(): pl.pallas_call(gram_kernel, out_shape=jax.ShapeDtypeStruct((TILES, 128),...  13.6 us
    ppermute x1, waiting for transfers between devices, shards(): right = lax.ppermute(head, ('x', 'z'), [(i + 1, i) for i in range(31)])  4.16 us
    ppermute x1, starting transfers between devices, shards(): left = lax.ppermute(tail, ('x', 'z'), [(i, i + 1) for i in range(31)])  3.81 us
    pallas_call x1, Pallas kernels, scale(): pl.pallas_call(scale_kernel, out_shape=jax.ShapeDtypeStruct((TILES, 128),...  3.42 us
    pallas_call x1, Pallas kernels, lay(): pl.pallas_call(lay_kernel, out_shape=(jax.ShapeDtypeStruct((ROWS, FEAT),...  3.34 us
  transfers between devices with their start and end apart: 4, of which 3 were waited for; matrix products, arithmetic and copies ran while one was open for 1% of the time, Pallas kernels for 0%

profile of v1, /device:TPU:8, one launch (start us, length us, event | category | flops | bytes accessed | tf_op | source)
XLA Modules:
  0.0 150.2 jit_solution(5121255263144830745)
XLA Ops:
  0.6 0.0 copy-start
  0.7 1.6 %copy-done = bf16[1024,1024]{1,0:T(8,128)(2,1)S(1)} copy-done((bf16[1024,1024]{1,0:T(8,128)(2,1)S(1)}, bf16[1024,1024]{1,0:T(8,128)(2,1)}, u32[]{:S(2)}) %copy-start) | copy-done | bytes 2097176
  2.2 1.4 fusion
  3.6 0.1 collective-permute-start
  3.7 0.1 slice_bitcast_fusion.1
  3.8 3.8 %collective-permute-start.1 = (f32[2,64]{0,1:T(8,128)S(1)}, f32[2,64]{0,1:T(8,128)S(1)}, u32[]{:S(2)}, u32[]{:S(2)}) collective-permute-start(f32[2,64]{0,1:T(8,128)S(1)} %get-tuple-element.10), channel_id=1, source_target_pairs={{0,1},{1,2},{2,3},{3,4},{4,5},{5,6},{6,7},{7,8},{8,9},{9,10},{10,1... | collective-permute-start | bytes 1544 | tf_op jit(solution)/shard_map/ppermute | solution.py:268
  7.6 1.3 collective-permute-start.2
  8.9 0.3 collective-permute-done.1
  9.2 0.1 copy.10
  9.3 4.2 %collective-permute-done.2 = f32[2,64]{0,1:T(8,128)S(1)} collective-permute-done((f32[2,64]{0,1:T(8,128)S(1)}, f32[2,64]{0,1:T(8,128)S(1)}, u32[]{:S(2)}, u32[]{:S(2)}) %collective-permute-start.2) | collective-permute-done | bytes 544 | tf_op jit(solution)/shard_map/ppermute | solution.py:269
  13.4 0.1 copy.11
  13.5 0.0 collective-permute-done
  13.6 0.1 broadcast_in_dim.12
  13.7 12.8 %all_to_all.25 = f32[4,72,512]{2,1,0:T(8,128)S(1)} all-to-all(f32[4,72,512]{2,1,0:T(8,128)S(1)} %broadcast_in_dim.12), channel_id=1, replica_groups=mesh['y'=4,'c'=2,'x'=4,'z'=8] {'y'}, dimensions={0} | all-to-all | bytes 1179648 | tf_op jit(solution)/shard_map/all_to_all | solution.py:37
  26.6 0.1 broadcast_in_dim.13
  26.6 14.7 %all_to_all.26 = f32[4,72,512]{2,1,0:T(8,128)S(1)} all-to-all(f32[4,72,512]{2,1,0:T(8,128)S(1)} %broadcast_in_dim.13), channel_id=1, replica_groups=mesh['y'=4,'c'=2,'x'=4,'z'=8] {'x'}, dimensions={0} | all-to-all | bytes 1179648 | tf_op jit(solution)/shard_map/all_to_all | solution.py:37
  41.3 0.0 collective-permute-start.3
  41.3 0.6 pad_add_fusion.place
  41.9 1.4 collective-permute-done.3
  43.3 1.2 select_bitcast_fusion
  44.5 13.6 %gram.1 = f32[1280,128]{1,0:T(8,128)} custom-call(s32[4]{0:T(128)} %pad_add_fusion.place, s32[16]{0:T(128)} %lengths.3, f32[1,4,72,512]{3,2,1,0:T(8,128)} %get-tuple-element.9.near, f32[1,4,72,512]{3,2,1,0:T(8,128)} %get-tuple-element.8.far), custom_call_target="tpu_custom_call" | custom-call | tf_op jit(solution)/shard_map/gram/pallas_call | solution.py:164
  58.1 26.6 %all_to_all.27 = f32[8,160,128]{2,1,0:T(8,128)S(1)} all-to-all(f32[8,160,128]{2,1,0:T(8,128)} %bitcast.16), channel_id=1, replica_groups=mesh['y'=4,'c'=2,'x'=4,'z'=8] {'z'}, dimensions={0} | all-to-all | bytes 1310720 | tf_op jit(solution)/shard_map/all_to_all | solution.py:280
  84.8 22.6 %all_to_all.28 = f32[8,160,128]{2,1,0:T(8,128)} all-to-all(f32[8,160,128]{2,1,0:T(8,128)S(1)} %broadcast_in_dim.16), channel_id=1, replica_groups=mesh['y'=4,'c'=2,'x'=4,'z'=8] {'z'}, dimensions={0} | all-to-all | bytes 1310720 | tf_op jit(solution)/shard_map/all_to_all | solution.py:37
  107.4 3.4 %scale.1 = f32[1280,128]{1,0:T(8,128)} custom-call(s32[4]{0:T(128)} %pad_add_fusion.place, s32[16]{0:T(128)} %lengths.3, f32[1280,128]{1,0:T(8,128)} %bitcast.17), custom_call_target="tpu_custom_call" | custom-call | tf_op jit(solution)/shard_map/scale/pallas_call | solution.py:224
  110.8 1.3 broadcast_in_dim.17
  112.1 33.2 %all_to_all.29.parts = f32[4,1280,128]{2,1,0:T(8,128)} all-to-all(f32[4,1280,128]{2,1,0:T(8,128)S(1)} %broadcast_in_dim.17), channel_id=1, replica_groups=mesh['y'=4,'c'=2,'x'=4,'z'=8] {'x'}, dimensions={0} | all-to-all | bytes 5242880 | tf_op jit(solution)/shard_map/all_to_all | solution.py:37
  145.2 3.3 %lay.1 = (f32[268,2144]{1,0:T(8,128)}, f32[268,64]{1,0:T(8,128)}) custom-call(f32[4,1280,128]{2,1,0:T(8,128)} %all_to_all.29.parts), custom_call_target="tpu_custom_call" | custom-call | tf_op jit(solution)/shard_map/lay/pallas_call | solution.py:251
  148.6 1.7 %copy.12 = f32[268,64]{0,1:T(8,128)} copy(f32[268,64]{1,0:T(8,128)} %get-tuple-element.7) | data formatting | bytes 137216 | tf_op jit(solution)/shard_map/lay/pallas_call | solution.py:251
  (7 shorter events, 0.2 us)
Async XLA Ops:
  0.6 1.6 %copy-start = (bf16[1024,1024]{1,0:T(8,128)(2,1)S(1)}, bf16[1024,1024]{1,0:T(8,128)(2,1)}, u32[]{:S(2)}) copy-start(bf16[1024,1024]{1,0:T(8,128)(2,1)} %param.3) | copy-start | bytes 6291460
  3.6 9.9 %collective-permute-start = (f32[64,512]{1,0:T(8,128)S(1)}, f32[64,512]{1,0:T(8,128)S(1)}, u32[]{:S(2)}, u32[]{:S(2)}) collective-permute-start(f32[64,512]{1,0:T(8,128)S(1)} %constant_dynamic-slice_fusion), channel_id=1, source_target_pairs={{0,32},{32,0},{1,33},{33,1},{2,34},{34,2},{3,35},{35,3},{4,36},{36... | collective-permute-start | bytes 393224 | tf_op jit(solution)/shard_map/ppermute | solution.py:31
  3.8 5.4 %collective-permute-start.1 = (f32[2,64]{0,1:T(8,128)S(1)}, f32[2,64]{0,1:T(8,128)S(1)}, u32[]{:S(2)}, u32[]{:S(2)}) collective-permute-start(f32[2,64]{0,1:T(8,128)S(1)} %get-tuple-element.10), channel_id=1, source_target_pairs={{0,1},{1,2},{2,3},{3,4},{4,5},{5,6},{6,7},{7,8},{8,9},{9,10},{10,1... | collective-permute-start | bytes 1544 | tf_op jit(solution)/shard_map/ppermute | solution.py:268
  7.6 5.8 %collective-permute-start.2 = (f32[2,64]{0,1:T(8,128)S(1)}, f32[2,64]{0,1:T(8,128)S(1)}, u32[]{:S(2)}, u32[]{:S(2)}) collective-permute-start(f32[2,64]{0,1:T(8,128)S(1)} %get-tuple-element.11), channel_id=1, source_target_pairs={{1,0},{2,1},{3,2},{4,3},{5,4},{6,5},{7,6},{8,7},{9,8},{10,9},{11,1... | collective-permute-start | bytes 1544 | tf_op jit(solution)/shard_map/ppermute | solution.py:269
  41.3 2.0 %collective-permute-start.3 = (f32[4,72,512]{2,1,0:T(8,128)S(1)}, f32[4,72,512]{2,1,0:T(8,128)S(1)}, u32[]{:S(2)}, u32[]{:S(2)}) collective-permute-start(f32[4,72,512]{2,1,0:T(8,128)S(1)} %all_to_all.26), channel_id=1, source_target_pairs={{0,32},{32,0},{1,33},{33,1},{2,34},{34,2},{3,35},{35,3},{4,36},{36... | collective-permute-start | bytes 1769480 | tf_op jit(solution)/shard_map/ppermute | solution.py:31

commit v2 on v1

v2 whole, which is shorter than its diff:
```python
import functools

import jax
import jax.numpy as jnp
from jax import lax
from jax.experimental import pallas as pl
from jax.experimental.pallas import tpu as pltpu
from jax.sharding import Mesh, PartitionSpec as P

R = 64
FEAT = 2144
SLOT = 2048
TRAJ = 16
BLOCK = 1024
HALF = 512
ROWS = 268
ROWS_PAD = 272
COLS = 512
TAIL_QUADS = 96
TAIL_SIDES = 32
TAIL_ROWS = 144
PICKS = ROWS_PAD + COLS + TAIL_QUADS
TAIL_AT = 4 * ROWS_PAD
ENERGY_AT = TAIL_AT + TAIL_ROWS
PIECE = 160
TILES = 8 * PIECE
UP = 2.0**16


def swap(value):
    return lax.ppermute(value, "c", [(0, 1), (1, 0)])


def turn(value, axis, by):
    count = lax.axis_size(axis)
    return lax.ppermute(value, axis, [(i, (i + by) % count) for i in range(count)])


def near_by(value):
    return pltpu.with_memory_space_constraint(value, pltpu.VMEM)


def everyone(value, axis):
    count = lax.axis_size(axis)
    spread = jnp.broadcast_to(value[None], (count,) + value.shape)
    return lax.all_to_all(spread, axis, 0, 0, tiled=True)


def one_hots(first_feature, count):
    lane = lax.broadcasted_iota(jnp.int32, (count, 256), 1)
    feature = lax.broadcasted_iota(jnp.int32, (count, 256), 0) + first_feature
    mode = lane & (R - 1)
    below = lane < 3 * R
    ends = R + (mode + 1) * R - (mode + 1) * mode // 2
    passed = jnp.where((lane < R) & (feature >= ends), 1.0, 0.0)
    row = jnp.sum(passed, axis=1, keepdims=True).astype(jnp.int32)
    start = R + row * R - row * (row - 1) // 2
    linear = feature < R
    first = jnp.where(linear, feature, row)
    second = jnp.where(linear, -1, feature - start + row)
    pick_first = below & (mode == first)
    pick_second = (below & (mode == second)) | (linear & (lane == 3 * R))
    as_type = lambda pick: jnp.where(pick, 1.0, 0.0).astype(jnp.bfloat16)
    return as_type(pick_first), as_type(pick_second)


def split3(value):
    high = value.astype(jnp.bfloat16)
    rest = value - high.astype(jnp.float32)
    middle = rest.astype(jnp.bfloat16)
    low = (rest - middle.astype(jnp.float32)).astype(jnp.bfloat16)
    return high, middle, low


def split2(value):
    high = value.astype(jnp.bfloat16)
    return high, (value - high.astype(jnp.float32)).astype(jnp.bfloat16)


def dot(left, right, dims):
    return lax.dot_general(left, right, (dims, ((), ())), preferred_element_type=jnp.float32)


NT = ((1,), (1,))
NN = ((1,), (0,))


def pick_kernel(place, first_pick, second_pick):
    space, x = place[0], place[1]
    for at, count, feature in (
        (0, ROWS_PAD, space * ROWS),
        (ROWS_PAD, COLS, x * COLS),
        (ROWS_PAD + COLS, TAIL_QUADS, 4 * COLS),
    ):
        first, second = one_hots(feature, count)
        first_pick[at : at + count, :] = first
        second_pick[at : at + count, :] = second


SMEM = pl.BlockSpec(memory_space=pltpu.SMEM)
VMEM = pl.BlockSpec(memory_space=pltpu.VMEM)


def picks(place):
    return pl.pallas_call(
        pick_kernel,
        out_shape=(pltpu.VMEM((PICKS, 256), jnp.bfloat16), pltpu.VMEM((PICKS, 256), jnp.bfloat16)),
        in_specs=[SMEM],
        out_specs=(VMEM, VMEM),
        name="picks",
    )(place)


def gram_kernel(place, lengths, first_pick, second_pick, *rest):
    mine, theirs = rest[:4], rest[4:8]
    out, stack, change, rows_hi, rows_lo, cols_hi, cols_lo, acc, tail, energy = rest[8:]
    x, z, core = place[1], place[2], place[3]
    index = lax.broadcasted_iota(jnp.int32, (R, BLOCK), 0)
    stack[3 * R :, :] = jnp.where(index == 0, 1.0, 0.0).astype(jnp.bfloat16)
    lane = lax.broadcasted_iota(jnp.int32, (1, BLOCK), 1)
    wide = lax.broadcasted_iota(jnp.int32, (R, BLOCK), 1)

    def features(at, count):
        first = dot(first_pick[at : at + count, :], stack[...], NN)
        second = dot(second_pick[at : at + count, :], stack[...], NN)
        return split2(first * second)

    for step in range(4):
        start = ((x + step) % 4 * 8 + z) * BLOCK
        own, other = mine[step], theirs[step]
        near = jnp.where(core == 0, own[:R, :], other[:R, :])
        far = jnp.where(core == 0, other[:R, :], own[:R, :])
        states = jnp.concatenate([near, far], axis=1) * UP
        ends = (own[R:, :128] + other[R:, :128]).T[:R, :] * UP
        position = (start + HALF) % SLOT
        one = lengths[(start + HALF) // SLOT % TRAJ]
        two = lengths[(start + 2 * HALF) // SLOT % TRAJ]
        offset = (position + lane) & (SLOT - 1)
        limit = jnp.where(lane < HALF, one, two) - 3
        living = jnp.where((offset >= 2) & (offset <= limit), 1.0, 0.0)
        before = jnp.where(wide == 0, ends[:, 1:2], pltpu.roll(states, 1, 1))
        before2 = jnp.where(wide == 0, ends[:, 0:1], jnp.where(wide == 1, ends[:, 1:2], pltpu.roll(states, 2, 1)))
        after = jnp.where(wide == BLOCK - 1, ends[:, 2:3], pltpu.roll(states, BLOCK - 1, 1))
        after2 = jnp.where(
            wide == BLOCK - 1, ends[:, 3:4], jnp.where(wide == BLOCK - 2, ends[:, 2:3], pltpu.roll(states, BLOCK - 2, 1))
        )
        change[...] = (before2 - 8.0 * before + 8.0 * after - after2) * (1.0 / 12.0) * living
        masked = states * living
        squares = masked * masked
        square = functools.reduce(lambda a, b: a + b, [squares[:, k * 128 : (k + 1) * 128] for k in range(BLOCK // 128)])
        energy[...] = square if step == 0 else energy[...] + square
        stack[:R, :], stack[R : 2 * R, :], stack[2 * R : 3 * R, :] = split3(masked)

        rows_hi[...], rows_lo[...] = features(0, ROWS_PAD)
        for at in range(0, COLS, 256):
            cols_hi[at : at + 256, :], cols_lo[at : at + 256, :] = features(ROWS_PAD + at, 256)
        cols_hi[COLS : COLS + TAIL_QUADS, :], cols_lo[COLS : COLS + TAIL_QUADS, :] = features(ROWS_PAD + COLS, TAIL_QUADS)
        side = change[pl.ds(pl.multiple_of(x // 2 * TAIL_SIDES, TAIL_SIDES), TAIL_SIDES), :]
        cols_hi[COLS + TAIL_QUADS :, :], cols_lo[COLS + TAIL_QUADS :, :] = split2(side)

        for at in range(0, COLS, 256):
            left_hi, left_lo = rows_hi[...], rows_lo[...]
            right_hi, right_lo = cols_hi[at : at + 256, :], cols_lo[at : at + 256, :]
            total = dot(left_hi, right_hi, NT) + (dot(left_hi, right_lo, NT) + dot(left_lo, right_hi, NT))
            acc[:, at : at + 256] = total if step == 0 else acc[:, at : at + 256] + total
        part = pl.ds(pl.multiple_of(x % 2 * 128, 128), TAIL_ROWS)
        left_hi, left_lo = rows_hi[part, :], rows_lo[part, :]
        right_hi, right_lo = cols_hi[COLS:, :], cols_lo[COLS:, :]
        total = dot(left_hi, right_hi, NT) + (dot(left_hi, right_lo, NT) + dot(left_lo, right_hi, NT))
        tail[...] = total if step == 0 else tail[...] + total

    for k in range(COLS // 128):
        out[k * ROWS_PAD : (k + 1) * ROWS_PAD, :] = acc[:, k * 128 : (k + 1) * 128]
    out[TAIL_AT:ENERGY_AT, :] = tail[...]
    out[ENERGY_AT:, :] = jnp.zeros((TILES - ENERGY_AT, 128), jnp.float32)
    out[ENERGY_AT : ENERGY_AT + 8, :R] = lax.dot_general(
        jnp.ones((8, 128), jnp.float32),
        energy[...],
        (NT, ((), ())),
        precision=lax.Precision.HIGHEST,
        preferred_element_type=jnp.float32,
    )


def gram(place, lengths, first_pick, second_pick, mine, theirs):
    return pl.pallas_call(
        gram_kernel,
        out_shape=pltpu.VMEM((TILES, 128), jnp.float32),
        in_specs=[SMEM, SMEM] + [VMEM] * 10,
        out_specs=VMEM,
        scratch_shapes=[
            pltpu.VMEM((4 * R, BLOCK), jnp.bfloat16),
            pltpu.VMEM((R, BLOCK), jnp.float32),
            pltpu.VMEM((ROWS_PAD, BLOCK), jnp.bfloat16),
            pltpu.VMEM((ROWS_PAD, BLOCK), jnp.bfloat16),
            pltpu.VMEM((COLS + 128, BLOCK), jnp.bfloat16),
            pltpu.VMEM((COLS + 128, BLOCK), jnp.bfloat16),
            pltpu.VMEM((ROWS_PAD, COLS), jnp.float32),
            pltpu.VMEM((TAIL_ROWS, 128), jnp.float32),
            pltpu.VMEM((R, 128), jnp.float32),
        ],
        name="gram",
    )(place, lengths, *[near_by(v) for v in (first_pick, second_pick, *mine, *theirs)])


def scale_kernel(place, lengths, first_pick, second_pick, block, out):
    x = place[1]
    samples = lengths[0] - 4
    for k in range(1, TRAJ):
        samples += lengths[k] - 4
    samples = samples.astype(jnp.float32)
    energy = block[ENERGY_AT : ENERGY_AT + 8, :R] * (1.0 / (UP * UP))
    inverse = (1.0 / UP) / jnp.sqrt(energy / samples + 1e-06)
    high, middle, low = [part.astype(jnp.float32) for part in split3(inverse)]
    fill = jnp.where(lax.broadcasted_iota(jnp.int32, (8, R), 1) == 0, 1.0, 0.0)
    weights = jnp.concatenate([high, middle, low, fill], axis=1)
    tall = jnp.broadcast_to(weights[0:1, :], (128, 256)).astype(jnp.bfloat16)
    weights = weights.astype(jnp.bfloat16)
    by_row = dot(first_pick[:ROWS_PAD, :], tall, NT) * dot(second_pick[:ROWS_PAD, :], tall, NT) / samples
    by_column = (dot(weights, first_pick[ROWS_PAD:, :], NT) * dot(weights, second_pick[ROWS_PAD:, :], NT))[0:1, :]
    for k in range(COLS // 128):
        rows = slice(k * ROWS_PAD, (k + 1) * ROWS_PAD)
        out[rows, :] = block[rows, :] * by_row * by_column[:, k * 128 : (k + 1) * 128]
    sides = jnp.where(x < 2, inverse[0:1, :TAIL_SIDES], inverse[0:1, TAIL_SIDES:])
    column = jnp.concatenate([by_column[:, COLS:], sides], axis=1)
    tail_rows = jnp.where(x % 2 == 0, by_row[:TAIL_ROWS, :], by_row[128:, :])
    out[TAIL_AT:ENERGY_AT, :] = block[TAIL_AT:ENERGY_AT, :] * tail_rows * column
    out[ENERGY_AT:, :] = jnp.zeros((TILES - ENERGY_AT, 128), jnp.float32)


def scale(place, lengths, first_pick, second_pick, block):
    return pl.pallas_call(
        scale_kernel,
        out_shape=pltpu.VMEM((TILES, 128), jnp.float32),
        in_specs=[SMEM, SMEM, VMEM, VMEM, VMEM],
        out_specs=VMEM,
        name="scale",
    )(place, lengths, *[near_by(v) for v in (first_pick, second_pick, block)])


def lay_kernel(place, own, left, right, far_top, far_bottom, gram_out, side_out, tails):
    x = place[1]
    half = TILES // 2

    def put(source, at, parts):
        for k in range(4):
            first = k * ROWS_PAD
            lanes = pl.ds(pl.multiple_of((source * 4 + k) * 128, 128), 128)
            for part, low, high in parts:
                begin, end = max(first, low), min(first + ROWS, high)
                if begin < end:
                    gram_out[begin - first : end - first, lanes] = part[begin - low : end - low, :]
        for part, low, high in parts:
            begin, end = max(TAIL_AT, low), min(ENERGY_AT, high)
            if begin < end:
                tails[source, begin - TAIL_AT : end - TAIL_AT, :] = part[begin - low : end - low, :]

    put(x, 0, [(own, 0, TILES)])
    put((x + 3) % 4, 1, [(left, 0, TILES)])
    put((x + 1) % 4, 2, [(right, 0, TILES)])
    put((x + 2) % 4, 3, [(far_top, 0, half), (far_bottom, half, TILES)])
    for x_of, low, high in ((0, 0, 128), (1, 128, ROWS)):
        count = high - low
        gram_out[low:high, 16 * 128 :] = tails[x_of, :count, :TAIL_QUADS]
        sides = jnp.concatenate([tails[x_of, :count, TAIL_QUADS:], tails[x_of + 2, :count, TAIL_QUADS:]], axis=1)
        side_out[low:high, :] = sides


def lay(place, *pieces):
    return pl.pallas_call(
        lay_kernel,
        out_shape=(
            jax.ShapeDtypeStruct((ROWS, FEAT), jnp.float32),
            jax.ShapeDtypeStruct((ROWS, R), jnp.float32),
        ),
        in_specs=[SMEM] + [VMEM] * 5,
        out_specs=(VMEM, VMEM),
        scratch_shapes=[pltpu.VMEM((4, TAIL_ROWS, 128), jnp.float32)],
        name="lay",
    )(place, *[near_by(v) for v in pieces])


def shards(snapshots, basis, lengths):
    core, x, z = lax.axis_index("c"), lax.axis_index("x"), lax.axis_index("z")
    space = lax.axis_index("y") * 2 + core
    place = jnp.stack([space, x, z, core]).astype(jnp.int32)
    head = snapshots[:, :2].T.astype(jnp.float32)
    tail = snapshots[:, BLOCK - 2 :].T.astype(jnp.float32)
    left = lax.ppermute(tail, ("x", "z"), [(i, i + 1) for i in range(31)])
    right = lax.ppermute(head, ("x", "z"), [(i + 1, i) for i in range(31)])
    partial = jnp.einsum("cr,ct->rt", basis, snapshots, preferred_element_type=jnp.float32)
    mine = lax.dynamic_slice_in_dim(partial, core * HALF, HALF, 1)
    other = lax.dynamic_slice_in_dim(partial, (1 - core) * HALF, HALF, 1)
    half = mine + swap(other)
    ends = jnp.einsum(
        "tc,cr->tr",
        jnp.concatenate([left, right], axis=0),
        basis.astype(jnp.float32),
        precision=lax.Precision.HIGHEST,
        preferred_element_type=jnp.float32,
    )
    ends = jnp.pad(ends, ((0, 4), (0, HALF - R)))
    message = jnp.concatenate([half, ends], axis=0)
    message = (message + turn(message, "y", 2)) + (turn(message, "y", 1) + turn(message, "y", 3))
    mine = (message, turn(message, "x", 3), turn(message, "x", 2), turn(message, "x", 1))
    theirs = tuple(swap(part) for part in mine)
    first_pick, second_pick = picks(place)
    block = gram(place, lengths, first_pick, second_pick, mine, theirs)
    piece = jnp.sum(lax.all_to_all(block.reshape(8, PIECE, 128), "z", 0, 0, tiled=True), axis=0)
    block = everyone(piece, "z").reshape(TILES, 128)
    block = scale(place, lengths, first_pick, second_pick, block)
    half = TILES // 2
    from_left, from_right = turn(block, "x", 1), turn(block, "x", 3)
    far_top, far_bottom = turn(from_left[:half], "x", 1), turn(from_right[half:], "x", 3)
    return lay(place, block, from_left, from_right, far_top, far_bottom)


def solution(mesh):
    grid = Mesh(mesh.devices.reshape(4, 2, 4, 8), ("y", "c", "x", "z"))
    return jax.shard_map(
        shards,
        mesh=grid,
        in_specs=(P(("y", "c"), ("x", "z")), P(("y", "c"), None), P()),
        out_specs=(P(("y", "c"), None), P(("y", "c"), None)),
        check_vma=False,
    )
```

time: 151 us -> 131 us (0.87)
  blocking collectives: 110 us -> 46.2 us
  waiting for transfers between devices: 5.83 us -> 34.4 us
  starting transfers between devices: 5.2 us -> 29.8 us
  Pallas kernels: 20.4 us -> 15 us
  local copies, waits for them, and re-layouts: 4.9 us -> 2.15 us
    all_to_all x4 -> x1, blocking collectives: 83.3 us -> 22.2 us  [everyone(): return lax.all_to_all(spread, axis, 0, 0, tiled=True)]
    ppermute x0 -> x10, waiting for transfers between devices: none -> 33.2 us  [turn(): lax.ppermute(value, axis, [(i, (i + by) % count) for i in range(count)])]
    ppermute x0 -> x10, starting transfers between devices: none -> 23.8 us  [turn(): lax.ppermute(value, axis, [(i, (i + by) % count) for i in range(count)])]
    pallas_call x2 -> x3, Pallas kernels: 17 us -> 12.7 us  [the longest x1 10.2 us: gram(): pl.pallas_call(gram_kernel, out_shape=pltpu.VMEM((TILES, 128), jnp.float3...]
    ppermute x1, waiting for transfers between devices: 4.16 us -> 0.01 us  [shards(): right = lax.ppermute(head, ('x', 'z'), [(i + 1, i) for i in range(31)])]
    all_to_all x1, blocking collectives: 26.6 us -> 24.1 us  [shards(): lax.all_to_all(block.reshape(8, PIECE, 128), 'z', 0, 0, tiled=True)]
  transfers between devices with their start and end apart: 4 -> 17, of which waited for: 3 -> 11; matrix products, arithmetic and copies ran while one was open for 1% -> 1% of each run, Pallas kernels for 0% -> 1%
where the time goes in v2:
time: 131 us
  blocking collectives  46.2 us (35%)
  waiting for transfers between devices  34.4 us (26%)
  starting transfers between devices  29.8 us (23%)
  Pallas kernels  15 us (11%)
  local copies, waits for them, and re-layouts  2.15 us (2%)
  other arithmetic  2.1 us (2%)
    ppermute x10, waiting for transfers between devices, turn(): lax.ppermute(value, axis, [(i, (i + by) % count) for i in range(count)])  33.2 us
    all_to_all x1, blocking collectives, shards(): lax.all_to_all(block.reshape(8, PIECE, 128), 'z', 0, 0, tiled=True)  24.1 us
    ppermute x10, starting transfers between devices, turn(): lax.ppermute(value, axis, [(i, (i + by) % count) for i in range(count)])  23.8 us
    all_to_all x1, blocking collectives, everyone(): return lax.all_to_all(spread, axis, 0, 0, tiled=True)  22.2 us
    pallas_call x1, Pallas kernels, gram(): pl.pallas_call(gram_kernel, out_shape=pltpu.VMEM((TILES, 128), jnp.float3...  10.2 us
    ppermute x1, starting transfers between devices, shards(): left = lax.ppermute(tail, ('x', 'z'), [(i, i + 1) for i in range(31)])  4.55 us
  transfers between devices with their start and end apart: 17, of which 11 were waited for; matrix products, arithmetic and copies ran while one was open for 1% of the time, Pallas kernels for 1%

profile of v2, /device:TPU:8, one launch (start us, length us, event | category | flops | bytes accessed | tf_op | source)
XLA Modules:
  0.0 131.1 jit_solution(13051774361616840014)
XLA Ops:
  0.6 0.0 copy-start
  0.7 1.3 %slice_convert_fusion.1 = (f32[1024,2]{1,0:T(8,128)S(1)}, f32[1024,2]{1,0:T(8,128)S(1)}) fusion(bf16[1024,1024]{1,0:T(8,128)(2,1)} %param.3), kind=kLoop, calls=%fused_computation.1 | loop fusion | flops 4096 | bytes 24576 | tf_op jit(solution)/shard_map/convert_element_type | solution.py:288
  2.0 0.2 copy.12
  2.2 1.3 collective-permute-start.2
  3.5 0.2 copy.11
  3.7 4.5 %collective-permute-start.1 = (f32[2,1024]{1,0:T(2,128)S(1)}, f32[2,1024]{1,0:T(2,128)S(1)}, u32[]{:S(2)}, u32[]{:S(2)}) collective-permute-start(f32[2,1024]{1,0:T(2,128)S(1)} %bitcast.14), channel_id=1, source_target_pairs={{0,1},{1,2},{2,3},{3,4},{4,5},{5,6},{6,7},{7,8},{8,9},{9,10},{10,1... | collective-permute-start | bytes 24584 | tf_op jit(solution)/shard_map/ppermute | solution.py:289
  8.2 0.5 fusion.5
  8.7 0.1 collective-permute-start
  8.8 0.0 collective-permute-done.2
  8.9 0.7 collective-permute-done.1
  9.6 0.2 fusion
  9.7 0.5 collective-permute-done
  10.2 1.7 %collective-permute-start.4 = (f32[72,512]{1,0:T(8,128)S(1)}, f32[72,512]{1,0:T(8,128)S(1)}, u32[]{:S(2)}, u32[]{:S(2)}) collective-permute-start(f32[72,512]{1,0:T(8,128)S(1)} %select_maximum_fusion), channel_id=1, source_target_pairs={{0,64},{64,128},{128,192},{192,0},{1,65},{65,129},{129,193},{193,1... | collective-permute-start | bytes 442376 | tf_op jit(solution)/shard_map/ppermute | solution.py:36
  11.9 0.7 collective-permute-start.5
  12.5 2.1 %collective-permute-start.3 = (f32[72,512]{1,0:T(8,128)S(1)}, f32[72,512]{1,0:T(8,128)S(1)}, u32[]{:S(2)}, u32[]{:S(2)}) collective-permute-start(f32[72,512]{1,0:T(8,128)S(1)} %select_maximum_fusion), channel_id=1, source_target_pairs={{0,128},{64,192},{128,0},{192,64},{1,129},{65,193},{129,1},{193,65... | collective-permute-start | bytes 442376 | tf_op jit(solution)/shard_map/ppermute | solution.py:36
  14.6 2.5 %collective-permute-done.4 = f32[72,512]{1,0:T(8,128)S(1)} collective-permute-done((f32[72,512]{1,0:T(8,128)S(1)}, f32[72,512]{1,0:T(8,128)S(1)}, u32[]{:S(2)}, u32[]{:S(2)}) %collective-permute-start.4) | collective-permute-done | bytes 147488 | tf_op jit(solution)/shard_map/ppermute | solution.py:36
  17.1 0.4 collective-permute-done.5
  17.5 4.1 %collective-permute-done.3 = f32[72,512]{1,0:T(8,128)S(1)} collective-permute-done((f32[72,512]{1,0:T(8,128)S(1)}, f32[72,512]{1,0:T(8,128)S(1)}, u32[]{:S(2)}, u32[]{:S(2)}) %collective-permute-start.3) | collective-permute-done | bytes 147488 | tf_op jit(solution)/shard_map/ppermute | solution.py:36
  21.6 7.4 %collective-permute-start.8 = (f32[72,512]{1,0:T(8,128)S(1)}, f32[72,512]{1,0:T(8,128)S(1)}, u32[]{:S(2)}, u32[]{:S(2)}) collective-permute-start(f32[72,512]{1,0:T(8,128)S(1)} %add_add_fusion.rest_0_), channel_id=1, source_target_pairs={{0,8},{8,16},{16,24},{24,0},{1,9},{9,17},{17,25},{25,1},{2,10},{10... | collective-permute-start | bytes 442376 | tf_op jit(solution)/shard_map/ppermute | solution.py:36
  29.0 3.0 %collective-permute-start.7 = (f32[72,512]{1,0:T(8,128)S(1)}, f32[72,512]{1,0:T(8,128)S(1)}, u32[]{:S(2)}, u32[]{:S(2)}) collective-permute-start(f32[72,512]{1,0:T(8,128)S(1)} %add_add_fusion.rest_0_), channel_id=1, source_target_pairs={{0,16},{8,24},{16,0},{24,8},{1,17},{9,25},{17,1},{25,9},{2,18},{10... | collective-permute-start | bytes 442376 | tf_op jit(solution)/shard_map/ppermute | solution.py:36
  32.1 1.1 collective-permute-start.6
  33.2 0.0 collective-permute-start.9
  33.2 1.1 collective-permute-done.8.rest_3_
  34.4 0.0 collective-permute-start.12
  34.4 2.4 %collective-permute-done.7.rest_2_ = f32[72,512]{1,0:T(8,128)S(1)} collective-permute-done((f32[72,512]{1,0:T(8,128)S(1)}, f32[72,512]{1,0:T(8,128)S(1)}, u32[]{:S(2)}, u32[]{:S(2)}) %collective-permute-start.7) | collective-permute-done | bytes 147488 | tf_op jit(solution)/shard_map/ppermute | solution.py:36
  36.8 0.0 collective-permute-start.11
  36.8 0.4 collective-permute-done.6.rest_1_
  37.2 0.1 collective-permute-start.10
  37.3 0.7 pad_add_fusion.place
  37.9 1.4 %picks.1 = (bf16[880,256]{1,0:T(8,128)(2,1)S(1)}, bf16[880,256]{1,0:T(8,128)(2,1)S(1)}) custom-call(s32[4]{0:T(128)} %pad_add_fusion.place), custom_call_target="tpu_custom_call" | custom-call | tf_op jit(solution)/shard_map/picks/pallas_call | solution.py:105
  39.3 0.0 collective-permute-done.9.rest_4_
  39.3 0.0 collective-permute-done.12.rest_7_
  39.3 0.0 collective-permute-done.11.rest_6_
  39.4 0.0 collective-permute-done.10.rest_5_
  39.4 10.2 %gram.1 = f32[1280,128]{1,0:T(8,128)S(1)} custom-call(s32[4]{0:T(128)} %pad_add_fusion.place, s32[16]{0:T(128)} %lengths.3, bf16[880,256]{1,0:T(8,128)(2,1)S(1)} %get-tuple-element.4.first_pick, bf16[880,256]{1,0:T(8,128)(2,1)S(1)} %get-tuple-element.5.second_pick, f32[72,512]{1,0:T(8,128)S(1)} %add_add_fusion.rest_0_, ...), custom_call_target="tpu_custom_call" | custom-call | tf_op jit(solution)/shard_map/gram/pallas_call | solution.py:186
  49.5 24.1 %all_to_all.10 = f32[8,160,128]{2,1,0:T(8,128)S(1)} all-to-all(f32[8,160,128]{2,1,0:T(8,128)S(1)} %bitcast.11), channel_id=1, replica_groups=mesh['y'=4,'c'=2,'x'=4,'z'=8] {'z'}, dimensions={0} | all-to-all | bytes 1310720 | tf_op jit(solution)/shard_map/all_to_all | solution.py:309
  73.7 22.2 %all_to_all.11 = f32[8,160,128]{2,1,0:T(8,128)S(1)} all-to-all(f32[8,160,128]{2,1,0:T(8,128)S(1)} %broadcast_in_dim.2), channel_id=1, replica_groups=mesh['y'=4,'c'=2,'x'=4,'z'=8] {'z'}, dimensions={0} | all-to-all | bytes 1310720 | tf_op jit(solution)/shard_map/all_to_all | solution.py:46
  95.9 1.2 scale.1.own
  97.0 3.9 %collective-permute-start.14 = (f32[1280,128]{1,0:T(8,128)S(1)}, f32[1280,128]{1,0:T(8,128)S(1)}, u32[]{:S(2)}, u32[]{:S(2)}) collective-permute-start(f32[1280,128]{1,0:T(8,128)S(1)} %scale.1.own), channel_id=1, source_target_pairs={{0,24},{8,0},{16,8},{24,16},{1,25},{9,1},{17,9},{25,17},{2,26},{10... | collective-permute-start | bytes 1966088 | tf_op jit(solution)/shard_map/ppermute | solution.py:36
  100.9 0.0 collective-permute-start.13
  100.9 13.4 %collective-permute-done.14.right = f32[1280,128]{1,0:T(8,128)S(1)} collective-permute-done((f32[1280,128]{1,0:T(8,128)S(1)}, f32[1280,128]{1,0:T(8,128)S(1)}, u32[]{:S(2)}, u32[]{:S(2)}) %collective-permute-start.14) | collective-permute-done | bytes 655392 | tf_op jit(solution)/shard_map/ppermute | solution.py:36
  114.4 3.8 %collective-permute-start.16 = (f32[640,128]{1,0:T(8,128)S(1)}, f32[640,128]{1,0:T(8,128)S(1)}, u32[]{:S(2)}, u32[]{:S(2)}) collective-permute-start(f32[640,128]{1,0:T(8,128)S(1)} %slice.17), channel_id=1, source_target_pairs={{0,24},{8,0},{16,8},{24,16},{1,25},{9,1},{17,9},{25,17},{2,26},{10... | collective-permute-start | bytes 983048 | tf_op jit(solution)/shard_map/ppermute | solution.py:36
  118.1 0.0 collective-permute-done.13.left
  118.2 0.1 collective-permute-start.15
  118.2 5.4 %collective-permute-done.16.far_bottom = f32[640,128]{1,0:T(8,128)S(1)} collective-permute-done((f32[640,128]{1,0:T(8,128)S(1)}, f32[640,128]{1,0:T(8,128)S(1)}, u32[]{:S(2)}, u32[]{:S(2)}) %collective-permute-start.16) | collective-permute-done | bytes 327712 | tf_op jit(solution)/shard_map/ppermute | solution.py:36
  123.6 3.5 %collective-permute-done.15.far_top = f32[640,128]{1,0:T(8,128)S(1)} collective-permute-done((f32[640,128]{1,0:T(8,128)S(1)}, f32[640,128]{1,0:T(8,128)S(1)}, u32[]{:S(2)}, u32[]{:S(2)}) %collective-permute-start.15) | collective-permute-done | bytes 327712 | tf_op jit(solution)/shard_map/ppermute | solution.py:36
  127.1 2.3 %lay.1 = (f32[268,2144]{1,0:T(8,128)}, f32[268,64]{1,0:T(8,128)}) custom-call(s32[4]{0:T(128)} %pad_add_fusion.place, f32[1280,128]{1,0:T(8,128)S(1)} %scale.1.own, f32[1280,128]{1,0:T(8,128)S(1)} %collective-permute-done.13.left, f32[1280,128]{1,0:T(8,128)S(1)} %collective-permute-done.14.right, f32[640,128]{1,0:T(8,128)S(1)} %collective-permute-done.15.far_top, ...), custom_call_target="tpu_custom_call" | custom-call | tf_op jit(solution)/shard_map/lay/pallas_call | solution.py:270
  129.5 1.7 %copy.8 = f32[268,64]{0,1:T(8,128)} copy(f32[268,64]{1,0:T(8,128)} %get-tuple-element.9) | data formatting | bytes 137216 | tf_op jit(solution)/shard_map/lay/pallas_call | solution.py:270
  (11 shorter events, 0.2 us)
Async XLA Ops:
  0.6 7.6 %copy-start = (bf16[1024,64]{0,1:T(8,128)(2,1)S(1)}, bf16[1024,64]{0,1:T(8,128)(2,1)}, u32[]{:S(2)}) copy-start(bf16[1024,64]{0,1:T(8,128)(2,1)} %param.4) | copy-start | bytes 393220
  0.6 7.6 %copy-start.1 = (bf16[1024,1024]{1,0:T(8,128)(2,1)S(1)}, bf16[1024,1024]{1,0:T(8,128)(2,1)}, u32[]{:S(2)}) copy-start(bf16[1024,1024]{1,0:T(8,128)(2,1)} %param.3) | copy-start | bytes 6291460
  2.2 6.7 %collective-permute-start.2 = (f32[2,1024]{1,0:T(2,128)S(1)}, f32[2,1024]{1,0:T(2,128)S(1)}, u32[]{:S(2)}, u32[]{:S(2)}) collective-permute-start(f32[2,1024]{1,0:T(2,128)S(1)} %bitcast.13), channel_id=1, source_target_pairs={{1,0},{2,1},{3,2},{4,3},{5,4},{6,5},{7,6},{8,7},{9,8},{10,9},{11,1... | collective-permute-start | bytes 24584 | tf_op jit(solution)/shard_map/ppermute | solution.py:290
  3.7 5.9 %collective-permute-start.1 = (f32[2,1024]{1,0:T(2,128)S(1)}, f32[2,1024]{1,0:T(2,128)S(1)}, u32[]{:S(2)}, u32[]{:S(2)}) collective-permute-start(f32[2,1024]{1,0:T(2,128)S(1)} %bitcast.14), channel_id=1, source_target_pairs={{0,1},{1,2},{2,3},{3,4},{4,5},{5,6},{6,7},{7,8},{8,9},{9,10},{10,1... | collective-permute-start | bytes 24584 | tf_op jit(solution)/shard_map/ppermute | solution.py:289
  8.7 1.4 %collective-permute-start = (f32[64,512]{1,0:T(8,128)S(1)}, f32[64,512]{1,0:T(8,128)S(1)}, u32[]{:S(2)}, u32[]{:S(2)}) collective-permute-start(f32[64,512]{1,0:T(8,128)S(1)} %constant_dynamic-slice_fusion), channel_id=1, source_target_pairs={{0,32},{32,0},{1,33},{33,1},{2,34},{34,2},{3,35},{35,3},{4,36},{36... | collective-permute-start | bytes 393224 | tf_op jit(solution)/shard_map/ppermute | solution.py:31
  10.2 6.9 %collective-permute-start.4 = (f32[72,512]{1,0:T(8,128)S(1)}, f32[72,512]{1,0:T(8,128)S(1)}, u32[]{:S(2)}, u32[]{:S(2)}) collective-permute-start(f32[72,512]{1,0:T(8,128)S(1)} %select_maximum_fusion), channel_id=1, source_target_pairs={{0,64},{64,128},{128,192},{192,0},{1,65},{65,129},{129,193},{193,1... | collective-permute-start | bytes 442376 | tf_op jit(solution)/shard_map/ppermute | solution.py:36
  11.9 5.6 %collective-permute-start.5 = (f32[72,512]{1,0:T(8,128)S(1)}, f32[72,512]{1,0:T(8,128)S(1)}, u32[]{:S(2)}, u32[]{:S(2)}) collective-permute-start(f32[72,512]{1,0:T(8,128)S(1)} %select_maximum_fusion), channel_id=1, source_target_pairs={{0,192},{64,0},{128,64},{192,128},{1,193},{65,1},{129,65},{193,129... | collective-permute-start | bytes 442376 | tf_op jit(solution)/shard_map/ppermute | solution.py:36
  12.5 9.0 %collective-permute-start.3 = (f32[72,512]{1,0:T(8,128)S(1)}, f32[72,512]{1,0:T(8,128)S(1)}, u32[]{:S(2)}, u32[]{:S(2)}) collective-permute-start(f32[72,512]{1,0:T(8,128)S(1)} %select_maximum_fusion), channel_id=1, source_target_pairs={{0,128},{64,192},{128,0},{192,64},{1,129},{65,193},{129,1},{193,65... | collective-permute-start | bytes 442376 | tf_op jit(solution)/shard_map/ppermute | solution.py:36
  21.6 12.7 %collective-permute-start.8 = (f32[72,512]{1,0:T(8,128)S(1)}, f32[72,512]{1,0:T(8,128)S(1)}, u32[]{:S(2)}, u32[]{:S(2)}) collective-permute-start(f32[72,512]{1,0:T(8,128)S(1)} %add_add_fusion.rest_0_), channel_id=1, source_target_pairs={{0,8},{8,16},{16,24},{24,0},{1,9},{9,17},{17,25},{25,1},{2,10},{10... | collective-permute-start | bytes 442376 | tf_op jit(solution)/shard_map/ppermute | solution.py:36
  29.0 7.7 %collective-permute-start.7 = (f32[72,512]{1,0:T(8,128)S(1)}, f32[72,512]{1,0:T(8,128)S(1)}, u32[]{:S(2)}, u32[]{:S(2)}) collective-permute-start(f32[72,512]{1,0:T(8,128)S(1)} %add_add_fusion.rest_0_), channel_id=1, source_target_pairs={{0,16},{8,24},{16,0},{24,8},{1,17},{9,25},{17,1},{25,9},{2,18},{10... | collective-permute-start | bytes 442376 | tf_op jit(solution)/shard_map/ppermute | solution.py:36
  32.1 5.1 %collective-permute-start.6 = (f32[72,512]{1,0:T(8,128)S(1)}, f32[72,512]{1,0:T(8,128)S(1)}, u32[]{:S(2)}, u32[]{:S(2)}) collective-permute-start(f32[72,512]{1,0:T(8,128)S(1)} %add_add_fusion.rest_0_), channel_id=1, source_target_pairs={{0,24},{8,0},{16,8},{24,16},{1,25},{9,1},{17,9},{25,17},{2,26},{10... | collective-permute-start | bytes 442376 | tf_op jit(solution)/shard_map/ppermute | solution.py:36
  33.2 6.1 %collective-permute-start.9 = (f32[72,512]{1,0:T(8,128)S(1)}, f32[72,512]{1,0:T(8,128)S(1)}, u32[]{:S(2)}, u32[]{:S(2)}) collective-permute-start(f32[72,512]{1,0:T(8,128)S(1)} %add_add_fusion.rest_0_), channel_id=1, source_target_pairs={{0,32},{32,0},{1,33},{33,1},{2,34},{34,2},{3,35},{35,3},{4,36},{36... | collective-permute-start | bytes 442376 | tf_op jit(solution)/shard_map/ppermute | solution.py:31
  34.4 5.0 %collective-permute-start.12 = (f32[72,512]{1,0:T(8,128)S(1)}, f32[72,512]{1,0:T(8,128)S(1)}, u32[]{:S(2)}, u32[]{:S(2)}) collective-permute-start(f32[72,512]{1,0:T(8,128)S(1)} %collective-permute-done.8.rest_3_), channel_id=1, source_target_pairs={{0,32},{32,0},{1,33},{33,1},{2,34},{34,2},{3,35},{35,3},{4,36},{36... | collective-permute-start | bytes 442376 | tf_op jit(solution)/shard_map/ppermute | solution.py:31
  36.8 2.6 %collective-permute-start.11 = (f32[72,512]{1,0:T(8,128)S(1)}, f32[72,512]{1,0:T(8,128)S(1)}, u32[]{:S(2)}, u32[]{:S(2)}) collective-permute-start(f32[72,512]{1,0:T(8,128)S(1)} %collective-permute-done.7.rest_2_), channel_id=1, source_target_pairs={{0,32},{32,0},{1,33},{33,1},{2,34},{34,2},{3,35},{35,3},{4,36},{36... | collective-permute-start | bytes 442376 | tf_op jit(solution)/shard_map/ppermute | solution.py:31
  37.2 2.1 %collective-permute-start.10 = (f32[72,512]{1,0:T(8,128)S(1)}, f32[72,512]{1,0:T(8,128)S(1)}, u32[]{:S(2)}, u32[]{:S(2)}) collective-permute-start(f32[72,512]{1,0:T(8,128)S(1)} %collective-permute-done.6.rest_1_), channel_id=1, source_target_pairs={{0,32},{32,0},{1,33},{33,1},{2,34},{34,2},{3,35},{35,3},{4,36},{36... | collective-permute-start | bytes 442376 | tf_op jit(solution)/shard_map/ppermute | solution.py:31
  97.0 17.3 %collective-permute-start.14 = (f32[1280,128]{1,0:T(8,128)S(1)}, f32[1280,128]{1,0:T(8,128)S(1)}, u32[]{:S(2)}, u32[]{:S(2)}) collective-permute-start(f32[1280,128]{1,0:T(8,128)S(1)} %scale.1.own), channel_id=1, source_target_pairs={{0,24},{8,0},{16,8},{24,16},{1,25},{9,1},{17,9},{25,17},{2,26},{10... | collective-permute-start | bytes 1966088 | tf_op jit(solution)/shard_map/ppermute | solution.py:36
  100.9 17.2 %collective-permute-start.13 = (f32[1280,128]{1,0:T(8,128)S(1)}, f32[1280,128]{1,0:T(8,128)S(1)}, u32[]{:S(2)}, u32[]{:S(2)}) collective-permute-start(f32[1280,128]{1,0:T(8,128)S(1)} %scale.1.own), channel_id=1, source_target_pairs={{0,8},{8,16},{16,24},{24,0},{1,9},{9,17},{17,25},{25,1},{2,10},{10... | collective-permute-start | bytes 1966088 | tf_op jit(solution)/shard_map/ppermute | solution.py:36
  114.4 9.3 %collective-permute-start.16 = (f32[640,128]{1,0:T(8,128)S(1)}, f32[640,128]{1,0:T(8,128)S(1)}, u32[]{:S(2)}, u32[]{:S(2)}) collective-permute-start(f32[640,128]{1,0:T(8,128)S(1)} %slice.17), channel_id=1, source_target_pairs={{0,24},{8,0},{16,8},{24,16},{1,25},{9,1},{17,9},{25,17},{2,26},{10... | collective-permute-start | bytes 983048 | tf_op jit(solution)/shard_map/ppermute | solution.py:36
  118.2 9.0 %collective-permute-start.15 = (f32[640,128]{1,0:T(8,128)S(1)}, f32[640,128]{1,0:T(8,128)S(1)}, u32[]{:S(2)}, u32[]{:S(2)}) collective-permute-start(f32[640,128]{1,0:T(8,128)S(1)} %slice.16), channel_id=1, source_target_pairs={{0,8},{8,16},{16,24},{24,0},{1,9},{9,17},{17,25},{25,1},{2,10},{10... | collective-permute-start | bytes 983048 | tf_op jit(solution)/shard_map/ppermute | solution.py:36

commit v3 on v2

v3 whole, which is shorter than its diff:
```python
import functools

import jax
import jax.numpy as jnp
from jax import lax
from jax.experimental import pallas as pl
from jax.experimental.pallas import tpu as pltpu
from jax.sharding import Mesh, PartitionSpec as P

R = 64
FEAT = 2144
SLOT = 2048
TRAJ = 16
BLOCK = 1024
HALF = 512
ROWS = 268
ROWS_PAD = 272
COLS = 512
TAIL_QUADS = 96
TAIL_SIDES = 32
TAIL_ROWS = 144
PICKS = ROWS_PAD + COLS + TAIL_QUADS
TAIL_AT = 4 * ROWS_PAD
ENERGY_AT = TAIL_AT + TAIL_ROWS
PIECE = 160
TILES = 8 * PIECE
UP = 2.0**16


def swap(value):
    return lax.ppermute(value, "c", [(0, 1), (1, 0)])


def turn(value, axis, by):
    count = lax.axis_size(axis)
    return lax.ppermute(value, axis, [(i, (i + by) % count) for i in range(count)])


def near_by(value):
    return pltpu.with_memory_space_constraint(value, pltpu.VMEM)


def everyone(value, axis):
    count = lax.axis_size(axis)
    spread = jnp.broadcast_to(value[None], (count,) + value.shape)
    return lax.all_to_all(spread, axis, 0, 0, tiled=True)


def one_hots(first_feature, count):
    lane = lax.broadcasted_iota(jnp.int32, (count, 256), 1)
    feature = lax.broadcasted_iota(jnp.int32, (count, 256), 0) + first_feature
    mode = lane & (R - 1)
    below = lane < 3 * R
    ends = R + (mode + 1) * R - (mode + 1) * mode // 2
    passed = jnp.where((lane < R) & (feature >= ends), 1.0, 0.0)
    row = jnp.sum(passed, axis=1, keepdims=True).astype(jnp.int32)
    start = R + row * R - row * (row - 1) // 2
    linear = feature < R
    first = jnp.where(linear, feature, row)
    second = jnp.where(linear, -1, feature - start + row)
    pick_first = below & (mode == first)
    pick_second = (below & (mode == second)) | (linear & (lane == 3 * R))
    as_type = lambda pick: jnp.where(pick, 1.0, 0.0).astype(jnp.bfloat16)
    return as_type(pick_first), as_type(pick_second)


def split3(value):
    high = value.astype(jnp.bfloat16)
    rest = value - high.astype(jnp.float32)
    middle = rest.astype(jnp.bfloat16)
    low = (rest - middle.astype(jnp.float32)).astype(jnp.bfloat16)
    return high, middle, low


def split2(value):
    high = value.astype(jnp.bfloat16)
    return high, (value - high.astype(jnp.float32)).astype(jnp.bfloat16)


def dot(left, right, dims):
    return lax.dot_general(left, right, (dims, ((), ())), preferred_element_type=jnp.float32)


NT = ((1,), (1,))
NN = ((1,), (0,))


def position():
    return lax.axis_index("c"), lax.axis_index("x"), lax.axis_index("z")


def pick_kernel(first_pick, second_pick):
    core, x, _ = position()
    space = lax.axis_index("y") * 2 + core
    for at, count, feature in (
        (0, ROWS_PAD, space * ROWS),
        (ROWS_PAD, COLS, x * COLS),
        (ROWS_PAD + COLS, TAIL_QUADS, 4 * COLS),
    ):
        first, second = one_hots(feature, count)
        first_pick[at : at + count, :] = first
        second_pick[at : at + count, :] = second


SMEM = pl.BlockSpec(memory_space=pltpu.SMEM)
VMEM = pl.BlockSpec(memory_space=pltpu.VMEM)
ROOM = pltpu.CompilerParams(vmem_limit_bytes=24 * 1024 * 1024)


def picks():
    return pl.pallas_call(
        pick_kernel,
        out_shape=(pltpu.VMEM((PICKS, 256), jnp.bfloat16), pltpu.VMEM((PICKS, 256), jnp.bfloat16)),
        out_specs=(VMEM, VMEM),
        compiler_params=ROOM,
        name="picks",
    )()


def whole_block(own, other, core):
    near = jnp.where(core == 0, own[...], other[...])
    far = jnp.where(core == 0, other[...], own[...])
    return jnp.concatenate([near, far], axis=1) * UP


def alive(lengths, start):
    lane = lax.broadcasted_iota(jnp.int32, (1, BLOCK), 1)
    one = lengths[(start + HALF) // SLOT % TRAJ]
    two = lengths[(start + 2 * HALF) // SLOT % TRAJ]
    offset = ((start + HALF) % SLOT + lane) & (SLOT - 1)
    limit = jnp.where(lane < HALF, one, two) - 3
    return jnp.where((offset >= 2) & (offset <= limit), 1.0, 0.0)


def features(first_pick, second_pick, stack, at, count):
    first = dot(first_pick[at : at + count, :], stack, NN)
    second = dot(second_pick[at : at + count, :], stack, NN)
    return split2(first * second)


def product(left_hi, left_lo, right_hi, right_lo):
    return dot(left_hi, right_hi, NT) + (dot(left_hi, right_lo, NT) + dot(left_lo, right_hi, NT))


def stacked(masked, stack):
    stack[:R, :], stack[R : 2 * R, :], stack[2 * R : 3 * R, :] = split3(masked)
    index = lax.broadcasted_iota(jnp.int32, masked.shape, 0)
    stack[3 * R :, :] = jnp.where(index == 0, 1.0, 0.0).astype(jnp.bfloat16)


def gram_kernel(lengths, first_pick, second_pick, *rest):
    mine, theirs = rest[:4], rest[4:8]
    out, stack, rows_hi, rows_lo, acc, energy = rest[8:]
    core, x, z = position()
    for step in range(4):
        start = ((x + step) % 4 * 8 + z) * BLOCK
        masked = whole_block(mine[step], theirs[step], core) * alive(lengths, start)
        squares = masked * masked
        square = functools.reduce(lambda a, b: a + b, [squares[:, k * 128 : (k + 1) * 128] for k in range(BLOCK // 128)])
        energy[...] = square if step == 0 else energy[...] + square
        stacked(masked, stack)
        rows_hi[...], rows_lo[...] = features(first_pick, second_pick, stack[...], 0, ROWS_PAD)
        for at in range(0, COLS, 256):
            right_hi, right_lo = features(first_pick, second_pick, stack[...], ROWS_PAD + at, 256)
            total = product(rows_hi[...], rows_lo[...], right_hi, right_lo)
            acc[:, at : at + 256] = total if step == 0 else acc[:, at : at + 256] + total
    for k in range(COLS // 128):
        out[k * ROWS_PAD : (k + 1) * ROWS_PAD, :] = acc[:, k * 128 : (k + 1) * 128]
    out[TAIL_AT:, :] = jnp.zeros((TILES - TAIL_AT, 128), jnp.float32)
    out[ENERGY_AT : ENERGY_AT + 8, :R] = lax.dot_general(
        jnp.ones((8, 128), jnp.float32),
        energy[...],
        (NT, ((), ())),
        precision=lax.Precision.HIGHEST,
        preferred_element_type=jnp.float32,
    )


def gram(lengths, first_pick, second_pick, mine, theirs):
    return pl.pallas_call(
        gram_kernel,
        out_shape=pltpu.VMEM((TILES, 128), jnp.float32),
        in_specs=[SMEM] + [VMEM] * 10,
        out_specs=VMEM,
        scratch_shapes=[
            pltpu.VMEM((4 * R, BLOCK), jnp.bfloat16),
            pltpu.VMEM((ROWS_PAD, BLOCK), jnp.bfloat16),
            pltpu.VMEM((ROWS_PAD, BLOCK), jnp.bfloat16),
            pltpu.VMEM((ROWS_PAD, COLS), jnp.float32),
            pltpu.VMEM((R, 128), jnp.float32),
        ],
        compiler_params=ROOM,
        name="gram",
    )(lengths, *[near_by(v) for v in (first_pick, second_pick, *mine, *theirs)])


def edge_kernel(*refs):
    parts, out = refs[:4], refs[4]
    core = lax.axis_index("c")
    lane = lax.broadcasted_iota(jnp.int32, (R, 128), 1)
    edges = jnp.zeros((R, 128), jnp.float32)
    for step, part in enumerate(parts):
        first, last = part[:, :128], pltpu.roll(part[:, HALF - 128 :], 2, 1)
        here = jnp.where(core == 0, first, last)
        edges = jnp.where((lane >> 1) == step, pltpu.roll(here, 2 * step, 1) if step else here, edges)
    out[...] = edges


def edges_of(parts):
    return pl.pallas_call(
        edge_kernel,
        out_shape=pltpu.VMEM((R, 128), jnp.float32),
        in_specs=[VMEM] * 4,
        out_specs=VMEM,
        compiler_params=ROOM,
        name="edges",
    )(*[near_by(v) for v in parts])


def tail_kernel(lengths, first_pick, second_pick, same, cross, *rest):
    mine, theirs = rest[:4], rest[4:8]
    block, out, stack, change, cols_hi, cols_lo, rows_hi, rows_lo, tail = rest[8:]
    core, x, z = position()
    wide = lax.broadcasted_iota(jnp.int32, (R, BLOCK), 1)
    lefts = jnp.where(core == 0, cross[...], same[...]) * UP
    rights = jnp.where(core == 0, same[...], cross[...]) * UP
    pair = lambda ends, step: ends[:, 2 * (step % 4) : 2 * (step % 4) + 2]
    part = pl.ds(pl.multiple_of(x % 2 * 128, 128), TAIL_ROWS)
    for step in range(4):
        where = (x + step) % 4
        start = (where * 8 + z) * BLOCK
        left = jnp.where(z == 0, pair(lefts, step + 3), pair(lefts, step))
        left = jnp.where((z == 0) & (where == 0), 0.0, left)
        right = jnp.where(z == 7, pair(rights, step + 1), pair(rights, step))
        right = jnp.where((z == 7) & (where == 3), 0.0, right)
        states = whole_block(mine[step], theirs[step], core)
        living = alive(lengths, start)
        before = jnp.where(wide == 0, left[:, 1:2], pltpu.roll(states, 1, 1))
        before2 = jnp.where(wide == 0, left[:, 0:1], jnp.where(wide == 1, left[:, 1:2], pltpu.roll(states, 2, 1)))
        after = jnp.where(wide == BLOCK - 1, right[:, 0:1], pltpu.roll(states, BLOCK - 1, 1))
        after2 = jnp.where(
            wide == BLOCK - 1, right[:, 1:2], jnp.where(wide == BLOCK - 2, right[:, 0:1], pltpu.roll(states, BLOCK - 2, 1))
        )
        change[...] = (before2 - 8.0 * before + 8.0 * after - after2) * (1.0 / 12.0) * living
        stacked(states * living, stack)
        first = dot(first_pick[part, :], stack[...], NN)
        second = dot(second_pick[part, :], stack[...], NN)
        rows_hi[...], rows_lo[...] = split2(first * second)
        cols_hi[:TAIL_QUADS, :], cols_lo[:TAIL_QUADS, :] = features(first_pick, second_pick, stack[...], ROWS_PAD + COLS, TAIL_QUADS)
        side = change[pl.ds(pl.multiple_of(x // 2 * TAIL_SIDES, TAIL_SIDES), TAIL_SIDES), :]
        cols_hi[TAIL_QUADS:, :], cols_lo[TAIL_QUADS:, :] = split2(side)
        total = product(rows_hi[...], rows_lo[...], cols_hi[...], cols_lo[...])
        tail[...] = total if step == 0 else tail[...] + total
    out[TAIL_AT:ENERGY_AT, :] = tail[...]


def with_tail(lengths, first_pick, second_pick, ends, mine, theirs, block):
    return pl.pallas_call(
        tail_kernel,
        out_shape=pltpu.VMEM((TILES, 128), jnp.float32),
        in_specs=[SMEM] + [VMEM] * 13,
        out_specs=VMEM,
        scratch_shapes=[
            pltpu.VMEM((4 * R, BLOCK), jnp.bfloat16),
            pltpu.VMEM((R, BLOCK), jnp.float32),
            pltpu.VMEM((128, BLOCK), jnp.bfloat16),
            pltpu.VMEM((128, BLOCK), jnp.bfloat16),
            pltpu.VMEM((TAIL_ROWS, BLOCK), jnp.bfloat16),
            pltpu.VMEM((TAIL_ROWS, BLOCK), jnp.bfloat16),
            pltpu.VMEM((TAIL_ROWS, 128), jnp.float32),
        ],
        input_output_aliases={13: 0},
        compiler_params=ROOM,
        name="tail",
    )(lengths, *[near_by(v) for v in (first_pick, second_pick, *ends, *mine, *theirs, block)])


def weights_of(lengths, energy):
    samples = lengths[0] - 4
    for k in range(1, TRAJ):
        samples += lengths[k] - 4
    samples = samples.astype(jnp.float32)
    inverse = (1.0 / UP) / jnp.sqrt(energy * (1.0 / (UP * UP)) / samples + 1e-06)
    high, middle, low = [part.astype(jnp.float32) for part in split3(inverse)]
    fill = jnp.where(lax.broadcasted_iota(jnp.int32, (8, R), 1) == 0, 1.0, 0.0)
    weights = jnp.concatenate([high, middle, low, fill], axis=1)
    tall = jnp.broadcast_to(weights[0:1, :], (128, 256)).astype(jnp.bfloat16)
    return samples, inverse, weights.astype(jnp.bfloat16), tall


def scale_kernel(lengths, first_pick, second_pick, block, out):
    x = lax.axis_index("x")
    samples, inverse, weights, tall = weights_of(lengths, block[ENERGY_AT : ENERGY_AT + 8, :R])
    by_row = dot(first_pick[:ROWS_PAD, :], tall, NT) * dot(second_pick[:ROWS_PAD, :], tall, NT) / samples
    by_column = (dot(weights, first_pick[ROWS_PAD:, :], NT) * dot(weights, second_pick[ROWS_PAD:, :], NT))[0:1, :]
    for k in range(COLS // 128):
        rows = slice(k * ROWS_PAD, (k + 1) * ROWS_PAD)
        out[rows, :] = block[rows, :] * by_row * by_column[:, k * 128 : (k + 1) * 128]
    sides = jnp.where(x < 2, inverse[0:1, :TAIL_SIDES], inverse[0:1, TAIL_SIDES:])
    column = jnp.concatenate([by_column[:, COLS:], sides], axis=1)
    tail_rows = jnp.where(x % 2 == 0, by_row[:TAIL_ROWS, :], by_row[128:, :])
    out[TAIL_AT:ENERGY_AT, :] = block[TAIL_AT:ENERGY_AT, :] * tail_rows * column


def scale(lengths, first_pick, second_pick, block):
    return pl.pallas_call(
        scale_kernel,
        out_shape=pltpu.VMEM((ENERGY_AT, 128), jnp.float32),
        in_specs=[SMEM, VMEM, VMEM, VMEM],
        out_specs=VMEM,
        compiler_params=ROOM,
        name="scale",
    )(lengths, *[near_by(v) for v in (first_pick, second_pick, block)])


def lay_kernel(own, left, right, far_top, far_bottom, gram_out, side_out, tails, sides):
    x = lax.axis_index("x")
    half = ENERGY_AT // 2

    def put(source, parts):
        for k in range(COLS // 128):
            first = k * ROWS_PAD
            lanes = pl.ds(pl.multiple_of((source * 4 + k) * 128, 128), 128)
            for part, low, high in parts:
                begin, end = max(first, low), min(first + ROWS, high)
                if begin < end:
                    gram_out[begin - first : end - first, lanes] = part[begin - low : end - low, :]
        for part, low, high in parts:
            begin, end = max(TAIL_AT, low), min(ENERGY_AT, high)
            if begin < end:
                tails[source, begin - TAIL_AT : end - TAIL_AT, :] = part[begin - low : end - low, :]

    put(x, [(own, 0, ENERGY_AT)])
    put((x + 3) % 4, [(left, 0, ENERGY_AT)])
    put((x + 1) % 4, [(right, 0, ENERGY_AT)])
    put((x + 2) % 4, [(far_top, 0, half), (far_bottom, half, ENERGY_AT)])
    sides[...] = jnp.zeros_like(sides)
    for x_of, low, high in ((0, 0, 128), (1, 128, ROWS)):
        count = high - low
        gram_out[low:high, 16 * 128 :] = tails[x_of, :count, :TAIL_QUADS]
        sides[low:high, :TAIL_SIDES] = tails[x_of, :count, TAIL_QUADS:]
        sides[low:high, TAIL_SIDES:R] = tails[x_of + 2, :count, TAIL_QUADS:]
    side_out[...] = sides[...].T[:R, :ROWS]


def lay(*pieces):
    return pl.pallas_call(
        lay_kernel,
        out_shape=(
            jax.ShapeDtypeStruct((ROWS, FEAT), jnp.float32),
            jax.ShapeDtypeStruct((R, ROWS), jnp.float32),
        ),
        in_specs=[VMEM] * 5,
        out_specs=(VMEM, VMEM),
        scratch_shapes=[pltpu.VMEM((4, TAIL_ROWS, 128), jnp.float32), pltpu.VMEM((384, 128), jnp.float32)],
        compiler_params=ROOM,
        name="lay",
    )(*[near_by(v) for v in pieces])


def ring(block):
    half = block.shape[0] // 2
    from_left, from_right = turn(block, "x", 1), turn(block, "x", 3)
    return block, from_left, from_right, turn(from_left[:half], "x", 1), turn(from_right[half:], "x", 3)


def shards(snapshots, basis, lengths):
    core = lax.axis_index("c")
    partial = jnp.einsum("cr,ct->rt", basis, snapshots, preferred_element_type=jnp.float32)
    mine = lax.dynamic_slice_in_dim(partial, core * HALF, HALF, 1)
    other = lax.dynamic_slice_in_dim(partial, (1 - core) * HALF, HALF, 1)
    half = mine + swap(other)
    message = (half + turn(half, "y", 2)) + (turn(half, "y", 1) + turn(half, "y", 3))
    first_pick, second_pick = picks()
    message, first_pick, second_pick = lax.optimization_barrier((message, first_pick, second_pick))
    mine = (message, turn(message, "x", 3), turn(message, "x", 2), turn(message, "x", 1))
    theirs = tuple(swap(part) for part in mine)
    edges = edges_of(mine)
    at = lambda c, z: c * 8 + z % 8
    same = lax.ppermute(edges, ("c", "z"), [(at(0, z), at(0, z + 7)) for z in range(8)] + [(at(1, z), at(1, z + 1)) for z in range(8)])
    cross = lax.ppermute(edges, ("c", "z"), [(at(0, z), at(1, z + 7)) for z in range(8)] + [(at(1, z), at(0, z + 1)) for z in range(8)])
    block = gram(lengths, first_pick, second_pick, mine, theirs)
    block = with_tail(lengths, first_pick, second_pick, (same, cross), mine, theirs, block)
    piece = jnp.sum(lax.all_to_all(block.reshape(8, PIECE, 128), "z", 0, 0, tiled=True), axis=0)
    block = everyone(piece, "z").reshape(TILES, 128)
    block = scale(lengths, first_pick, second_pick, block)
    gram_out, side_out = lay(*ring(block))
    return gram_out, side_out.T


def solution(mesh):
    grid = Mesh(mesh.devices.reshape(4, 2, 4, 8), ("y", "c", "x", "z"))
    return jax.shard_map(
        shards,
        mesh=grid,
        in_specs=(P(("y", "c"), ("x", "z")), P(("y", "c"), None), P()),
        out_specs=(P(("y", "c"), None), P(("y", "c"), None)),
        check_vma=False,
    )
```

time: 131 us -> 122 us (0.931); the launches traced: 131 us -> 121 us
  starting transfers between devices: 29.8 us -> 22.8 us
  waiting for transfers between devices: 34.4 us -> 29.7 us
    ppermute x10, starting transfers between devices: 23.8 us -> 15.6 us  [turn(): lax.ppermute(value, axis, [(i, (i + by) % count) for i in range(count)])]
    ppermute x10, waiting for transfers between devices: 33.2 us -> 28.3 us  [turn(): lax.ppermute(value, axis, [(i, (i + by) % count) for i in range(count)])]
    pallas_call x1 -> x3, Pallas kernels: 1.16 us -> 5.26 us  [the longest x1 4.07 us: with_tail(): pl.pallas_call(tail_kernel, out_shape=pltpu.VMEM((TILES, 128), jnp.float3...]
    pallas_call x1, Pallas kernels: 10.2 us -> 7.89 us  [gram(): pl.pallas_call(gram_kernel, out_shape=pltpu.VMEM((TILES, 128), jnp.float3...]
    pallas_call x1 -> x0, local copies, waits for them, and re-layouts: 1.66 us -> none  [lay(): pl.pallas_call(lay_kernel, out_shape=(jax.ShapeDtypeStruct((ROWS, FEAT),...]
    convert_element_type x1 -> x0, other arithmetic: 1.33 us -> none  [shards(): tail = snapshots[:, BLOCK - 2:].T.astype(jnp.float32)]
  transfers between devices with their start and end apart: 17 -> 17, of which waited for: 11 -> 8; matrix products, arithmetic and copies ran while one was open for 1% -> 0% of each run, Pallas kernels for 1% -> 7%
where the time goes in v3:
time: 122 us; the launch traced here: 121 us
  blocking collectives  47.4 us (39%)
  waiting for transfers between devices  29.7 us (24%)
  starting transfers between devices  22.8 us (19%)
  Pallas kernels  15.6 us (13%)
  local copies, waits for them, and re-layouts  1.69 us (1%)
  matrix products  1.39 us (1%)
    ppermute x10, waiting for transfers between devices, turn(): lax.ppermute(value, axis, [(i, (i + by) % count) for i in range(count)])  28.3 us
    all_to_all x1, blocking collectives, shards(): lax.all_to_all(block.reshape(8, PIECE, 128), 'z', 0, 0, tiled=True)  24.2 us
    all_to_all x1, blocking collectives, everyone(): return lax.all_to_all(spread, axis, 0, 0, tiled=True)  23.2 us
    ppermute x10, starting transfers between devices, turn(): lax.ppermute(value, axis, [(i, (i + by) % count) for i in range(count)])  15.6 us
    pallas_call x1, Pallas kernels, gram(): pl.pallas_call(gram_kernel, out_shape=pltpu.VMEM((TILES, 128), jnp.float3...  7.89 us
    ppermute x1, starting transfers between devices, shards(): lax.ppermute(edges, ('c', 'z'), [(at(0, z), at(1, z + 7)) for z in range(...  5.55 us
    pallas_call x1, Pallas kernels, with_tail(): pl.pallas_call(tail_kernel, out_shape=pltpu.VMEM((TILES, 128), jnp.float3...  4.07 us
  transfers between devices with their start and end apart: 17, of which 8 were waited for; matrix products, arithmetic and copies ran while one was open for 0% of the time, Pallas kernels for 7%

profile of v3, /device:TPU:8, one launch (start us, length us, event | category | flops | bytes accessed | tf_op | source)
XLA Modules:
  0.0 120.6 jit_solution(9901117129772416324)
XLA Ops:
  0.6 0.0 copy-start
  0.7 1.6 %copy-done = bf16[1024,1024]{1,0:T(8,128)(2,1)S(1)} copy-done((bf16[1024,1024]{1,0:T(8,128)(2,1)S(1)}, bf16[1024,1024]{1,0:T(8,128)(2,1)}, u32[]{:S(2)}) %copy-start) | copy-done | bytes 2097176
  2.2 0.0 copy-start.1
  2.2 1.4 %fusion = f32[64,1024]{1,0:T(8,128)S(1)} fusion(bf16[1024,64]{0,1:T(8,128)(2,1)} %param.4, bf16[1024,1024]{1,0:T(8,128)(2,1)S(1)} %copy-done), kind=kOutput, calls=%fused_computation.3 | convolution fusion | flops 134217728 | bytes 2490368 | tf_op jit(solution)/shard_map/cr,ct->rt/dot_general | solution.py:369
  3.7 0.1 collective-permute-start
  3.8 1.3 %collective-permute-done = f32[64,512]{1,0:T(8,128)S(1)} collective-permute-done((f32[64,512]{1,0:T(8,128)S(1)}, f32[64,512]{1,0:T(8,128)S(1)}, u32[]{:S(2)}, u32[]{:S(2)}) %collective-permute-start) | collective-permute-done | bytes 131104 | tf_op jit(solution)/shard_map/ppermute | solution.py:31
  5.1 2.2 %collective-permute-start.3 = (f32[64,512]{1,0:T(8,128)S(1)}, f32[64,512]{1,0:T(8,128)S(1)}, u32[]{:S(2)}, u32[]{:S(2)}) collective-permute-start(f32[64,512]{1,0:T(8,128)S(1)} %dynamic-slice_add_fusion), channel_id=1, source_target_pairs={{0,192},{64,0},{128,64},{192,128},{1,193},{65,1},{129,65},{193,129... | collective-permute-start | bytes 393224 | tf_op jit(solution)/shard_map/ppermute | solution.py:36
  7.3 0.0 collective-permute-start.2
  7.4 3.4 %collective-permute-start.1 = (f32[64,512]{1,0:T(8,128)S(1)}, f32[64,512]{1,0:T(8,128)S(1)}, u32[]{:S(2)}, u32[]{:S(2)}) collective-permute-start(f32[64,512]{1,0:T(8,128)S(1)} %dynamic-slice_add_fusion), channel_id=1, source_target_pairs={{0,128},{64,192},{128,0},{192,64},{1,129},{65,193},{129,1},{193,65... | collective-permute-start | bytes 393224 | tf_op jit(solution)/shard_map/ppermute | solution.py:36
  10.7 0.7 picks.1
  11.4 0.0 collective-permute-done.3
  11.4 2.3 %collective-permute-done.2 = f32[64,512]{1,0:T(8,128)S(1)} collective-permute-done((f32[64,512]{1,0:T(8,128)S(1)}, f32[64,512]{1,0:T(8,128)S(1)}, u32[]{:S(2)}, u32[]{:S(2)}) %collective-permute-start.2) | collective-permute-done | bytes 131104 | tf_op jit(solution)/shard_map/ppermute | solution.py:36
  13.7 0.8 collective-permute-done.1
  14.6 1.6 %collective-permute-start.6 = (f32[64,512]{1,0:T(8,128)S(1)}, f32[64,512]{1,0:T(8,128)S(1)}, u32[]{:S(2)}, u32[]{:S(2)}) collective-permute-start(f32[64,512]{1,0:T(8,128)S(1)} %add_add_fusion.refs_0_.rest_0_), channel_id=1, source_target_pairs={{0,8},{8,16},{16,24},{24,0},{1,9},{9,17},{17,25},{25,1},{2,10},{10... | collective-permute-start | bytes 393224 | tf_op jit(solution)/shard_map/ppermute | solution.py:36
  16.2 2.7 %collective-permute-start.5 = (f32[64,512]{1,0:T(8,128)S(1)}, f32[64,512]{1,0:T(8,128)S(1)}, u32[]{:S(2)}, u32[]{:S(2)}) collective-permute-start(f32[64,512]{1,0:T(8,128)S(1)} %add_add_fusion.refs_0_.rest_0_), channel_id=1, source_target_pairs={{0,16},{8,24},{16,0},{24,8},{1,17},{9,25},{17,1},{25,9},{2,18},{10... | collective-permute-start | bytes 393224 | tf_op jit(solution)/shard_map/ppermute | solution.py:36
  18.9 1.4 %collective-permute-start.4 = (f32[64,512]{1,0:T(8,128)S(1)}, f32[64,512]{1,0:T(8,128)S(1)}, u32[]{:S(2)}, u32[]{:S(2)}) collective-permute-start(f32[64,512]{1,0:T(8,128)S(1)} %add_add_fusion.refs_0_.rest_0_), channel_id=1, source_target_pairs={{0,24},{8,0},{16,8},{24,16},{1,25},{9,1},{17,9},{25,17},{2,26},{10... | collective-permute-start | bytes 393224 | tf_op jit(solution)/shard_map/ppermute | solution.py:36
  20.3 0.0 collective-permute-start.9
  20.3 1.0 collective-permute-done.6.refs_3_.rest_3_
  21.4 0.0 collective-permute-start.12
  21.4 3.2 %collective-permute-done.5.refs_2_.rest_2_ = f32[64,512]{1,0:T(8,128)S(1)} collective-permute-done((f32[64,512]{1,0:T(8,128)S(1)}, f32[64,512]{1,0:T(8,128)S(1)}, u32[]{:S(2)}, u32[]{:S(2)}) %collective-permute-start.5) | collective-permute-done | bytes 131104 | tf_op jit(solution)/shard_map/ppermute | solution.py:36
  24.6 0.0 collective-permute-start.11
  24.6 0.0 collective-permute-done.4.refs_1_.rest_1_
  24.6 0.5 collective-permute-start.10
  25.1 0.2 edges.1
  25.3 5.5 %collective-permute-start.8 = (f32[64,128]{1,0:T(8,128)S(1)}, f32[64,128]{1,0:T(8,128)S(1)}, u32[]{:S(2)}, u32[]{:S(2)}) collective-permute-start(f32[64,128]{1,0:T(8,128)S(1)} %edges.1), channel_id=1, source_target_pairs={{0,39},{1,32},{2,33},{3,34},{4,35},{5,36},{6,37},{7,38},{32,1},{33... | collective-permute-start | bytes 98312 | tf_op jit(solution)/shard_map/ppermute | solution.py:381
  30.8 0.0 collective-permute-done.9.rest_4_
  30.8 1.0 collective-permute-start.7
  31.8 0.0 collective-permute-done.12.rest_7_
  31.9 0.0 collective-permute-done.11.rest_6_
  31.9 0.0 collective-permute-done.10.rest_5_
  31.9 0.0 copy-done.1
  31.9 7.9 %gram.1.rest_8_ = f32[1280,128]{1,0:T(8,128)S(1)} custom-call(s32[16]{0:T(128)S(1)} %copy-done.1, bf16[880,256]{1,0:T(8,128)(2,1)S(1)} %get-tuple-element.11.first_pick, bf16[880,256]{1,0:T(8,128)(2,1)S(1)} %get-tuple-element.12.second_pick, f32[64,512]{1,0:T(8,128)S(1)} %add_add_fusion.refs_0_.rest_0_, ...), custom_call_target="tpu_custom_call" | custom-call | tf_op jit(solution)/shard_map/gram/pallas_call | solution.py:180
  39.8 0.0 collective-permute-done.8.cross
  39.8 0.0 collective-permute-done.7.same
  39.8 4.1 %tail.1 = f32[1280,128]{1,0:T(8,128)S(1)} custom-call(s32[16]{0:T(128)S(1)} %copy-done.1, bf16[880,256]{1,0:T(8,128)(2,1)S(1)} %get-tuple-element.11.first_pick, bf16[880,256]{1,0:T(8,128)(2,1)S(1)} %get-tuple-element.12.second_pick, f32[64,128]{1,0:T(8,128)S(1)} %collective-permute-done.7.same, ...), custom_call_target="tpu_custom_call", output_to_operand_aliasing={{}: (13, {})} | custom-call | tf_op jit(solution)/shard_map/tail/pallas_call | solution.py:258
  43.8 24.2 %all_to_all.10 = f32[8,160,128]{2,1,0:T(8,128)} all-to-all(f32[8,160,128]{2,1,0:T(8,128)S(1)} %bitcast.5), channel_id=1, replica_groups=mesh['y'=4,'c'=2,'x'=4,'z'=8] {'z'}, dimensions={0} | all-to-all | bytes 1310720 | tf_op jit(solution)/shard_map/all_to_all | solution.py:384
  68.1 1.1 reduce_sum.9
  69.3 23.2 %all_to_all.11 = f32[8,160,128]{2,1,0:T(8,128)S(1)} all-to-all(f32[8,160,128]{2,1,0:T(8,128)S(1)} %broadcast_in_dim.2), channel_id=1, replica_groups=mesh['y'=4,'c'=2,'x'=4,'z'=8] {'z'}, dimensions={0} | all-to-all | bytes 1310720 | tf_op jit(solution)/shard_map/all_to_all | solution.py:46
  92.5 1.0 scale.1.own
  93.5 1.0 collective-permute-start.14
  94.5 1.1 collective-permute-start.13
  95.6 13.3 %collective-permute-done.14.right = f32[1232,128]{1,0:T(8,128)S(1)} collective-permute-done((f32[1232,128]{1,0:T(8,128)S(1)}, f32[1232,128]{1,0:T(8,128)S(1)}, u32[]{:S(2)}, u32[]{:S(2)}) %collective-permute-start.14) | collective-permute-done | bytes 630816 | tf_op jit(solution)/shard_map/ppermute | solution.py:36
  109.0 1.6 %collective-permute-start.16 = (f32[616,128]{1,0:T(8,128)S(1)}, f32[616,128]{1,0:T(8,128)S(1)}, u32[]{:S(2)}, u32[]{:S(2)}) collective-permute-start(f32[616,128]{1,0:T(8,128)S(1)} %slice.9), channel_id=1, source_target_pairs={{0,24},{8,0},{16,8},{24,16},{1,25},{9,1},{17,9},{25,17},{2,26},{10... | collective-permute-start | bytes 946184 | tf_op jit(solution)/shard_map/ppermute | solution.py:36
  110.5 0.0 collective-permute-done.13.left
  110.6 0.6 collective-permute-start.15
  111.2 5.6 %collective-permute-done.16.far_bottom = f32[616,128]{1,0:T(8,128)S(1)} collective-permute-done((f32[616,128]{1,0:T(8,128)S(1)}, f32[616,128]{1,0:T(8,128)S(1)}, u32[]{:S(2)}, u32[]{:S(2)}) %collective-permute-start.16) | collective-permute-done | bytes 315424 | tf_op jit(solution)/shard_map/ppermute | solution.py:36
  116.8 2.0 %collective-permute-done.15.far_top = f32[616,128]{1,0:T(8,128)S(1)} collective-permute-done((f32[616,128]{1,0:T(8,128)S(1)}, f32[616,128]{1,0:T(8,128)S(1)}, u32[]{:S(2)}, u32[]{:S(2)}) %collective-permute-start.15) | collective-permute-done | bytes 315424 | tf_op jit(solution)/shard_map/ppermute | solution.py:36
  118.8 1.8 %lay.1 = (f32[268,2144]{1,0:T(8,128)}, f32[64,268]{1,0:T(8,128)}) custom-call(f32[1232,128]{1,0:T(8,128)S(1)} %scale.1.own, f32[1232,128]{1,0:T(8,128)S(1)} %collective-permute-done.13.left, f32[1232,128]{1,0:T(8,128)S(1)} %collective-permute-done.14.right, f32[616,128]{1,0:T(8,128)S(1)} %collective-permute-done.15.far_top, ...), custom_call_target="tpu_custom_call" | custom-call | tf_op jit(solution)/shard_map/lay/pallas_call | solution.py:347
  (6 shorter events, 0.2 us)
Async XLA Ops:
  0.6 1.6 %copy-start = (bf16[1024,1024]{1,0:T(8,128)(2,1)S(1)}, bf16[1024,1024]{1,0:T(8,128)(2,1)}, u32[]{:S(2)}) copy-start(bf16[1024,1024]{1,0:T(8,128)(2,1)} %param.3) | copy-start | bytes 6291460
  2.2 29.6 %copy-start.1 = (s32[16]{0:T(128)S(1)}, s32[16]{0:T(128)}, u32[]{:S(2)}) copy-start(s32[16]{0:T(128)} %lengths.5) | copy-start | bytes 196
  3.7 1.4 %collective-permute-start = (f32[64,512]{1,0:T(8,128)S(1)}, f32[64,512]{1,0:T(8,128)S(1)}, u32[]{:S(2)}, u32[]{:S(2)}) collective-permute-start(f32[64,512]{1,0:T(8,128)S(1)} %constant_dynamic-slice_fusion), channel_id=1, source_target_pairs={{0,32},{32,0},{1,33},{33,1},{2,34},{34,2},{3,35},{35,3},{4,36},{36... | collective-permute-start | bytes 393224 | tf_op jit(solution)/shard_map/ppermute | solution.py:31
  5.1 6.3 %collective-permute-start.3 = (f32[64,512]{1,0:T(8,128)S(1)}, f32[64,512]{1,0:T(8,128)S(1)}, u32[]{:S(2)}, u32[]{:S(2)}) collective-permute-start(f32[64,512]{1,0:T(8,128)S(1)} %dynamic-slice_add_fusion), channel_id=1, source_target_pairs={{0,192},{64,0},{128,64},{192,128},{1,193},{65,1},{129,65},{193,129... | collective-permute-start | bytes 393224 | tf_op jit(solution)/shard_map/ppermute | solution.py:36
  7.3 6.4 %collective-permute-start.2 = (f32[64,512]{1,0:T(8,128)S(1)}, f32[64,512]{1,0:T(8,128)S(1)}, u32[]{:S(2)}, u32[]{:S(2)}) collective-permute-start(f32[64,512]{1,0:T(8,128)S(1)} %dynamic-slice_add_fusion), channel_id=1, source_target_pairs={{0,64},{64,128},{128,192},{192,0},{1,65},{65,129},{129,193},{193,1... | collective-permute-start | bytes 393224 | tf_op jit(solution)/shard_map/ppermute | solution.py:36
  7.4 7.2 %collective-permute-start.1 = (f32[64,512]{1,0:T(8,128)S(1)}, f32[64,512]{1,0:T(8,128)S(1)}, u32[]{:S(2)}, u32[]{:S(2)}) collective-permute-start(f32[64,512]{1,0:T(8,128)S(1)} %dynamic-slice_add_fusion), channel_id=1, source_target_pairs={{0,128},{64,192},{128,0},{192,64},{1,129},{65,193},{129,1},{193,65... | collective-permute-start | bytes 393224 | tf_op jit(solution)/shard_map/ppermute | solution.py:36
  14.6 6.8 %collective-permute-start.6 = (f32[64,512]{1,0:T(8,128)S(1)}, f32[64,512]{1,0:T(8,128)S(1)}, u32[]{:S(2)}, u32[]{:S(2)}) collective-permute-start(f32[64,512]{1,0:T(8,128)S(1)} %add_add_fusion.refs_0_.rest_0_), channel_id=1, source_target_pairs={{0,8},{8,16},{16,24},{24,0},{1,9},{9,17},{17,25},{25,1},{2,10},{10... | collective-permute-start | bytes 393224 | tf_op jit(solution)/shard_map/ppermute | solution.py:36
  16.2 8.4 %collective-permute-start.5 = (f32[64,512]{1,0:T(8,128)S(1)}, f32[64,512]{1,0:T(8,128)S(1)}, u32[]{:S(2)}, u32[]{:S(2)}) collective-permute-start(f32[64,512]{1,0:T(8,128)S(1)} %add_add_fusion.refs_0_.rest_0_), channel_id=1, source_target_pairs={{0,16},{8,24},{16,0},{24,8},{1,17},{9,25},{17,1},{25,9},{2,18},{10... | collective-permute-start | bytes 393224 | tf_op jit(solution)/shard_map/ppermute | solution.py:36
  18.9 5.7 %collective-permute-start.4 = (f32[64,512]{1,0:T(8,128)S(1)}, f32[64,512]{1,0:T(8,128)S(1)}, u32[]{:S(2)}, u32[]{:S(2)}) collective-permute-start(f32[64,512]{1,0:T(8,128)S(1)} %add_add_fusion.refs_0_.rest_0_), channel_id=1, source_target_pairs={{0,24},{8,0},{16,8},{24,16},{1,25},{9,1},{17,9},{25,17},{2,26},{10... | collective-permute-start | bytes 393224 | tf_op jit(solution)/shard_map/ppermute | solution.py:36
  20.3 10.5 %collective-permute-start.9 = (f32[64,512]{1,0:T(8,128)S(1)}, f32[64,512]{1,0:T(8,128)S(1)}, u32[]{:S(2)}, u32[]{:S(2)}) collective-permute-start(f32[64,512]{1,0:T(8,128)S(1)} %add_add_fusion.refs_0_.rest_0_), channel_id=1, source_target_pairs={{0,32},{32,0},{1,33},{33,1},{2,34},{34,2},{3,35},{35,3},{4,36},{36... | collective-permute-start | bytes 393224 | tf_op jit(solution)/shard_map/ppermute | solution.py:31
  21.4 10.5 %collective-permute-start.12 = (f32[64,512]{1,0:T(8,128)S(1)}, f32[64,512]{1,0:T(8,128)S(1)}, u32[]{:S(2)}, u32[]{:S(2)}) collective-permute-start(f32[64,512]{1,0:T(8,128)S(1)} %collective-permute-done.6.refs_3_.rest_3_), channel_id=1, source_target_pairs={{0,32},{32,0},{1,33},{33,1},{2,34},{34,2},{3,35},{35,3},{4,36},{36... | collective-permute-start | bytes 393224 | tf_op jit(solution)/shard_map/ppermute | solution.py:31
  24.6 7.2 %collective-permute-start.11 = (f32[64,512]{1,0:T(8,128)S(1)}, f32[64,512]{1,0:T(8,128)S(1)}, u32[]{:S(2)}, u32[]{:S(2)}) collective-permute-start(f32[64,512]{1,0:T(8,128)S(1)} %collective-permute-done.5.refs_2_.rest_2_), channel_id=1, source_target_pairs={{0,32},{32,0},{1,33},{33,1},{2,34},{34,2},{3,35},{35,3},{4,36},{36... | collective-permute-start | bytes 393224 | tf_op jit(solution)/shard_map/ppermute | solution.py:31
  24.6 7.2 %collective-permute-start.10 = (f32[64,512]{1,0:T(8,128)S(1)}, f32[64,512]{1,0:T(8,128)S(1)}, u32[]{:S(2)}, u32[]{:S(2)}) collective-permute-start(f32[64,512]{1,0:T(8,128)S(1)} %collective-permute-done.4.refs_1_.rest_1_), channel_id=1, source_target_pairs={{0,32},{32,0},{1,33},{33,1},{2,34},{34,2},{3,35},{35,3},{4,36},{36... | collective-permute-start | bytes 393224 | tf_op jit(solution)/shard_map/ppermute | solution.py:31
  25.3 14.5 %collective-permute-start.8 = (f32[64,128]{1,0:T(8,128)S(1)}, f32[64,128]{1,0:T(8,128)S(1)}, u32[]{:S(2)}, u32[]{:S(2)}) collective-permute-start(f32[64,128]{1,0:T(8,128)S(1)} %edges.1), channel_id=1, source_target_pairs={{0,39},{1,32},{2,33},{3,34},{4,35},{5,36},{6,37},{7,38},{32,1},{33... | collective-permute-start | bytes 98312 | tf_op jit(solution)/shard_map/ppermute | solution.py:381
  30.8 8.9 %collective-permute-start.7 = (f32[64,128]{1,0:T(8,128)S(1)}, f32[64,128]{1,0:T(8,128)S(1)}, u32[]{:S(2)}, u32[]{:S(2)}) collective-permute-start(f32[64,128]{1,0:T(8,128)S(1)} %edges.1), channel_id=1, source_target_pairs={{0,7},{1,0},{2,1},{3,2},{4,3},{5,4},{6,5},{7,6},{32,33},{33,34},{3... | collective-permute-start | bytes 98312 | tf_op jit(solution)/shard_map/ppermute | solution.py:380
  93.5 15.4 %collective-permute-start.14 = (f32[1232,128]{1,0:T(8,128)S(1)}, f32[1232,128]{1,0:T(8,128)S(1)}, u32[]{:S(2)}, u32[]{:S(2)}) collective-permute-start(f32[1232,128]{1,0:T(8,128)S(1)} %scale.1.own), channel_id=1, source_target_pairs={{0,24},{8,0},{16,8},{24,16},{1,25},{9,1},{17,9},{25,17},{2,26},{10... | collective-permute-start | bytes 1892360 | tf_op jit(solution)/shard_map/ppermute | solution.py:36
  94.5 16.1 %collective-permute-start.13 = (f32[1232,128]{1,0:T(8,128)S(1)}, f32[1232,128]{1,0:T(8,128)S(1)}, u32[]{:S(2)}, u32[]{:S(2)}) collective-permute-start(f32[1232,128]{1,0:T(8,128)S(1)} %scale.1.own), channel_id=1, source_target_pairs={{0,8},{8,16},{16,24},{24,0},{1,9},{9,17},{17,25},{25,1},{2,10},{10... | collective-permute-start | bytes 1892360 | tf_op jit(solution)/shard_map/ppermute | solution.py:36
  109.0 7.8 %collective-permute-start.16 = (f32[616,128]{1,0:T(8,128)S(1)}, f32[616,128]{1,0:T(8,128)S(1)}, u32[]{:S(2)}, u32[]{:S(2)}) collective-permute-start(f32[616,128]{1,0:T(8,128)S(1)} %slice.9), channel_id=1, source_target_pairs={{0,24},{8,0},{16,8},{24,16},{1,25},{9,1},{17,9},{25,17},{2,26},{10... | collective-permute-start | bytes 946184 | tf_op jit(solution)/shard_map/ppermute | solution.py:36
  110.6 8.2 %collective-permute-start.15 = (f32[616,128]{1,0:T(8,128)S(1)}, f32[616,128]{1,0:T(8,128)S(1)}, u32[]{:S(2)}, u32[]{:S(2)}) collective-permute-start(f32[616,128]{1,0:T(8,128)S(1)} %slice.8), channel_id=1, source_target_pairs={{0,8},{8,16},{16,24},{24,0},{1,9},{9,17},{17,25},{25,1},{2,10},{10... | collective-permute-start | bytes 946184 | tf_op jit(solution)/shard_map/ppermute | solution.py:36

commit v4 on v3

v4 whole, which is shorter than its diff:
```python
import functools

import jax
import jax.numpy as jnp
from jax import lax
from jax.experimental import pallas as pl
from jax.experimental.pallas import tpu as pltpu
from jax.sharding import Mesh, PartitionSpec as P


R = 64
FEAT = 2144
SLOT = 2048
TRAJ = 16
BLOCK = 1024
HALF = 512
ROWS = 268
ROWS_PAD = 272
COLS = 512
TAIL_QUADS = 96
TAIL_SIDES = 32
TAIL_ROWS = 144
TAIL_KEPT = 140
PICKS = ROWS_PAD + COLS + TAIL_QUADS
TAIL_AT = 4 * ROWS
PIECE = 152
EXTRA = 16
TILES = 8 * PIECE
OUT_TAIL = 4 * ROWS_PAD
OUT_ROWS = OUT_TAIL + TAIL_ROWS
UP = 2.0**16


def swap(value):
    return lax.ppermute(value, "c", [(0, 1), (1, 0)])


def turn(value, axis, by):
    count = lax.axis_size(axis)
    return lax.ppermute(value, axis, [(i, (i + by) % count) for i in range(count)])


def near_by(value):
    return pltpu.with_memory_space_constraint(value, pltpu.VMEM)


def everyone(value, axis):
    count = lax.axis_size(axis)
    spread = jnp.broadcast_to(value[None], (count,) + value.shape)
    return lax.all_to_all(spread, axis, 0, 0, tiled=True)


def one_hots(first_feature, count):
    lane = lax.broadcasted_iota(jnp.int32, (count, 256), 1)
    feature = lax.broadcasted_iota(jnp.int32, (count, 256), 0) + first_feature
    mode = lane & (R - 1)
    below = lane < 3 * R
    ends = R + (mode + 1) * R - (mode + 1) * mode // 2
    passed = jnp.where((lane < R) & (feature >= ends), 1.0, 0.0)
    row = jnp.sum(passed, axis=1, keepdims=True).astype(jnp.int32)
    start = R + row * R - row * (row - 1) // 2
    linear = feature < R
    first = jnp.where(linear, feature, row)
    second = jnp.where(linear, -1, feature - start + row)
    pick_first = below & (mode == first)
    pick_second = (below & (mode == second)) | (linear & (lane == 3 * R))
    as_type = lambda pick: jnp.where(pick, 1.0, 0.0).astype(jnp.bfloat16)
    return as_type(pick_first), as_type(pick_second)


def split3(value):
    high = value.astype(jnp.bfloat16)
    rest = value - high.astype(jnp.float32)
    middle = rest.astype(jnp.bfloat16)
    low = (rest - middle.astype(jnp.float32)).astype(jnp.bfloat16)
    return high, middle, low


def split2(value):
    high = value.astype(jnp.bfloat16)
    return high, (value - high.astype(jnp.float32)).astype(jnp.bfloat16)


def dot(left, right, dims):
    return lax.dot_general(left, right, (dims, ((), ())), preferred_element_type=jnp.float32)


NT = ((1,), (1,))
NN = ((1,), (0,))


def position():
    return lax.axis_index("c"), lax.axis_index("x"), lax.axis_index("z")


def pick_kernel(first_pick, second_pick):
    core, x, _ = position()
    space = lax.axis_index("y") * 2 + core
    for at, count, feature in (
        (0, ROWS_PAD, space * ROWS),
        (ROWS_PAD, COLS, x * COLS),
        (ROWS_PAD + COLS, TAIL_QUADS, 4 * COLS),
    ):
        first, second = one_hots(feature, count)
        first_pick[at : at + count, :] = first
        second_pick[at : at + count, :] = second


SMEM = pl.BlockSpec(memory_space=pltpu.SMEM)
VMEM = pl.BlockSpec(memory_space=pltpu.VMEM)
ROOM = pltpu.CompilerParams(vmem_limit_bytes=24 * 1024 * 1024)


def picks():
    return pl.pallas_call(
        pick_kernel,
        out_shape=(pltpu.VMEM((PICKS, 256), jnp.bfloat16), pltpu.VMEM((PICKS, 256), jnp.bfloat16)),
        out_specs=(VMEM, VMEM),
        compiler_params=ROOM,
        name="picks",
    )()


def whole_block(own, other, core):
    near = jnp.where(core == 0, own[...], other[...])
    far = jnp.where(core == 0, other[...], own[...])
    return jnp.concatenate([near, far], axis=1) * UP


def alive(lengths, start):
    lane = lax.broadcasted_iota(jnp.int32, (1, BLOCK), 1)
    one = lengths[(start + HALF) // SLOT % TRAJ]
    two = lengths[(start + 2 * HALF) // SLOT % TRAJ]
    offset = ((start + HALF) % SLOT + lane) & (SLOT - 1)
    limit = jnp.where(lane < HALF, one, two) - 3
    return jnp.where((offset >= 2) & (offset <= limit), 1.0, 0.0)


def features(first_pick, second_pick, stack, at, count):
    first = dot(first_pick[at : at + count, :], stack, NN)
    second = dot(second_pick[at : at + count, :], stack, NN)
    return split2(first * second)


def product(left_hi, left_lo, right_hi, right_lo):
    return dot(left_hi, right_hi, NT) + (dot(left_hi, right_lo, NT) + dot(left_lo, right_hi, NT))


def stacked(masked, stack):
    stack[:R, :], stack[R : 2 * R, :], stack[2 * R : 3 * R, :] = split3(masked)
    index = lax.broadcasted_iota(jnp.int32, masked.shape, 0)
    stack[3 * R :, :] = jnp.where(index == 0, 1.0, 0.0).astype(jnp.bfloat16)


def project_kernel(basis, snapshots, mine, other, basis_in, cells, total, arrived):
    core = lax.axis_index("c")
    parts = cells.shape[0]
    size = BLOCK // parts
    first = pltpu.make_async_copy(basis, basis_in, arrived.at[parts])
    loads = [
        pltpu.make_async_copy(snapshots.at[pl.ds(k * size, size), :], cells.at[k], arrived.at[k]) for k in range(parts)
    ]
    first.start()
    for load in loads:
        load.start()
    first.wait()
    for k, load in enumerate(loads):
        load.wait()
        part = dot(basis_in[:, k * size : (k + 1) * size], cells[k], NN)
        total[...] = part if k == 0 else total[...] + part
    low, high = total[:, :HALF], total[:, HALF:]
    mine[...] = jnp.where(core == 0, low, high)
    other[...] = jnp.where(core == 0, high, low)


def project(basis, snapshots):
    parts = 4
    return pl.pallas_call(
        project_kernel,
        out_shape=(pltpu.VMEM((R, HALF), jnp.float32), pltpu.VMEM((R, HALF), jnp.float32)),
        in_specs=[pl.BlockSpec(memory_space=pltpu.HBM)] * 2,
        out_specs=(VMEM, VMEM),
        scratch_shapes=[
            pltpu.VMEM((R, BLOCK), jnp.bfloat16),
            pltpu.VMEM((parts, BLOCK // parts, BLOCK), jnp.bfloat16),
            pltpu.VMEM((R, BLOCK), jnp.float32),
            pltpu.SemaphoreType.DMA((parts + 1,)),
        ],
        compiler_params=ROOM,
        name="project",
    )(*[pltpu.with_memory_space_constraint(v, pltpu.HBM) for v in (basis, snapshots)])


def stacked(masked, stack):
    stack[:R, :], stack[R : 2 * R, :], stack[2 * R : 3 * R, :] = split3(masked)
    index = lax.broadcasted_iota(jnp.int32, masked.shape, 0)
    stack[3 * R :, :] = jnp.where(index == 0, 1.0, 0.0).astype(jnp.bfloat16)


def add_blocks(lengths, first_pick, second_pick, steps, mine, theirs, sums, scratch, fresh):
    acc, tail, energy, ends = sums
    stack, change, rows_hi, rows_lo, cols_hi, cols_lo = scratch
    core, x, z = position()
    wide = lax.broadcasted_iota(jnp.int32, (R, BLOCK), 1)
    lane = lax.broadcasted_iota(jnp.int32, (R, 128), 1)
    part = pl.ds(pl.multiple_of(x % 2 * 128, 128), TAIL_ROWS)

    def add(ref, value, now, at=slice(None)):
        ref[:, at] = value if now else ref[:, at] + value

    for index, step in enumerate(steps):
        now = fresh and index == 0
        where = (x + step) % 4
        states = whole_block(mine[index], theirs[index], core)
        living = alive(lengths, (where * 8 + z) * BLOCK)
        before = jnp.where(wide < 1, 0.0, pltpu.roll(states, 1, 1))
        before2 = jnp.where(wide < 2, 0.0, pltpu.roll(states, 2, 1))
        after = jnp.where(wide >= BLOCK - 1, 0.0, pltpu.roll(states, BLOCK - 1, 1))
        after2 = jnp.where(wide >= BLOCK - 2, 0.0, pltpu.roll(states, BLOCK - 2, 1))
        change[...] = (before2 - 8.0 * before + 8.0 * after - after2) * (1.0 / 12.0) * living
        masked = states * living
        squares = masked * masked
        add(energy, functools.reduce(lambda a, b: a + b, [squares[:, k * 128 : (k + 1) * 128] for k in range(BLOCK // 128)]), now)
        four = states[:, 0:1]
        for e, at in ((1, 1), (2, BLOCK - 2), (3, BLOCK - 1)):
            four = jnp.where((lane & 3) == e, states[:, at : at + 1], four)
        ends[...] = jnp.where((lane >> 2) == where, four, jnp.zeros_like(four) if now else ends[...])
        stacked(masked, stack)
        rows_hi[...], rows_lo[...] = features(first_pick, second_pick, stack[...], 0, ROWS_PAD)
        for at in range(0, COLS, 256):
            right_hi, right_lo = features(first_pick, second_pick, stack[...], ROWS_PAD + at, 256)
            add(acc, product(rows_hi[...], rows_lo[...], right_hi, right_lo), now, slice(at, at + 256))
        cols_hi[:TAIL_QUADS, :], cols_lo[:TAIL_QUADS, :] = features(first_pick, second_pick, stack[...], ROWS_PAD + COLS, TAIL_QUADS)
        side = change[pl.ds(pl.multiple_of(x // 2 * TAIL_SIDES, TAIL_SIDES), TAIL_SIDES), :]
        cols_hi[TAIL_QUADS:, :], cols_lo[TAIL_QUADS:, :] = split2(side)
        add(tail, product(rows_hi[part, :], rows_lo[part, :], cols_hi[...], cols_lo[...]), now)


def gram_own_kernel(lengths, first_pick, second_pick, mine, theirs, *rest):
    add_blocks(lengths, first_pick, second_pick, (0,), (mine,), (theirs,), rest[:4], rest[4:], True)


def gram_rest_kernel(lengths, first_pick, second_pick, *rest):
    mine, theirs, given, (out, extra), sums, scratch = rest[:3], rest[3:6], rest[6:10], rest[10:12], rest[12:16], rest[16:]
    for ref, value in zip(sums, given):
        ref[...] = value[...]
    add_blocks(lengths, first_pick, second_pick, (1, 3, 2), mine, theirs, sums, scratch, False)
    acc, tail, energy, ends = sums
    for k in range(COLS // 128):
        out[k * ROWS : (k + 1) * ROWS, :] = acc[:ROWS, k * 128 : (k + 1) * 128]
    out[TAIL_AT : TAIL_AT + TAIL_KEPT, :] = tail[:TAIL_KEPT, :]
    out[TAIL_AT + TAIL_KEPT :, :] = jnp.zeros((TILES - TAIL_AT - TAIL_KEPT, 128), jnp.float32)
    total = lax.dot_general(
        jnp.ones((EXTRA, 128), jnp.float32),
        energy[...],
        (NT, ((), ())),
        precision=lax.Precision.HIGHEST,
        preferred_element_type=jnp.float32,
    )
    extra[...] = jnp.concatenate([ends[...].T[:EXTRA, :], total], axis=1)


SUMS = ((ROWS_PAD, COLS), (TAIL_ROWS, 128), (R, 128), (R, 128))
WORK = (
    pltpu.VMEM((4 * R, BLOCK), jnp.bfloat16),
    pltpu.VMEM((R, BLOCK), jnp.float32),
    pltpu.VMEM((ROWS_PAD, BLOCK), jnp.bfloat16),
    pltpu.VMEM((ROWS_PAD, BLOCK), jnp.bfloat16),
    pltpu.VMEM((128, BLOCK), jnp.bfloat16),
    pltpu.VMEM((128, BLOCK), jnp.bfloat16),
)


def gram(lengths, first_pick, second_pick, mine, theirs):
    own = pl.pallas_call(
        gram_own_kernel,
        out_shape=tuple(pltpu.VMEM(shape, jnp.float32) for shape in SUMS),
        in_specs=[SMEM] + [VMEM] * 4,
        out_specs=(VMEM,) * 4,
        scratch_shapes=WORK,
        compiler_params=ROOM,
        name="gram_own",
    )
    sums = own(lengths, *[near_by(v) for v in (first_pick, second_pick, mine[0], theirs[0])])
    order = (1, 3, 2)
    return pl.pallas_call(
        gram_rest_kernel,
        out_shape=(pltpu.VMEM((TILES, 128), jnp.float32), pltpu.VMEM((EXTRA, 128), jnp.float32)),
        in_specs=[SMEM] + [VMEM] * 12,
        out_specs=(VMEM, VMEM),
        scratch_shapes=tuple(pltpu.VMEM(shape, jnp.float32) for shape in SUMS) + WORK,
        compiler_params=ROOM,
        name="gram_rest",
    )(lengths, *[near_by(v) for v in (first_pick, second_pick, *[mine[k] for k in order], *[theirs[k] for k in order], *sums)])


def fold_kernel(parts, extra, out):
    out[:PIECE, :] = functools.reduce(lambda a, b: a + b, [parts[k] for k in range(8)])
    out[PIECE:, :] = extra[...]


def fold(parts, extra):
    return pl.pallas_call(
        fold_kernel,
        out_shape=pltpu.VMEM((PIECE + EXTRA, 128), jnp.float32),
        in_specs=[VMEM, VMEM],
        out_specs=VMEM,
        compiler_params=ROOM,
        name="fold",
    )(near_by(parts), near_by(extra))


def weights_of(lengths, energy):
    samples = lengths[0] - 4
    for k in range(1, TRAJ):
        samples += lengths[k] - 4
    samples = samples.astype(jnp.float32)
    inverse = (1.0 / UP) / jnp.sqrt(energy * (1.0 / (UP * UP)) / samples + 1e-06)
    high, middle, low = [part.astype(jnp.float32) for part in split3(inverse)]
    fill = jnp.where(lax.broadcasted_iota(jnp.int32, (8, R), 1) == 0, 1.0, 0.0)
    weights = jnp.concatenate([high, middle, low, fill], axis=1)
    tall = jnp.broadcast_to(weights[0:1, :], (128, 256)).astype(jnp.bfloat16)
    return samples, inverse, weights.astype(jnp.bfloat16), tall


def beyond_ends(lengths, first_pick, second_pick, parts, change):
    x = lax.axis_index("x")
    ends = jnp.concatenate([parts[k, PIECE:, :] for k in range(8)], axis=0).T[:R, :]
    lane = lax.broadcasted_iota(jnp.int32, (R, 128), 1)
    z, where, e = lane >> 4, (lane >> 2) & 3, lane & 3
    block = where * 8 + z
    before2 = jnp.where(z == 0, pltpu.roll(ends, 18, 1), pltpu.roll(ends, 14, 1))
    before = jnp.where(z == 0, pltpu.roll(ends, 17, 1), pltpu.roll(ends, 13, 1))
    after2 = jnp.where(z == 7, pltpu.roll(ends, 110, 1), pltpu.roll(ends, 114, 1))
    after = jnp.where(z == 7, pltpu.roll(ends, 111, 1), pltpu.roll(ends, 115, 1))
    left = jnp.where(block == 0, 0.0, jnp.where(e == 0, before2 - 8.0 * before, before2))
    right = jnp.where(block == 31, 0.0, jnp.where(e == 3, 8.0 * after - after2, -after2))
    time = block * BLOCK + jnp.where(e < 2, e, BLOCK - 4 + e) + HALF
    owner, offset = (time >> 11) & (TRAJ - 1), time & (SLOT - 1)
    limit = jnp.zeros_like(time)
    for k in range(TRAJ):
        limit = jnp.where(owner == k, lengths[k] - 3, limit)
    living = jnp.where((offset >= 2) & (offset <= limit), 1.0, 0.0)
    change[...] = jnp.where(e < 2, left, right) * (1.0 / 12.0) * living
    high, middle, low = [part.astype(jnp.float32) for part in split3(ends * living)]
    ones = jnp.where(lax.broadcasted_iota(jnp.int32, (R, 128), 0) == 0, 1.0, 0.0)
    stack = jnp.concatenate([high, middle, low, ones], axis=0).astype(jnp.bfloat16)
    part = pl.ds(pl.multiple_of(x % 2 * 128, 128), TAIL_ROWS)
    rows_hi, rows_lo = split2(dot(first_pick[part, :], stack, NN) * dot(second_pick[part, :], stack, NN))
    side = change[pl.ds(pl.multiple_of(x // 2 * TAIL_SIDES, TAIL_SIDES), TAIL_SIDES), :]
    cols_hi, cols_lo = split2(jnp.concatenate([jnp.zeros((TAIL_QUADS, 128), jnp.float32), side], axis=0))
    return product(rows_hi, rows_lo, cols_hi, cols_lo)


def scale_kernel(lengths, first_pick, second_pick, parts, out, change, row_weight, tail):
    x = lax.axis_index("x")
    energy = functools.reduce(lambda a, b: a + b, [parts[k, PIECE : PIECE + 8, R:] for k in range(8)])
    samples, inverse, weights, tall = weights_of(lengths, energy)
    row_weight[...] = dot(first_pick[:ROWS_PAD, :], tall, NT) * dot(second_pick[:ROWS_PAD, :], tall, NT) / samples
    by_column = (dot(weights, first_pick[ROWS_PAD:, :], NT) * dot(weights, second_pick[ROWS_PAD:, :], NT))[0:1, :]

    def pieces(begin, count):
        at = begin
        while at < begin + count:
            k, row = divmod(at, PIECE)
            size = min(PIECE - row, begin + count - at)
            yield at - begin, size, parts[k, row : row + size, :]
            at += size

    for k in range(COLS // 128):
        for at, size, part in pieces(k * ROWS, ROWS):
            to = k * ROWS_PAD + at
            out[to : to + size, :] = part * row_weight[at : at + size, :] * by_column[:, k * 128 : (k + 1) * 128]
    tail[...] = beyond_ends(lengths, first_pick, second_pick, parts, change)
    for at, size, part in pieces(TAIL_AT, TAIL_KEPT):
        tail[at : at + size, :] = tail[at : at + size, :] + part
    sides = jnp.where(x < 2, inverse[0:1, :TAIL_SIDES], inverse[0:1, TAIL_SIDES:])
    column = jnp.concatenate([by_column[:, COLS:], sides], axis=1)
    tail_rows = jnp.where(x % 2 == 0, row_weight[:TAIL_ROWS, :], row_weight[128:, :])
    out[OUT_TAIL:, :] = tail[...] * tail_rows * column
    for k in range(COLS // 128):
        out[k * ROWS_PAD + ROWS : (k + 1) * ROWS_PAD, :] = jnp.zeros((ROWS_PAD - ROWS, 128), jnp.float32)


def scale(lengths, first_pick, second_pick, parts):
    return pl.pallas_call(
        scale_kernel,
        out_shape=pltpu.VMEM((OUT_ROWS, 128), jnp.float32),
        in_specs=[SMEM, VMEM, VMEM, VMEM],
        out_specs=VMEM,
        scratch_shapes=[
            pltpu.VMEM((R, 128), jnp.float32),
            pltpu.VMEM((ROWS_PAD, 128), jnp.float32),
            pltpu.VMEM((TAIL_ROWS, 128), jnp.float32),
        ],
        compiler_params=ROOM,
        name="scale",
    )(lengths, *[near_by(v) for v in (first_pick, second_pick, parts)])


def lay_kernel(own, left, right, far_top, far_bottom, gram_out, side_out, tails, sides):
    x = lax.axis_index("x")
    half = OUT_ROWS // 2

    def put(source, parts):
        for k in range(COLS // 128):
            first = k * ROWS_PAD
            lanes = pl.ds(pl.multiple_of((source * 4 + k) * 128, 128), 128)
            for part, low, high in parts:
                begin, end = max(first, low), min(first + ROWS, high)
                if begin < end:
                    gram_out[begin - first : end - first, lanes] = part[begin - low : end - low, :]
        for part, low, high in parts:
            begin, end = max(OUT_TAIL, low), min(OUT_ROWS, high)
            if begin < end:
                tails[source, begin - OUT_TAIL : end - OUT_TAIL, :] = part[begin - low : end - low, :]

    put(x, [(own, 0, OUT_ROWS)])
    put((x + 3) % 4, [(left, 0, OUT_ROWS)])
    put((x + 1) % 4, [(right, 0, OUT_ROWS)])
    put((x + 2) % 4, [(far_top, 0, half), (far_bottom, half, OUT_ROWS)])
    sides[...] = jnp.zeros_like(sides)
    for x_of, low, high in ((0, 0, 128), (1, 128, ROWS)):
        count = high - low
        gram_out[low:high, 16 * 128 :] = tails[x_of, :count, :TAIL_QUADS]
        sides[low:high, :TAIL_SIDES] = tails[x_of, :count, TAIL_QUADS:]
        sides[low:high, TAIL_SIDES:R] = tails[x_of + 2, :count, TAIL_QUADS:]
    side_out[...] = sides[...].T[:R, :ROWS]


def lay(*pieces):
    return pl.pallas_call(
        lay_kernel,
        out_shape=(
            jax.ShapeDtypeStruct((ROWS, FEAT), jnp.float32),
            jax.ShapeDtypeStruct((R, ROWS), jnp.float32),
        ),
        in_specs=[VMEM] * 5,
        out_specs=(VMEM, VMEM),
        scratch_shapes=[pltpu.VMEM((4, TAIL_ROWS, 128), jnp.float32), pltpu.VMEM((384, 128), jnp.float32)],
        compiler_params=ROOM,
        name="lay",
    )(*[near_by(v) for v in pieces])


def ring(block):
    half = block.shape[0] // 2
    from_left, from_right = turn(block, "x", 1), turn(block, "x", 3)
    return block, from_left, from_right, turn(from_left[:half], "x", 1), turn(from_right[half:], "x", 3)


def shards(snapshots, basis, lengths):
    mine, other = project(basis.T, snapshots)
    half = mine + swap(other)
    message = (half + turn(half, "y", 2)) + (turn(half, "y", 1) + turn(half, "y", 3))
    first_pick, second_pick = picks()
    message, first_pick, second_pick = lax.optimization_barrier((message, first_pick, second_pick))
    across = turn(message, "x", 2)
    mine = (message, turn(message, "x", 3), across, turn(message, "x", 1))
    theirs = tuple(swap(part) for part in mine)
    block, extra = gram(lengths, first_pick, second_pick, mine, theirs)
    piece = fold(lax.all_to_all(block.reshape(8, PIECE, 128), "z", 0, 0, tiled=True), extra)
    parts = everyone(piece, "z").reshape(8, PIECE + EXTRA, 128)
    gram_out, side_out = lay(*ring(scale(lengths, first_pick, second_pick, parts)))
    return gram_out, side_out.T


def solution(mesh):
    grid = Mesh(mesh.devices.reshape(4, 2, 4, 8), ("y", "c", "x", "z"))
    return jax.shard_map(
        shards,
        mesh=grid,
        in_specs=(P(("y", "c"), ("x", "z")), P(("y", "c"), None), P()),
        out_specs=(P(("y", "c"), None), P(("y", "c"), None)),
        check_vma=False,
    )
```

time: 122 us -> 121 us (level)
  blocking collectives: 47.4 us -> 50.7 us
  starting transfers between devices: 22.8 us -> 20.7 us
  local copies, waits for them, and re-layouts: 1.69 us -> 0.09 us
  matrix products: 1.39 us -> 0 us
    ppermute x2 -> x0, starting transfers between devices: 6.56 us -> none  [the longest x1 5.55 us: shards(): lax.ppermute(edges, ('c', 'z'), [(at(0, z), at(1, z + 7)) for z in range(...]
    ppermute x10, starting transfers between devices: 15.6 us -> 20.1 us  [turn(): lax.ppermute(value, axis, [(i, (i + by) % count) for i in range(count)])]
    all_to_all x1, blocking collectives: 24.2 us -> 28 us  [shards(): lax.all_to_all(block.reshape(8, PIECE, 128), 'z', 0, 0, tiled=True)]
    unnamed x4 -> x2, local copies, waits for them, and re-layouts: 1.59 us -> 0.01 us
    dot_general x1 -> x0, matrix products: 1.39 us -> none  [shards(): jnp.einsum('cr,ct->rt', basis, snapshots, preferred_element_type=jnp.floa...]
    pallas_call x4 -> x5, Pallas kernels: 13.2 us -> 13.7 us  [the longest x1 7.49 us: gram(): pl.pallas_call(gram_rest_kernel, out_shape=(pltpu.VMEM((TILES, 128), jnp....]
  transfers between devices with their start and end apart: 17 -> 15, of which waited for: 8 -> 8; matrix products, arithmetic and copies ran while one was open for 0% -> 0% of each run, Pallas kernels for 7% -> 3%
where the time goes in v4:
time: 121 us; the launch traced here: 119 us
  blocking collectives  50.7 us (42%)
  waiting for transfers between devices  30.7 us (25%)
  starting transfers between devices  20.7 us (17%)
  Pallas kernels  16.1 us (13%)
    ppermute x10, waiting for transfers between devices, turn(): lax.ppermute(value, axis, [(i, (i + by) % count) for i in range(count)])  29.3 us
    all_to_all x1, blocking collectives, shards(): lax.all_to_all(block.reshape(8, PIECE, 128), 'z', 0, 0, tiled=True)  28 us
    all_to_all x1, blocking collectives, everyone(): return lax.all_to_all(spread, axis, 0, 0, tiled=True)  22.7 us
    ppermute x10, starting transfers between devices, turn(): lax.ppermute(value, axis, [(i, (i + by) % count) for i in range(count)])  20.1 us
    pallas_call x1, Pallas kernels, gram(): pl.pallas_call(gram_rest_kernel, out_shape=(pltpu.VMEM((TILES, 128), jnp....  7.49 us
    pallas_call x1, Pallas kernels, gram(): own(lengths, *[near_by(v) for v in (first_pick, second_pick, mine[0], the...  3.05 us
  transfers between devices with their start and end apart: 15, of which 8 were waited for; matrix products, arithmetic and copies ran while one was open for 0% of the time, Pallas kernels for 3%

profile of v4, /device:TPU:8, one launch (start us, length us, event | category | flops | bytes accessed | tf_op | source)
XLA Modules:
  0.0 119.1 jit_solution(1605544367275174565)
XLA Ops:
  0.6 0.0 copy-start
  0.6 1.9 %project.1 = (f32[64,512]{1,0:T(8,128)S(1)}, f32[64,512]{1,0:T(8,128)S(1)}) custom-call(bf16[64,1024]{1,0:T(8,128)(2,1)} %bitcast.4, bf16[1024,1024]{1,0:T(8,128)(2,1)} %snapshots.1), custom_call_target="tpu_custom_call" | custom-call | tf_op jit(solution)/shard_map/project/pallas_call | solution.py:178
  2.5 0.1 collective-permute-start
  2.6 1.3 %collective-permute-done = f32[64,512]{1,0:T(8,128)S(1)} collective-permute-done((f32[64,512]{1,0:T(8,128)S(1)}, f32[64,512]{1,0:T(8,128)S(1)}, u32[]{:S(2)}, u32[]{:S(2)}) %collective-permute-start) | collective-permute-done | bytes 131104 | tf_op jit(solution)/shard_map/ppermute | solution.py:35
  4.0 2.2 %collective-permute-start.3 = (f32[64,512]{1,0:T(8,128)S(1)}, f32[64,512]{1,0:T(8,128)S(1)}, u32[]{:S(2)}, u32[]{:S(2)}) collective-permute-start(f32[64,512]{1,0:T(8,128)S(1)} %add.12), channel_id=1, source_target_pairs={{0,192},{64,0},{128,64},{192,128},{1,193},{65,1},{129,65},{193,129... | collective-permute-start | bytes 393224 | tf_op jit(solution)/shard_map/ppermute | solution.py:40
  6.2 0.0 collective-permute-start.2
  6.2 3.4 %collective-permute-start.1 = (f32[64,512]{1,0:T(8,128)S(1)}, f32[64,512]{1,0:T(8,128)S(1)}, u32[]{:S(2)}, u32[]{:S(2)}) collective-permute-start(f32[64,512]{1,0:T(8,128)S(1)} %add.12), channel_id=1, source_target_pairs={{0,128},{64,192},{128,0},{192,64},{1,129},{65,193},{129,1},{193,65... | collective-permute-start | bytes 393224 | tf_op jit(solution)/shard_map/ppermute | solution.py:40
  9.6 0.7 picks.1
  10.3 0.0 collective-permute-done.3
  10.3 2.3 %collective-permute-done.2 = f32[64,512]{1,0:T(8,128)S(1)} collective-permute-done((f32[64,512]{1,0:T(8,128)S(1)}, f32[64,512]{1,0:T(8,128)S(1)}, u32[]{:S(2)}, u32[]{:S(2)}) %collective-permute-start.2) | collective-permute-done | bytes 131104 | tf_op jit(solution)/shard_map/ppermute | solution.py:40
  12.6 0.8 collective-permute-done.1
  13.4 3.1 %collective-permute-start.6 = (f32[64,512]{1,0:T(8,128)S(1)}, f32[64,512]{1,0:T(8,128)S(1)}, u32[]{:S(2)}, u32[]{:S(2)}) collective-permute-start(f32[64,512]{1,0:T(8,128)S(1)} %add_add_fusion.mine), channel_id=1, source_target_pairs={{0,16},{8,24},{16,0},{24,8},{1,17},{9,25},{17,1},{25,9},{2,18},{10... | collective-permute-start | bytes 393224 | tf_op jit(solution)/shard_map/ppermute | solution.py:40
  16.6 0.6 collective-permute-start.5
  17.1 2.6 %collective-permute-start.4 = (f32[64,512]{1,0:T(8,128)S(1)}, f32[64,512]{1,0:T(8,128)S(1)}, u32[]{:S(2)}, u32[]{:S(2)}) collective-permute-start(f32[64,512]{1,0:T(8,128)S(1)} %add_add_fusion.mine), channel_id=1, source_target_pairs={{0,24},{8,0},{16,8},{24,16},{1,25},{9,1},{17,9},{25,17},{2,26},{10... | collective-permute-start | bytes 393224 | tf_op jit(solution)/shard_map/ppermute | solution.py:40
  19.8 0.0 collective-permute-start.10
  19.8 1.2 %collective-permute-done.6.rest_2_ = f32[64,512]{1,0:T(8,128)S(1)} collective-permute-done((f32[64,512]{1,0:T(8,128)S(1)}, f32[64,512]{1,0:T(8,128)S(1)}, u32[]{:S(2)}, u32[]{:S(2)}) %collective-permute-start.6) | collective-permute-done | bytes 131104 | tf_op jit(solution)/shard_map/ppermute | solution.py:40
  21.0 0.0 collective-permute-start.9
  21.0 2.1 %collective-permute-done.5.rest_1_ = f32[64,512]{1,0:T(8,128)S(1)} collective-permute-done((f32[64,512]{1,0:T(8,128)S(1)}, f32[64,512]{1,0:T(8,128)S(1)}, u32[]{:S(2)}, u32[]{:S(2)}) %collective-permute-start.5) | collective-permute-done | bytes 131104 | tf_op jit(solution)/shard_map/ppermute | solution.py:40
  23.1 0.0 collective-permute-start.8
  23.1 0.0 collective-permute-done.4.rest_0_
  23.1 0.5 collective-permute-start.7
  23.6 0.0 collective-permute-done.10.theirs
  23.6 0.0 copy-done
  23.6 3.1 %gram_own.1 = (f32[272,512]{1,0:T(8,128)S(1)}, f32[144,128]{1,0:T(8,128)S(1)}, f32[64,128]{1,0:T(8,128)S(1)}, f32[64,128]{1,0:T(8,128)S(1)}) custom-call(s32[16]{0:T(128)S(1)} %copy-done, bf16[880,256]{1,0:T(8,128)(2,1)S(1)} %get-tuple-element.21.first_pick, bf16[880,256]{1,0:T(8,128)(2,1)S(1)} %get-tuple-element.22.second_pick, ...), custom_call_target="tpu_custom_call" | custom-call | tf_op jit(solution)/shard_map/gram_own/pallas_call | solution.py:284
  26.7 0.0 collective-permute-done.9.rest_5_
  26.7 0.0 collective-permute-done.8.rest_4_
  26.7 0.0 collective-permute-done.7.rest_3_
  26.7 7.5 %gram_rest.1 = (f32[1216,128]{1,0:T(8,128)S(1)}, f32[16,128]{1,0:T(8,128)S(1)}) custom-call(s32[16]{0:T(128)S(1)} %copy-done, bf16[880,256]{1,0:T(8,128)(2,1)S(1)} %get-tuple-element.21.first_pick, bf16[880,256]{1,0:T(8,128)(2,1)S(1)} %get-tuple-element.22.second_pick, f32[64,512]{1,0:T(8,128)S(1)} %collective-permute-done.4.rest_0_, ...), custom_call_target="tpu_custom_call" | custom-call | tf_op jit(solution)/shard_map/gram_rest/pallas_call | solution.py:286
  34.2 28.0 %all_to_all.10.parts = f32[8,152,128]{2,1,0:T(8,128)S(1)} all-to-all(f32[8,152,128]{2,1,0:T(8,128)S(1)} %bitcast.3), channel_id=1, replica_groups=mesh['y'=4,'c'=2,'x'=4,'z'=8] {'z'}, dimensions={0} | all-to-all | bytes 1245184 | tf_op jit(solution)/shard_map/all_to_all | solution.py:462
  62.4 22.7 %all_to_all.11.parts = f32[8,168,128]{2,1,0:T(8,128)S(1)} all-to-all(f32[8,168,128]{2,1,0:T(8,128)S(1)} %broadcast_in_dim.2), channel_id=1, replica_groups=mesh['y'=4,'c'=2,'x'=4,'z'=8] {'z'}, dimensions={0} | all-to-all | bytes 1376256 | tf_op jit(solution)/shard_map/all_to_all | solution.py:50
  85.0 1.2 %scale.1.own = f32[1232,128]{1,0:T(8,128)S(1)} custom-call(s32[16]{0:T(128)S(1)} %copy-done, bf16[880,256]{1,0:T(8,128)(2,1)S(1)} %get-tuple-element.21.first_pick, bf16[880,256]{1,0:T(8,128)(2,1)S(1)} %get-tuple-element.22.second_pick, f32[8,168,128]{2,1,0:T(8,128)S(1)} %all_to_all.11.parts), custom_call_target="tpu_custom_call" | custom-call | tf_op jit(solution)/shard_map/scale/pallas_call | solution.py:386
  86.3 4.3 %collective-permute-start.12 = (f32[1232,128]{1,0:T(8,128)S(1)}, f32[1232,128]{1,0:T(8,128)S(1)}, u32[]{:S(2)}, u32[]{:S(2)}) collective-permute-start(f32[1232,128]{1,0:T(8,128)S(1)} %scale.1.own), channel_id=1, source_target_pairs={{0,24},{8,0},{16,8},{24,16},{1,25},{9,1},{17,9},{25,17},{2,26},{10... | collective-permute-start | bytes 1892360 | tf_op jit(solution)/shard_map/ppermute | solution.py:40
  90.6 0.0 collective-permute-start.11
  90.6 13.5 %collective-permute-done.12.right = f32[1232,128]{1,0:T(8,128)S(1)} collective-permute-done((f32[1232,128]{1,0:T(8,128)S(1)}, f32[1232,128]{1,0:T(8,128)S(1)}, u32[]{:S(2)}, u32[]{:S(2)}) %collective-permute-start.12) | collective-permute-done | bytes 630816 | tf_op jit(solution)/shard_map/ppermute | solution.py:40
  104.2 3.8 %collective-permute-start.14 = (f32[616,128]{1,0:T(8,128)S(1)}, f32[616,128]{1,0:T(8,128)S(1)}, u32[]{:S(2)}, u32[]{:S(2)}) collective-permute-start(f32[616,128]{1,0:T(8,128)S(1)} %slice.9), channel_id=1, source_target_pairs={{0,24},{8,0},{16,8},{24,16},{1,25},{9,1},{17,9},{25,17},{2,26},{10... | collective-permute-start | bytes 946184 | tf_op jit(solution)/shard_map/ppermute | solution.py:40
  107.9 0.0 collective-permute-done.11.left
  108.0 0.1 collective-permute-start.13
  108.0 5.8 %collective-permute-done.14.far_bottom = f32[616,128]{1,0:T(8,128)S(1)} collective-permute-done((f32[616,128]{1,0:T(8,128)S(1)}, f32[616,128]{1,0:T(8,128)S(1)}, u32[]{:S(2)}, u32[]{:S(2)}) %collective-permute-start.14) | collective-permute-done | bytes 315424 | tf_op jit(solution)/shard_map/ppermute | solution.py:40
  113.9 3.5 %collective-permute-done.13.far_top = f32[616,128]{1,0:T(8,128)S(1)} collective-permute-done((f32[616,128]{1,0:T(8,128)S(1)}, f32[616,128]{1,0:T(8,128)S(1)}, u32[]{:S(2)}, u32[]{:S(2)}) %collective-permute-start.13) | collective-permute-done | bytes 315424 | tf_op jit(solution)/shard_map/ppermute | solution.py:40
  117.4 1.8 %lay.1 = (f32[268,2144]{1,0:T(8,128)}, f32[64,268]{1,0:T(8,128)}) custom-call(f32[1232,128]{1,0:T(8,128)S(1)} %scale.1.own, f32[1232,128]{1,0:T(8,128)S(1)} %collective-permute-done.11.left, f32[1232,128]{1,0:T(8,128)S(1)} %collective-permute-done.12.right, f32[616,128]{1,0:T(8,128)S(1)} %collective-permute-done.13.far_top, ...), custom_call_target="tpu_custom_call" | custom-call | tf_op jit(solution)/shard_map/lay/pallas_call | solution.py:432
  (6 shorter events, 0.2 us)
Async XLA Ops:
  0.6 23.0 %copy-start = (s32[16]{0:T(128)S(1)}, s32[16]{0:T(128)}, u32[]{:S(2)}) copy-start(s32[16]{0:T(128)} %lengths.5) | copy-start | bytes 196
  2.5 1.4 %collective-permute-start = (f32[64,512]{1,0:T(8,128)S(1)}, f32[64,512]{1,0:T(8,128)S(1)}, u32[]{:S(2)}, u32[]{:S(2)}) collective-permute-start(f32[64,512]{1,0:T(8,128)S(1)} %get-tuple-element.18), channel_id=1, source_target_pairs={{0,32},{32,0},{1,33},{33,1},{2,34},{34,2},{3,35},{35,3},{4,36},{36... | collective-permute-start | bytes 393224 | tf_op jit(solution)/shard_map/ppermute | solution.py:35
  4.0 6.3 %collective-permute-start.3 = (f32[64,512]{1,0:T(8,128)S(1)}, f32[64,512]{1,0:T(8,128)S(1)}, u32[]{:S(2)}, u32[]{:S(2)}) collective-permute-start(f32[64,512]{1,0:T(8,128)S(1)} %add.12), channel_id=1, source_target_pairs={{0,192},{64,0},{128,64},{192,128},{1,193},{65,1},{129,65},{193,129... | collective-permute-start | bytes 393224 | tf_op jit(solution)/shard_map/ppermute | solution.py:40
  6.2 6.4 %collective-permute-start.2 = (f32[64,512]{1,0:T(8,128)S(1)}, f32[64,512]{1,0:T(8,128)S(1)}, u32[]{:S(2)}, u32[]{:S(2)}) collective-permute-start(f32[64,512]{1,0:T(8,128)S(1)} %add.12), channel_id=1, source_target_pairs={{0,64},{64,128},{128,192},{192,0},{1,65},{65,129},{129,193},{193,1... | collective-permute-start | bytes 393224 | tf_op jit(solution)/shard_map/ppermute | solution.py:40
  6.2 7.2 %collective-permute-start.1 = (f32[64,512]{1,0:T(8,128)S(1)}, f32[64,512]{1,0:T(8,128)S(1)}, u32[]{:S(2)}, u32[]{:S(2)}) collective-permute-start(f32[64,512]{1,0:T(8,128)S(1)} %add.12), channel_id=1, source_target_pairs={{0,128},{64,192},{128,0},{192,64},{1,129},{65,193},{129,1},{193,65... | collective-permute-start | bytes 393224 | tf_op jit(solution)/shard_map/ppermute | solution.py:40
  13.4 7.6 %collective-permute-start.6 = (f32[64,512]{1,0:T(8,128)S(1)}, f32[64,512]{1,0:T(8,128)S(1)}, u32[]{:S(2)}, u32[]{:S(2)}) collective-permute-start(f32[64,512]{1,0:T(8,128)S(1)} %add_add_fusion.mine), channel_id=1, source_target_pairs={{0,16},{8,24},{16,0},{24,8},{1,17},{9,25},{17,1},{25,9},{2,18},{10... | collective-permute-start | bytes 393224 | tf_op jit(solution)/shard_map/ppermute | solution.py:40
  16.6 6.6 %collective-permute-start.5 = (f32[64,512]{1,0:T(8,128)S(1)}, f32[64,512]{1,0:T(8,128)S(1)}, u32[]{:S(2)}, u32[]{:S(2)}) collective-permute-start(f32[64,512]{1,0:T(8,128)S(1)} %add_add_fusion.mine), channel_id=1, source_target_pairs={{0,8},{8,16},{16,24},{24,0},{1,9},{9,17},{17,25},{25,1},{2,10},{10... | collective-permute-start | bytes 393224 | tf_op jit(solution)/shard_map/ppermute | solution.py:40
  17.1 6.0 %collective-permute-start.4 = (f32[64,512]{1,0:T(8,128)S(1)}, f32[64,512]{1,0:T(8,128)S(1)}, u32[]{:S(2)}, u32[]{:S(2)}) collective-permute-start(f32[64,512]{1,0:T(8,128)S(1)} %add_add_fusion.mine), channel_id=1, source_target_pairs={{0,24},{8,0},{16,8},{24,16},{1,25},{9,1},{17,9},{25,17},{2,26},{10... | collective-permute-start | bytes 393224 | tf_op jit(solution)/shard_map/ppermute | solution.py:40
  19.8 3.9 %collective-permute-start.10 = (f32[64,512]{1,0:T(8,128)S(1)}, f32[64,512]{1,0:T(8,128)S(1)}, u32[]{:S(2)}, u32[]{:S(2)}) collective-permute-start(f32[64,512]{1,0:T(8,128)S(1)} %add_add_fusion.mine), channel_id=1, source_target_pairs={{0,32},{32,0},{1,33},{33,1},{2,34},{34,2},{3,35},{35,3},{4,36},{36... | collective-permute-start | bytes 393224 | tf_op jit(solution)/shard_map/ppermute | solution.py:35
  21.0 5.7 %collective-permute-start.9 = (f32[64,512]{1,0:T(8,128)S(1)}, f32[64,512]{1,0:T(8,128)S(1)}, u32[]{:S(2)}, u32[]{:S(2)}) collective-permute-start(f32[64,512]{1,0:T(8,128)S(1)} %collective-permute-done.6.rest_2_), channel_id=1, source_target_pairs={{0,32},{32,0},{1,33},{33,1},{2,34},{34,2},{3,35},{35,3},{4,36},{36... | collective-permute-start | bytes 393224 | tf_op jit(solution)/shard_map/ppermute | solution.py:35
  23.1 3.6 %collective-permute-start.8 = (f32[64,512]{1,0:T(8,128)S(1)}, f32[64,512]{1,0:T(8,128)S(1)}, u32[]{:S(2)}, u32[]{:S(2)}) collective-permute-start(f32[64,512]{1,0:T(8,128)S(1)} %collective-permute-done.5.rest_1_), channel_id=1, source_target_pairs={{0,32},{32,0},{1,33},{33,1},{2,34},{34,2},{3,35},{35,3},{4,36},{36... | collective-permute-start | bytes 393224 | tf_op jit(solution)/shard_map/ppermute | solution.py:35
  23.1 3.6 %collective-permute-start.7 = (f32[64,512]{1,0:T(8,128)S(1)}, f32[64,512]{1,0:T(8,128)S(1)}, u32[]{:S(2)}, u32[]{:S(2)}) collective-permute-start(f32[64,512]{1,0:T(8,128)S(1)} %collective-permute-done.4.rest_0_), channel_id=1, source_target_pairs={{0,32},{32,0},{1,33},{33,1},{2,34},{34,2},{3,35},{35,3},{4,36},{36... | collective-permute-start | bytes 393224 | tf_op jit(solution)/shard_map/ppermute | solution.py:35
  86.3 17.9 %collective-permute-start.12 = (f32[1232,128]{1,0:T(8,128)S(1)}, f32[1232,128]{1,0:T(8,128)S(1)}, u32[]{:S(2)}, u32[]{:S(2)}) collective-permute-start(f32[1232,128]{1,0:T(8,128)S(1)} %scale.1.own), channel_id=1, source_target_pairs={{0,24},{8,0},{16,8},{24,16},{1,25},{9,1},{17,9},{25,17},{2,26},{10... | collective-permute-start | bytes 1892360 | tf_op jit(solution)/shard_map/ppermute | solution.py:40
  90.6 17.3 %collective-permute-start.11 = (f32[1232,128]{1,0:T(8,128)S(1)}, f32[1232,128]{1,0:T(8,128)S(1)}, u32[]{:S(2)}, u32[]{:S(2)}) collective-permute-start(f32[1232,128]{1,0:T(8,128)S(1)} %scale.1.own), channel_id=1, source_target_pairs={{0,8},{8,16},{16,24},{24,0},{1,9},{9,17},{17,25},{25,1},{2,10},{10... | collective-permute-start | bytes 1892360 | tf_op jit(solution)/shard_map/ppermute | solution.py:40
  104.2 9.7 %collective-permute-start.14 = (f32[616,128]{1,0:T(8,128)S(1)}, f32[616,128]{1,0:T(8,128)S(1)}, u32[]{:S(2)}, u32[]{:S(2)}) collective-permute-start(f32[616,128]{1,0:T(8,128)S(1)} %slice.9), channel_id=1, source_target_pairs={{0,24},{8,0},{16,8},{24,16},{1,25},{9,1},{17,9},{25,17},{2,26},{10... | collective-permute-start | bytes 946184 | tf_op jit(solution)/shard_map/ppermute | solution.py:40
  108.0 9.4 %collective-permute-start.13 = (f32[616,128]{1,0:T(8,128)S(1)}, f32[616,128]{1,0:T(8,128)S(1)}, u32[]{:S(2)}, u32[]{:S(2)}) collective-permute-start(f32[616,128]{1,0:T(8,128)S(1)} %slice.8), channel_id=1, source_target_pairs={{0,8},{8,16},{16,24},{24,0},{1,9},{9,17},{17,25},{25,1},{2,10},{10... | collective-permute-start | bytes 946184 | tf_op jit(solution)/shard_map/ppermute | solution.py:40

commit v5 on v4

--- a/solution.py
+++ b/solution.py
@@ -24,10 +24,12 @@
 PICKS = ROWS_PAD + COLS + TAIL_QUADS
 TAIL_AT = 4 * ROWS
 PIECE = 152
-EXTRA = 16
+EXTRA = 8
 TILES = 8 * PIECE
+ENERGY_AT = TAIL_AT + TAIL_KEPT
 OUT_TAIL = 4 * ROWS_PAD
 OUT_ROWS = OUT_TAIL + TAIL_ROWS
+OUT_HALF = OUT_ROWS // 2
 UP = 2.0**16
 
 
@@ -197,7 +199,7 @@
     stack[3 * R :, :] = jnp.where(index == 0, 1.0, 0.0).astype(jnp.bfloat16)
 
 
-def add_blocks(lengths, first_pick, second_pick, steps, mine, theirs, sums, scratch, fresh):
+def add_blocks(lengths, first_pick, second_pick, steps, mine, theirs, sums, scratch, fresh, out=None):
     acc, tail, energy, ends = sums
     stack, change, rows_hi, rows_lo, cols_hi, cols_lo = scratch
     core, x, z = position()
@@ -229,7 +231,13 @@
         rows_hi[...], rows_lo[...] = features(first_pick, second_pick, stack[...], 0, ROWS_PAD)
         for at in range(0, COLS, 256):
             right_hi, right_lo = features(first_pick, second_pick, stack[...], ROWS_PAD + at, 256)
-            add(acc, product(rows_hi[...], rows_lo[...], right_hi, right_lo), now, slice(at, at + 256))
+            value = product(rows_hi[...], rows_lo[...], right_hi, right_lo)
+            if out is None:
+                add(acc, value, now, slice(at, at + 256))
+                continue
+            value = acc[:, at : at + 256] + value
+            for k in range(at // 128, at // 128 + 2):
+                out[k * ROWS : (k + 1) * ROWS, :] = value[:ROWS, k * 128 - at : (k + 1) * 128 - at]
         cols_hi[:TAIL_QUADS, :], cols_lo[:TAIL_QUADS, :] = features(first_pick, second_pick, stack[...], ROWS_PAD + COLS, TAIL_QUADS)
         side = change[pl.ds(pl.multiple_of(x // 2 * TAIL_SIDES, TAIL_SIDES), TAIL_SIDES), :]
         cols_hi[TAIL_QUADS:, :], cols_lo[TAIL_QUADS:, :] = split2(side)
@@ -240,24 +248,29 @@
     add_blocks(lengths, first_pick, second_pick, (0,), (mine,), (theirs,), rest[:4], rest[4:], True)
 
 
-def gram_rest_kernel(lengths, first_pick, second_pick, *rest):
-    mine, theirs, given, (out, extra), sums, scratch = rest[:3], rest[3:6], rest[6:10], rest[10:12], rest[12:16], rest[16:]
-    for ref, value in zip(sums, given):
+def gram_beside_kernel(lengths, first_pick, second_pick, *rest):
+    mine, theirs, sums, scratch = rest[:2], rest[2:4], rest[8:12], rest[12:]
+    add_blocks(lengths, first_pick, second_pick, (1, 3), mine, theirs, sums, scratch, False)
+
+
+def gram_across_kernel(lengths, first_pick, second_pick, *rest):
+    mine, theirs, given, (out, extra), more, scratch = rest[:1], rest[1:2], rest[2:6], rest[6:8], rest[8:11], rest[11:]
+    for ref, value in zip(more, given[1:]):
         ref[...] = value[...]
-    add_blocks(lengths, first_pick, second_pick, (1, 3, 2), mine, theirs, sums, scratch, False)
-    acc, tail, energy, ends = sums
-    for k in range(COLS // 128):
-        out[k * ROWS : (k + 1) * ROWS, :] = acc[:ROWS, k * 128 : (k + 1) * 128]
+    sums = (given[0], *more)
+    add_blocks(lengths, first_pick, second_pick, (2,), mine, theirs, sums, scratch, False, out)
+    _, tail, energy, ends = sums
     out[TAIL_AT : TAIL_AT + TAIL_KEPT, :] = tail[:TAIL_KEPT, :]
-    out[TAIL_AT + TAIL_KEPT :, :] = jnp.zeros((TILES - TAIL_AT - TAIL_KEPT, 128), jnp.float32)
     total = lax.dot_general(
-        jnp.ones((EXTRA, 128), jnp.float32),
+        jnp.ones((8, 128), jnp.float32),
         energy[...],
         (NT, ((), ())),
         precision=lax.Precision.HIGHEST,
         preferred_element_type=jnp.float32,
     )
-    extra[...] = jnp.concatenate([ends[...].T[:EXTRA, :], total], axis=1)
+    out[ENERGY_AT:, :] = jnp.concatenate([total, jnp.zeros_like(total)], axis=1)[: TILES - ENERGY_AT, :]
+    flat = ends[...].T
+    extra[...] = jnp.concatenate([flat[:EXTRA, :], flat[EXTRA : 2 * EXTRA, :]], axis=1)
 
 
 SUMS = ((ROWS_PAD, COLS), (TAIL_ROWS, 128), (R, 128), (R, 128))
@@ -272,26 +285,39 @@
 
 
 def gram(lengths, first_pick, second_pick, mine, theirs):
+    shapes = tuple(pltpu.VMEM(shape, jnp.float32) for shape in SUMS)
     own = pl.pallas_call(
         gram_own_kernel,
-        out_shape=tuple(pltpu.VMEM(shape, jnp.float32) for shape in SUMS),
+        out_shape=shapes,
         in_specs=[SMEM] + [VMEM] * 4,
         out_specs=(VMEM,) * 4,
         scratch_shapes=WORK,
         compiler_params=ROOM,
         name="gram_own",
     )
-    sums = own(lengths, *[near_by(v) for v in (first_pick, second_pick, mine[0], theirs[0])])
-    order = (1, 3, 2)
-    return pl.pallas_call(
-        gram_rest_kernel,
+    beside = pl.pallas_call(
+        gram_beside_kernel,
+        out_shape=shapes,
+        in_specs=[SMEM] + [VMEM] * 10,
+        out_specs=(VMEM,) * 4,
+        scratch_shapes=WORK,
+        input_output_aliases={7 + k: k for k in range(4)},
+        compiler_params=ROOM,
+        name="gram_beside",
+    )
+    across = pl.pallas_call(
+        gram_across_kernel,
         out_shape=(pltpu.VMEM((TILES, 128), jnp.float32), pltpu.VMEM((EXTRA, 128), jnp.float32)),
-        in_specs=[SMEM] + [VMEM] * 12,
+        in_specs=[SMEM] + [VMEM] * 8,
         out_specs=(VMEM, VMEM),
-        scratch_shapes=tuple(pltpu.VMEM(shape, jnp.float32) for shape in SUMS) + WORK,
-        compiler_params=ROOM,
-        name="gram_rest",
-    )(lengths, *[near_by(v) for v in (first_pick, second_pick, *[mine[k] for k in order], *[theirs[k] for k in order], *sums)])
+        scratch_shapes=tuple(pltpu.VMEM(shape, jnp.float32) for shape in SUMS[1:]) + WORK,
+        compiler_params=ROOM,
+        name="gram_across",
+    )
+    kept = [near_by(v) for v in (first_pick, second_pick)]
+    sums = own(lengths, *kept, near_by(mine[0]), near_by(theirs[0]))
+    sums = beside(lengths, *kept, *[near_by(v) for v in (mine[1], mine[3], theirs[1], theirs[3], *sums)])
+    return across(lengths, *kept, *[near_by(v) for v in (mine[2], theirs[2], *sums)])
 
 
 def fold_kernel(parts, extra, out):
@@ -325,7 +351,9 @@
 
 def beyond_ends(lengths, first_pick, second_pick, parts, change):
     x = lax.axis_index("x")
-    ends = jnp.concatenate([parts[k, PIECE:, :] for k in range(8)], axis=0).T[:R, :]
+    flat = [parts[k, PIECE:, at : at + R] for k in range(8) for at in (0, R)]
+    flat = jnp.concatenate(flat, axis=0)
+    ends = jnp.concatenate([flat, flat], axis=1).T[:R, :]
     lane = lax.broadcasted_iota(jnp.int32, (R, 128), 1)
     z, where, e = lane >> 4, (lane >> 2) & 3, lane & 3
     block = where * 8 + z
@@ -352,9 +380,18 @@
     return product(rows_hi, rows_lo, cols_hi, cols_lo)
 
 
-def scale_kernel(lengths, first_pick, second_pick, parts, out, change, row_weight, tail):
+def scale_kernel(lengths, first_pick, second_pick, parts, top, bottom, change, row_weight, tail):
     x = lax.axis_index("x")
-    energy = functools.reduce(lambda a, b: a + b, [parts[k, PIECE : PIECE + 8, R:] for k in range(8)])
+
+    def put(at, value):
+        cut = min(max(OUT_HALF - at, 0), value.shape[0])
+        if cut:
+            top[at : at + cut, :] = value[:cut, :]
+        if cut < value.shape[0]:
+            bottom[at + cut - OUT_HALF : at + value.shape[0] - OUT_HALF, :] = value[cut:, :]
+
+    at = ENERGY_AT - 7 * PIECE
+    energy = jnp.broadcast_to(parts[7, at : at + 1, :R], (8, R))
     samples, inverse, weights, tall = weights_of(lengths, energy)
     row_weight[...] = dot(first_pick[:ROWS_PAD, :], tall, NT) * dot(second_pick[:ROWS_PAD, :], tall, NT) / samples
     by_column = (dot(weights, first_pick[ROWS_PAD:, :], NT) * dot(weights, second_pick[ROWS_PAD:, :], NT))[0:1, :]
@@ -369,25 +406,24 @@
 
     for k in range(COLS // 128):
         for at, size, part in pieces(k * ROWS, ROWS):
-            to = k * ROWS_PAD + at
-            out[to : to + size, :] = part * row_weight[at : at + size, :] * by_column[:, k * 128 : (k + 1) * 128]
+            put(k * ROWS_PAD + at, part * row_weight[at : at + size, :] * by_column[:, k * 128 : (k + 1) * 128])
     tail[...] = beyond_ends(lengths, first_pick, second_pick, parts, change)
     for at, size, part in pieces(TAIL_AT, TAIL_KEPT):
         tail[at : at + size, :] = tail[at : at + size, :] + part
     sides = jnp.where(x < 2, inverse[0:1, :TAIL_SIDES], inverse[0:1, TAIL_SIDES:])
     column = jnp.concatenate([by_column[:, COLS:], sides], axis=1)
     tail_rows = jnp.where(x % 2 == 0, row_weight[:TAIL_ROWS, :], row_weight[128:, :])
-    out[OUT_TAIL:, :] = tail[...] * tail_rows * column
+    put(OUT_TAIL, tail[...] * tail_rows * column)
     for k in range(COLS // 128):
-        out[k * ROWS_PAD + ROWS : (k + 1) * ROWS_PAD, :] = jnp.zeros((ROWS_PAD - ROWS, 128), jnp.float32)
+        put(k * ROWS_PAD + ROWS, jnp.zeros((ROWS_PAD - ROWS, 128), jnp.float32))
 
 
 def scale(lengths, first_pick, second_pick, parts):
     return pl.pallas_call(
         scale_kernel,
-        out_shape=pltpu.VMEM((OUT_ROWS, 128), jnp.float32),
+        out_shape=(pltpu.VMEM((OUT_HALF, 128), jnp.float32), pltpu.VMEM((OUT_HALF, 128), jnp.float32)),
         in_specs=[SMEM, VMEM, VMEM, VMEM],
-        out_specs=VMEM,
+        out_specs=(VMEM, VMEM),
         scratch_shapes=[
             pltpu.VMEM((R, 128), jnp.float32),
             pltpu.VMEM((ROWS_PAD, 128), jnp.float32),
@@ -398,9 +434,9 @@
     )(lengths, *[near_by(v) for v in (first_pick, second_pick, parts)])
 
 
-def lay_kernel(own, left, right, far_top, far_bottom, gram_out, side_out, tails, sides):
+def lay_kernel(*refs):
+    pieces, (gram_out, side_out, tails, sides) = refs[:8], refs[8:]
     x = lax.axis_index("x")
-    half = OUT_ROWS // 2
 
     def put(source, parts):
         for k in range(COLS // 128):
@@ -415,10 +451,8 @@
             if begin < end:
                 tails[source, begin - OUT_TAIL : end - OUT_TAIL, :] = part[begin - low : end - low, :]
 
-    put(x, [(own, 0, OUT_ROWS)])
-    put((x + 3) % 4, [(left, 0, OUT_ROWS)])
-    put((x + 1) % 4, [(right, 0, OUT_ROWS)])
-    put((x + 2) % 4, [(far_top, 0, half), (far_bottom, half, OUT_ROWS)])
+    for by, top, bottom in zip((0, 3, 1, 2), pieces[::2], pieces[1::2]):
+        put((x + by) % 4, [(top, 0, OUT_HALF), (bottom, OUT_HALF, OUT_ROWS)])
     sides[...] = jnp.zeros_like(sides)
     for x_of, low, high in ((0, 0, 128), (1, 128, ROWS)):
         count = high - low
@@ -435,7 +469,7 @@
             jax.ShapeDtypeStruct((ROWS, FEAT), jnp.float32),
             jax.ShapeDtypeStruct((R, ROWS), jnp.float32),
         ),
-        in_specs=[VMEM] * 5,
+        in_specs=[VMEM] * 8,
         out_specs=(VMEM, VMEM),
         scratch_shapes=[pltpu.VMEM((4, TAIL_ROWS, 128), jnp.float32), pltpu.VMEM((384, 128), jnp.float32)],
         compiler_params=ROOM,
@@ -443,10 +477,11 @@
     )(*[near_by(v) for v in pieces])
 
 
-def ring(block):
-    half = block.shape[0] // 2
-    from_left, from_right = turn(block, "x", 1), turn(block, "x", 3)
-    return block, from_left, from_right, turn(from_left[:half], "x", 1), turn(from_right[half:], "x", 3)
+def ring(top, bottom):
+    left_top, right_bottom = turn(top, "x", 1), turn(bottom, "x", 3)
+    left_bottom, right_top = turn(bottom, "x", 1), turn(top, "x", 3)
+    far_top, far_bottom = turn(left_top, "x", 1), turn(right_bottom, "x", 3)
+    return top, bottom, left_top, left_bottom, right_top, right_bottom, far_top, far_bottom
 
 
 def shards(snapshots, basis, lengths):
@@ -457,11 +492,12 @@
     message, first_pick, second_pick = lax.optimization_barrier((message, first_pick, second_pick))
     across = turn(message, "x", 2)
     mine = (message, turn(message, "x", 3), across, turn(message, "x", 1))
-    theirs = tuple(swap(part) for part in mine)
+    theirs = tuple(swap(part) for part in (mine[0], mine[1], mine[3]))
+    theirs = (*theirs[:2], swap(across), theirs[2])
     block, extra = gram(lengths, first_pick, second_pick, mine, theirs)
     piece = fold(lax.all_to_all(block.reshape(8, PIECE, 128), "z", 0, 0, tiled=True), extra)
     parts = everyone(piece, "z").reshape(8, PIECE + EXTRA, 128)
-    gram_out, side_out = lay(*ring(scale(lengths, first_pick, second_pick, parts)))
+    gram_out, side_out = lay(*ring(*scale(lengths, first_pick, second_pick, parts)))
     return gram_out, side_out.T
 
 

time: 121 us -> 116 us (0.959)
  the two profiles are of different devices: /device:TPU:8 before, /device:TPU:6 now
where the time goes in v5:
time: 116 us
  blocking collectives  50 us (43%)
  waiting for transfers between devices  29.5 us (25%)
  starting transfers between devices  19 us (16%)
  Pallas kernels  17 us (15%)
    ppermute x12, waiting for transfers between devices, turn(): lax.ppermute(value, axis, [(i, (i + by) % count) for i in range(count)])  28.1 us
    all_to_all x1, blocking collectives, shards(): lax.all_to_all(block.reshape(8, PIECE, 128), 'z', 0, 0, tiled=True)  28 us
    all_to_all x1, blocking collectives, everyone(): return lax.all_to_all(spread, axis, 0, 0, tiled=True)  21.9 us
    ppermute x12, starting transfers between devices, turn(): lax.ppermute(value, axis, [(i, (i + by) % count) for i in range(count)])  18.4 us
    pallas_call x1, Pallas kernels, gram(): beside(lengths, *kept, *[near_by(v) for v in (mine[1], mine[3], theirs[1]...  5.29 us
    pallas_call x1, Pallas kernels, gram(): across(lengths, *kept, *[near_by(v) for v in (mine[2], theirs[2], *sums)])  3.07 us
    pallas_call x1, Pallas kernels, gram(): sums = own(lengths, *kept, near_by(mine[0]), near_by(theirs[0]))  3.06 us
  transfers between devices with their start and end apart: 17, of which 9 were waited for; matrix products, arithmetic and copies ran while one was open for 0% of the time, Pallas kernels for 8%

profile of v5, /device:TPU:6, one launch (start us, length us, event | category | flops | bytes accessed | tf_op | source)
XLA Modules:
  0.0 116.3 jit_solution(3061719550159009685)
XLA Ops:
  0.6 0.0 copy-start
  0.6 1.9 %project.1 = (f32[64,512]{1,0:T(8,128)S(1)}, f32[64,512]{1,0:T(8,128)S(1)}) custom-call(bf16[64,1024]{1,0:T(8,128)(2,1)} %bitcast.4, bf16[1024,1024]{1,0:T(8,128)(2,1)} %snapshots.1), custom_call_target="tpu_custom_call" | custom-call | tf_op jit(solution)/shard_map/project/pallas_call | solution.py:180
  2.5 0.1 collective-permute-start
  2.6 1.3 %collective-permute-done = f32[64,512]{1,0:T(8,128)S(1)} collective-permute-done((f32[64,512]{1,0:T(8,128)S(1)}, f32[64,512]{1,0:T(8,128)S(1)}, u32[]{:S(2)}, u32[]{:S(2)}) %collective-permute-start) | collective-permute-done | bytes 131104 | tf_op jit(solution)/shard_map/ppermute | solution.py:37
  4.0 3.1 %collective-permute-start.3 = (f32[64,512]{1,0:T(8,128)S(1)}, f32[64,512]{1,0:T(8,128)S(1)}, u32[]{:S(2)}, u32[]{:S(2)}) collective-permute-start(f32[64,512]{1,0:T(8,128)S(1)} %add.12), channel_id=1, source_target_pairs={{0,192},{64,0},{128,64},{192,128},{1,193},{65,1},{129,65},{193,129... | collective-permute-start | bytes 393224 | tf_op jit(solution)/shard_map/ppermute | solution.py:42
  7.0 0.0 collective-permute-start.2
  7.1 2.2 %collective-permute-start.1 = (f32[64,512]{1,0:T(8,128)S(1)}, f32[64,512]{1,0:T(8,128)S(1)}, u32[]{:S(2)}, u32[]{:S(2)}) collective-permute-start(f32[64,512]{1,0:T(8,128)S(1)} %add.12), channel_id=1, source_target_pairs={{0,128},{64,192},{128,0},{192,64},{1,129},{65,193},{129,1},{193,65... | collective-permute-start | bytes 393224 | tf_op jit(solution)/shard_map/ppermute | solution.py:42
  9.3 0.7 picks.1
  10.0 0.2 collective-permute-done.3
  10.1 6.2 %collective-permute-done.2 = f32[64,512]{1,0:T(8,128)S(1)} collective-permute-done((f32[64,512]{1,0:T(8,128)S(1)}, f32[64,512]{1,0:T(8,128)S(1)}, u32[]{:S(2)}, u32[]{:S(2)}) %collective-permute-start.2) | collective-permute-done | bytes 131104 | tf_op jit(solution)/shard_map/ppermute | solution.py:42
  16.3 0.0 collective-permute-done.1
  16.4 0.6 collective-permute-start.7
  16.9 1.5 %collective-permute-start.6 = (f32[64,512]{1,0:T(8,128)S(1)}, f32[64,512]{1,0:T(8,128)S(1)}, u32[]{:S(2)}, u32[]{:S(2)}) collective-permute-start(f32[64,512]{1,0:T(8,128)S(1)} %add_add_fusion.mine), channel_id=1, source_target_pairs={{0,24},{8,0},{16,8},{24,16},{1,25},{9,1},{17,9},{25,17},{2,26},{10... | collective-permute-start | bytes 393224 | tf_op jit(solution)/shard_map/ppermute | solution.py:42
  18.5 1.4 %collective-permute-start.4 = (f32[64,512]{1,0:T(8,128)S(1)}, f32[64,512]{1,0:T(8,128)S(1)}, u32[]{:S(2)}, u32[]{:S(2)}) collective-permute-start(f32[64,512]{1,0:T(8,128)S(1)} %add_add_fusion.mine), channel_id=1, source_target_pairs={{0,16},{8,24},{16,0},{24,8},{1,17},{9,25},{17,1},{25,9},{2,18},{10... | collective-permute-start | bytes 393224 | tf_op jit(solution)/shard_map/ppermute | solution.py:42
  19.9 0.0 collective-permute-start.10
  19.9 2.7 %collective-permute-done.7.rest_1_ = f32[64,512]{1,0:T(8,128)S(1)} collective-permute-done((f32[64,512]{1,0:T(8,128)S(1)}, f32[64,512]{1,0:T(8,128)S(1)}, u32[]{:S(2)}, u32[]{:S(2)}) %collective-permute-start.7) | collective-permute-done | bytes 131104 | tf_op jit(solution)/shard_map/ppermute | solution.py:42
  22.6 0.0 collective-permute-start.9
  22.6 3.0 %collective-permute-done.6.rest_0_ = f32[64,512]{1,0:T(8,128)S(1)} collective-permute-done((f32[64,512]{1,0:T(8,128)S(1)}, f32[64,512]{1,0:T(8,128)S(1)}, u32[]{:S(2)}, u32[]{:S(2)}) %collective-permute-start.6) | collective-permute-done | bytes 131104 | tf_op jit(solution)/shard_map/ppermute | solution.py:42
  25.6 0.0 collective-permute-start.8
  25.6 0.0 collective-permute-done.4.rest_0_
  25.6 0.5 collective-permute-start.5
  26.1 0.0 collective-permute-done.10.theirs
  26.1 0.0 copy-done
  26.1 3.1 %gram_own.1 = (f32[272,512]{1,0:T(8,128)S(1)}, f32[144,128]{1,0:T(8,128)S(1)}, f32[64,128]{1,0:T(8,128)S(1)}, f32[64,128]{1,0:T(8,128)S(1)}) custom-call(s32[16]{0:T(128)S(1)} %copy-done, bf16[880,256]{1,0:T(8,128)(2,1)S(1)} %get-tuple-element.27.first_pick, bf16[880,256]{1,0:T(8,128)(2,1)S(1)} %get-tuple-element.28.second_pick, ...), custom_call_target="tpu_custom_call" | custom-call | tf_op jit(solution)/shard_map/gram_own/pallas_call | solution.py:318
  29.2 0.0 collective-permute-done.9.rest_3_
  29.2 0.0 collective-permute-done.8.rest_2_
  29.2 5.3 %gram_beside.1 = (f32[272,512]{1,0:T(8,128)S(1)}, f32[144,128]{1,0:T(8,128)S(1)}, f32[64,128]{1,0:T(8,128)S(1)}, f32[64,128]{1,0:T(8,128)S(1)}) custom-call(s32[16]{0:T(128)S(1)} %copy-done, bf16[880,256]{1,0:T(8,128)(2,1)S(1)} %get-tuple-element.27.first_pick, ...), custom_call_target="tpu_custom_call", output_to_operand_aliasing={{0}: (7, {}), {1}: (8, {}), {2}: (9, {}), {3}: (10, {})} | custom-call | tf_op jit(solution)/shard_map/gram_beside/pallas_call | solution.py:319
  34.5 0.0 collective-permute-done.5.rest_1_
  34.5 3.1 %gram_across.1 = (f32[1216,128]{1,0:T(8,128)S(1)}, f32[8,128]{1,0:T(8,128)S(1)}) custom-call(s32[16]{0:T(128)S(1)} %copy-done, bf16[880,256]{1,0:T(8,128)(2,1)S(1)} %get-tuple-element.27.first_pick, bf16[880,256]{1,0:T(8,128)(2,1)S(1)} %get-tuple-element.28.second_pick, f32[64,512]{1,0:T(8,128)S(1)} %collective-permute-done.4.rest_0_, ...), custom_call_target="tpu_custom_call" | custom-call | tf_op jit(solution)/shard_map/gram_across/pallas_call | solution.py:320
  37.6 28.0 %all_to_all.10.parts = f32[8,152,128]{2,1,0:T(8,128)S(1)} all-to-all(f32[8,152,128]{2,1,0:T(8,128)S(1)} %bitcast.3), channel_id=1, replica_groups=mesh['y'=4,'c'=2,'x'=4,'z'=8] {'z'}, dimensions={0} | all-to-all | bytes 1245184 | tf_op jit(solution)/shard_map/all_to_all | solution.py:498
  65.7 21.9 %all_to_all.11.parts = f32[8,160,128]{2,1,0:T(8,128)S(1)} all-to-all(f32[8,160,128]{2,1,0:T(8,128)S(1)} %broadcast_in_dim.2), channel_id=1, replica_groups=mesh['y'=4,'c'=2,'x'=4,'z'=8] {'z'}, dimensions={0} | all-to-all | bytes 1310720 | tf_op jit(solution)/shard_map/all_to_all | solution.py:52
  87.7 1.3 %scale.1 = (f32[616,128]{1,0:T(8,128)S(1)}, f32[616,128]{1,0:T(8,128)S(1)}) custom-call(s32[16]{0:T(128)S(1)} %copy-done, bf16[880,256]{1,0:T(8,128)(2,1)S(1)} %get-tuple-element.27.first_pick, bf16[880,256]{1,0:T(8,128)(2,1)S(1)} %get-tuple-element.28.second_pick, f32[8,160,128]{2,1,0:T(8,128)S(1)} %all_to_all.11.parts), custom_call_target="tpu_custom_call" | custom-call | tf_op jit(solution)/shard_map/scale/pallas_call | solution.py:422
  88.9 2.6 %collective-permute-start.11 = (f32[616,128]{1,0:T(8,128)S(1)}, f32[616,128]{1,0:T(8,128)S(1)}, u32[]{:S(2)}, u32[]{:S(2)}) collective-permute-start(f32[616,128]{1,0:T(8,128)S(1)} %get-tuple-element.40.refs_0_), channel_id=1, source_target_pairs={{0,8},{8,16},{16,24},{24,0},{1,9},{9,17},{17,25},{25,1},{2,10},{10... | collective-permute-start | bytes 946184 | tf_op jit(solution)/shard_map/ppermute | solution.py:42
  91.5 0.0 collective-permute-start.14
  91.5 0.9 collective-permute-start.13
  92.4 2.4 %collective-permute-start.12 = (f32[616,128]{1,0:T(8,128)S(1)}, f32[616,128]{1,0:T(8,128)S(1)}, u32[]{:S(2)}, u32[]{:S(2)}) collective-permute-start(f32[616,128]{1,0:T(8,128)S(1)} %get-tuple-element.41.refs_1_), channel_id=1, source_target_pairs={{0,8},{8,16},{16,24},{24,0},{1,9},{9,17},{17,25},{25,1},{2,10},{10... | collective-permute-start | bytes 946184 | tf_op jit(solution)/shard_map/ppermute | solution.py:42
  94.8 4.6 %collective-permute-done.11.refs_2_ = f32[616,128]{1,0:T(8,128)S(1)} collective-permute-done((f32[616,128]{1,0:T(8,128)S(1)}, f32[616,128]{1,0:T(8,128)S(1)}, u32[]{:S(2)}, u32[]{:S(2)}) %collective-permute-start.11) | collective-permute-done | bytes 315424 | tf_op jit(solution)/shard_map/ppermute | solution.py:42
  99.4 3.7 %collective-permute-start.15 = (f32[616,128]{1,0:T(8,128)S(1)}, f32[616,128]{1,0:T(8,128)S(1)}, u32[]{:S(2)}, u32[]{:S(2)}) collective-permute-start(f32[616,128]{1,0:T(8,128)S(1)} %collective-permute-done.11.refs_2_), channel_id=1, source_target_pairs={{0,8},{8,16},{16,24},{24,0},{1,9},{9,17},{17,25},{25,1},{2,10},{10... | collective-permute-start | bytes 946184 | tf_op jit(solution)/shard_map/ppermute | solution.py:42
  103.1 0.0 collective-permute-done.14.refs_5_
  103.1 0.0 collective-permute-start.16
  103.1 6.8 %collective-permute-done.13.refs_4_ = f32[616,128]{1,0:T(8,128)S(1)} collective-permute-done((f32[616,128]{1,0:T(8,128)S(1)}, f32[616,128]{1,0:T(8,128)S(1)}, u32[]{:S(2)}, u32[]{:S(2)}) %collective-permute-start.13) | collective-permute-done | bytes 315424 | tf_op jit(solution)/shard_map/ppermute | solution.py:42
  109.8 0.0 collective-permute-done.12.refs_3_
  109.8 1.3 %collective-permute-done.15.refs_6_ = f32[616,128]{1,0:T(8,128)S(1)} collective-permute-done((f32[616,128]{1,0:T(8,128)S(1)}, f32[616,128]{1,0:T(8,128)S(1)}, u32[]{:S(2)}, u32[]{:S(2)}) %collective-permute-start.15) | collective-permute-done | bytes 315424 | tf_op jit(solution)/shard_map/ppermute | solution.py:42
  111.1 3.4 %collective-permute-done.16.refs_7_ = f32[616,128]{1,0:T(8,128)S(1)} collective-permute-done((f32[616,128]{1,0:T(8,128)S(1)}, f32[616,128]{1,0:T(8,128)S(1)}, u32[]{:S(2)}, u32[]{:S(2)}) %collective-permute-start.16) | collective-permute-done | bytes 315424 | tf_op jit(solution)/shard_map/ppermute | solution.py:42
  114.5 1.8 %lay.1 = (f32[268,2144]{1,0:T(8,128)}, f32[64,268]{1,0:T(8,128)}) custom-call(f32[616,128]{1,0:T(8,128)S(1)} %get-tuple-element.40.refs_0_, f32[616,128]{1,0:T(8,128)S(1)} %get-tuple-element.41.refs_1_, f32[616,128]{1,0:T(8,128)S(1)} %collective-permute-done.11.refs_2_, f32[616,128]{1,0:T(8,128)S(1)} %collective-permute-done.12.refs_3_, ...), custom_call_target="tpu_custom_call" | custom-call | tf_op jit(solution)/shard_map/lay/pallas_call | solution.py:466
  (4 shorter events, 0.1 us)
Async XLA Ops:
  0.6 25.5 %copy-start = (s32[16]{0:T(128)S(1)}, s32[16]{0:T(128)}, u32[]{:S(2)}) copy-start(s32[16]{0:T(128)} %lengths.7) | copy-start | bytes 196
  2.5 1.4 %collective-permute-start = (f32[64,512]{1,0:T(8,128)S(1)}, f32[64,512]{1,0:T(8,128)S(1)}, u32[]{:S(2)}, u32[]{:S(2)}) collective-permute-start(f32[64,512]{1,0:T(8,128)S(1)} %get-tuple-element.24), channel_id=1, source_target_pairs={{0,32},{32,0},{1,33},{33,1},{2,34},{34,2},{3,35},{35,3},{4,36},{36... | collective-permute-start | bytes 393224 | tf_op jit(solution)/shard_map/ppermute | solution.py:37
  4.0 6.2 %collective-permute-start.3 = (f32[64,512]{1,0:T(8,128)S(1)}, f32[64,512]{1,0:T(8,128)S(1)}, u32[]{:S(2)}, u32[]{:S(2)}) collective-permute-start(f32[64,512]{1,0:T(8,128)S(1)} %add.12), channel_id=1, source_target_pairs={{0,192},{64,0},{128,64},{192,128},{1,193},{65,1},{129,65},{193,129... | collective-permute-start | bytes 393224 | tf_op jit(solution)/shard_map/ppermute | solution.py:42
  7.0 9.3 %collective-permute-start.2 = (f32[64,512]{1,0:T(8,128)S(1)}, f32[64,512]{1,0:T(8,128)S(1)}, u32[]{:S(2)}, u32[]{:S(2)}) collective-permute-start(f32[64,512]{1,0:T(8,128)S(1)} %add.12), channel_id=1, source_target_pairs={{0,64},{64,128},{128,192},{192,0},{1,65},{65,129},{129,193},{193,1... | collective-permute-start | bytes 393224 | tf_op jit(solution)/shard_map/ppermute | solution.py:42
  7.1 9.3 %collective-permute-start.1 = (f32[64,512]{1,0:T(8,128)S(1)}, f32[64,512]{1,0:T(8,128)S(1)}, u32[]{:S(2)}, u32[]{:S(2)}) collective-permute-start(f32[64,512]{1,0:T(8,128)S(1)} %add.12), channel_id=1, source_target_pairs={{0,128},{64,192},{128,0},{192,64},{1,129},{65,193},{129,1},{193,65... | collective-permute-start | bytes 393224 | tf_op jit(solution)/shard_map/ppermute | solution.py:42
  16.4 6.2 %collective-permute-start.7 = (f32[64,512]{1,0:T(8,128)S(1)}, f32[64,512]{1,0:T(8,128)S(1)}, u32[]{:S(2)}, u32[]{:S(2)}) collective-permute-start(f32[64,512]{1,0:T(8,128)S(1)} %add_add_fusion.mine), channel_id=1, source_target_pairs={{0,8},{8,16},{16,24},{24,0},{1,9},{9,17},{17,25},{25,1},{2,10},{10... | collective-permute-start | bytes 393224 | tf_op jit(solution)/shard_map/ppermute | solution.py:42
  16.9 8.7 %collective-permute-start.6 = (f32[64,512]{1,0:T(8,128)S(1)}, f32[64,512]{1,0:T(8,128)S(1)}, u32[]{:S(2)}, u32[]{:S(2)}) collective-permute-start(f32[64,512]{1,0:T(8,128)S(1)} %add_add_fusion.mine), channel_id=1, source_target_pairs={{0,24},{8,0},{16,8},{24,16},{1,25},{9,1},{17,9},{25,17},{2,26},{10... | collective-permute-start | bytes 393224 | tf_op jit(solution)/shard_map/ppermute | solution.py:42
  18.5 7.1 %collective-permute-start.4 = (f32[64,512]{1,0:T(8,128)S(1)}, f32[64,512]{1,0:T(8,128)S(1)}, u32[]{:S(2)}, u32[]{:S(2)}) collective-permute-start(f32[64,512]{1,0:T(8,128)S(1)} %add_add_fusion.mine), channel_id=1, source_target_pairs={{0,16},{8,24},{16,0},{24,8},{1,17},{9,25},{17,1},{25,9},{2,18},{10... | collective-permute-start | bytes 393224 | tf_op jit(solution)/shard_map/ppermute | solution.py:42
  19.9 6.2 %collective-permute-start.10 = (f32[64,512]{1,0:T(8,128)S(1)}, f32[64,512]{1,0:T(8,128)S(1)}, u32[]{:S(2)}, u32[]{:S(2)}) collective-permute-start(f32[64,512]{1,0:T(8,128)S(1)} %add_add_fusion.mine), channel_id=1, source_target_pairs={{0,32},{32,0},{1,33},{33,1},{2,34},{34,2},{3,35},{35,3},{4,36},{36... | collective-permute-start | bytes 393224 | tf_op jit(solution)/shard_map/ppermute | solution.py:37
  22.6 6.6 %collective-permute-start.9 = (f32[64,512]{1,0:T(8,128)S(1)}, f32[64,512]{1,0:T(8,128)S(1)}, u32[]{:S(2)}, u32[]{:S(2)}) collective-permute-start(f32[64,512]{1,0:T(8,128)S(1)} %collective-permute-done.7.rest_1_), channel_id=1, source_target_pairs={{0,32},{32,0},{1,33},{33,1},{2,34},{34,2},{3,35},{35,3},{4,36},{36... | collective-permute-start | bytes 393224 | tf_op jit(solution)/shard_map/ppermute | solution.py:37
  25.6 3.6 %collective-permute-start.8 = (f32[64,512]{1,0:T(8,128)S(1)}, f32[64,512]{1,0:T(8,128)S(1)}, u32[]{:S(2)}, u32[]{:S(2)}) collective-permute-start(f32[64,512]{1,0:T(8,128)S(1)} %collective-permute-done.6.rest_0_), channel_id=1, source_target_pairs={{0,32},{32,0},{1,33},{33,1},{2,34},{34,2},{3,35},{35,3},{4,36},{36... | collective-permute-start | bytes 393224 | tf_op jit(solution)/shard_map/ppermute | solution.py:37
  25.6 8.9 %collective-permute-start.5 = (f32[64,512]{1,0:T(8,128)S(1)}, f32[64,512]{1,0:T(8,128)S(1)}, u32[]{:S(2)}, u32[]{:S(2)}) collective-permute-start(f32[64,512]{1,0:T(8,128)S(1)} %collective-permute-done.4.rest_0_), channel_id=1, source_target_pairs={{0,32},{32,0},{1,33},{33,1},{2,34},{34,2},{3,35},{35,3},{4,36},{36... | collective-permute-start | bytes 393224 | tf_op jit(solution)/shard_map/ppermute | solution.py:37
  88.9 10.4 %collective-permute-start.11 = (f32[616,128]{1,0:T(8,128)S(1)}, f32[616,128]{1,0:T(8,128)S(1)}, u32[]{:S(2)}, u32[]{:S(2)}) collective-permute-start(f32[616,128]{1,0:T(8,128)S(1)} %get-tuple-element.40.refs_0_), channel_id=1, source_target_pairs={{0,8},{8,16},{16,24},{24,0},{1,9},{9,17},{17,25},{25,1},{2,10},{10... | collective-permute-start | bytes 946184 | tf_op jit(solution)/shard_map/ppermute | solution.py:42
  91.5 11.5 %collective-permute-start.14 = (f32[616,128]{1,0:T(8,128)S(1)}, f32[616,128]{1,0:T(8,128)S(1)}, u32[]{:S(2)}, u32[]{:S(2)}) collective-permute-start(f32[616,128]{1,0:T(8,128)S(1)} %get-tuple-element.41.refs_1_), channel_id=1, source_target_pairs={{0,24},{8,0},{16,8},{24,16},{1,25},{9,1},{17,9},{25,17},{2,26},{10... | collective-permute-start | bytes 946184 | tf_op jit(solution)/shard_map/ppermute | solution.py:42
  91.5 18.3 %collective-permute-start.13 = (f32[616,128]{1,0:T(8,128)S(1)}, f32[616,128]{1,0:T(8,128)S(1)}, u32[]{:S(2)}, u32[]{:S(2)}) collective-permute-start(f32[616,128]{1,0:T(8,128)S(1)} %get-tuple-element.40.refs_0_), channel_id=1, source_target_pairs={{0,24},{8,0},{16,8},{24,16},{1,25},{9,1},{17,9},{25,17},{2,26},{10... | collective-permute-start | bytes 946184 | tf_op jit(solution)/shard_map/ppermute | solution.py:42
  92.4 17.4 %collective-permute-start.12 = (f32[616,128]{1,0:T(8,128)S(1)}, f32[616,128]{1,0:T(8,128)S(1)}, u32[]{:S(2)}, u32[]{:S(2)}) collective-permute-start(f32[616,128]{1,0:T(8,128)S(1)} %get-tuple-element.41.refs_1_), channel_id=1, source_target_pairs={{0,8},{8,16},{16,24},{24,0},{1,9},{9,17},{17,25},{25,1},{2,10},{10... | collective-permute-start | bytes 946184 | tf_op jit(solution)/shard_map/ppermute | solution.py:42
  99.4 11.8 %collective-permute-start.15 = (f32[616,128]{1,0:T(8,128)S(1)}, f32[616,128]{1,0:T(8,128)S(1)}, u32[]{:S(2)}, u32[]{:S(2)}) collective-permute-start(f32[616,128]{1,0:T(8,128)S(1)} %collective-permute-done.11.refs_2_), channel_id=1, source_target_pairs={{0,8},{8,16},{16,24},{24,0},{1,9},{9,17},{17,25},{25,1},{2,10},{10... | collective-permute-start | bytes 946184 | tf_op jit(solution)/shard_map/ppermute | solution.py:42
  103.1 11.5 %collective-permute-start.16 = (f32[616,128]{1,0:T(8,128)S(1)}, f32[616,128]{1,0:T(8,128)S(1)}, u32[]{:S(2)}, u32[]{:S(2)}) collective-permute-start(f32[616,128]{1,0:T(8,128)S(1)} %collective-permute-done.14.refs_5_), channel_id=1, source_target_pairs={{0,24},{8,0},{16,8},{24,16},{1,25},{9,1},{17,9},{25,17},{2,26},{10... | collective-permute-start | bytes 946184 | tf_op jit(solution)/shard_map/ppermute | solution.py:42

commit v6 on v5

--- a/solution.py
+++ b/solution.py
@@ -145,7 +145,7 @@
 
 
 def product(left_hi, left_lo, right_hi, right_lo):
-    return dot(left_hi, right_hi, NT) + (dot(left_hi, right_lo, NT) + dot(left_lo, right_hi, NT))
+    return dot(left_hi, right_hi, NT) + dot(left_lo, right_hi, NT) + dot(left_hi, right_lo, NT)
 
 
 def stacked(masked, stack):
@@ -229,18 +229,22 @@
         ends[...] = jnp.where((lane >> 2) == where, four, jnp.zeros_like(four) if now else ends[...])
         stacked(masked, stack)
         rows_hi[...], rows_lo[...] = features(first_pick, second_pick, stack[...], 0, ROWS_PAD)
+        right = features(first_pick, second_pick, stack[...], ROWS_PAD, 256)
         for at in range(0, COLS, 256):
-            right_hi, right_lo = features(first_pick, second_pick, stack[...], ROWS_PAD + at, 256)
-            value = product(rows_hi[...], rows_lo[...], right_hi, right_lo)
+            if at + 256 < COLS:
+                coming = features(first_pick, second_pick, stack[...], ROWS_PAD + at + 256, 256)
+            else:
+                cols_hi[:TAIL_QUADS, :], cols_lo[:TAIL_QUADS, :] = features(first_pick, second_pick, stack[...], ROWS_PAD + COLS, TAIL_QUADS)
+                side = change[pl.ds(pl.multiple_of(x // 2 * TAIL_SIDES, TAIL_SIDES), TAIL_SIDES), :]
+                cols_hi[TAIL_QUADS:, :], cols_lo[TAIL_QUADS:, :] = split2(side)
+            value = product(rows_hi[...], rows_lo[...], *right)
+            right = coming
             if out is None:
                 add(acc, value, now, slice(at, at + 256))
                 continue
             value = acc[:, at : at + 256] + value
             for k in range(at // 128, at // 128 + 2):
                 out[k * ROWS : (k + 1) * ROWS, :] = value[:ROWS, k * 128 - at : (k + 1) * 128 - at]
-        cols_hi[:TAIL_QUADS, :], cols_lo[:TAIL_QUADS, :] = features(first_pick, second_pick, stack[...], ROWS_PAD + COLS, TAIL_QUADS)
-        side = change[pl.ds(pl.multiple_of(x // 2 * TAIL_SIDES, TAIL_SIDES), TAIL_SIDES), :]
-        cols_hi[TAIL_QUADS:, :], cols_lo[TAIL_QUADS:, :] = split2(side)
         add(tail, product(rows_hi[part, :], rows_lo[part, :], cols_hi[...], cols_lo[...]), now)
 
 

time: 116 us -> 116 us (level)
  no operation moved by 1% of the time
where the time goes in v6:
time: 116 us
  blocking collectives  50 us (43%)
  waiting for transfers between devices  29.5 us (25%)
  starting transfers between devices  19 us (16%)
  Pallas kernels  16.8 us (14%)
    ppermute x12, waiting for transfers between devices, turn(): lax.ppermute(value, axis, [(i, (i + by) % count) for i in range(count)])  28.1 us
    all_to_all x1, blocking collectives, shards(): lax.all_to_all(block.reshape(8, PIECE, 128), 'z', 0, 0, tiled=True)  28 us
    all_to_all x1, blocking collectives, everyone(): return lax.all_to_all(spread, axis, 0, 0, tiled=True)  21.9 us
    ppermute x12, starting transfers between devices, turn(): lax.ppermute(value, axis, [(i, (i + by) % count) for i in range(count)])  18.4 us
    pallas_call x1, Pallas kernels, gram(): beside(lengths, *kept, *[near_by(v) for v in (mine[1], mine[3], theirs[1]...  5.16 us
    pallas_call x1, Pallas kernels, gram(): across(lengths, *kept, *[near_by(v) for v in (mine[2], theirs[2], *sums)])  3.06 us
    pallas_call x1, Pallas kernels, gram(): sums = own(lengths, *kept, near_by(mine[0]), near_by(theirs[0]))  2.99 us
  transfers between devices with their start and end apart: 17, of which 9 were waited for; matrix products, arithmetic and copies ran while one was open for 0% of the time, Pallas kernels for 8%

profile of v6, /device:TPU:6, one launch (start us, length us, event | category | flops | bytes accessed | tf_op | source)
XLA Modules:
  0.0 116.1 jit_solution(194286820047520605)
XLA Ops:
  0.6 0.0 copy-start
  0.6 1.9 %project.1 = (f32[64,512]{1,0:T(8,128)S(1)}, f32[64,512]{1,0:T(8,128)S(1)}) custom-call(bf16[64,1024]{1,0:T(8,128)(2,1)} %bitcast.4, bf16[1024,1024]{1,0:T(8,128)(2,1)} %snapshots.1), custom_call_target="tpu_custom_call" | custom-call | tf_op jit(solution)/shard_map/project/pallas_call | solution.py:180
  2.5 0.1 collective-permute-start
  2.6 1.3 %collective-permute-done = f32[64,512]{1,0:T(8,128)S(1)} collective-permute-done((f32[64,512]{1,0:T(8,128)S(1)}, f32[64,512]{1,0:T(8,128)S(1)}, u32[]{:S(2)}, u32[]{:S(2)}) %collective-permute-start) | collective-permute-done | bytes 131104 | tf_op jit(solution)/shard_map/ppermute | solution.py:37
  4.0 3.1 %collective-permute-start.3 = (f32[64,512]{1,0:T(8,128)S(1)}, f32[64,512]{1,0:T(8,128)S(1)}, u32[]{:S(2)}, u32[]{:S(2)}) collective-permute-start(f32[64,512]{1,0:T(8,128)S(1)} %add.12), channel_id=1, source_target_pairs={{0,192},{64,0},{128,64},{192,128},{1,193},{65,1},{129,65},{193,129... | collective-permute-start | bytes 393224 | tf_op jit(solution)/shard_map/ppermute | solution.py:42
  7.0 0.0 collective-permute-start.2
  7.1 2.2 %collective-permute-start.1 = (f32[64,512]{1,0:T(8,128)S(1)}, f32[64,512]{1,0:T(8,128)S(1)}, u32[]{:S(2)}, u32[]{:S(2)}) collective-permute-start(f32[64,512]{1,0:T(8,128)S(1)} %add.12), channel_id=1, source_target_pairs={{0,128},{64,192},{128,0},{192,64},{1,129},{65,193},{129,1},{193,65... | collective-permute-start | bytes 393224 | tf_op jit(solution)/shard_map/ppermute | solution.py:42
  9.3 0.7 picks.1
  10.0 0.2 collective-permute-done.3
  10.1 6.2 %collective-permute-done.2 = f32[64,512]{1,0:T(8,128)S(1)} collective-permute-done((f32[64,512]{1,0:T(8,128)S(1)}, f32[64,512]{1,0:T(8,128)S(1)}, u32[]{:S(2)}, u32[]{:S(2)}) %collective-permute-start.2) | collective-permute-done | bytes 131104 | tf_op jit(solution)/shard_map/ppermute | solution.py:42
  16.3 0.0 collective-permute-done.1
  16.4 0.6 collective-permute-start.7
  16.9 1.5 %collective-permute-start.6 = (f32[64,512]{1,0:T(8,128)S(1)}, f32[64,512]{1,0:T(8,128)S(1)}, u32[]{:S(2)}, u32[]{:S(2)}) collective-permute-start(f32[64,512]{1,0:T(8,128)S(1)} %add_add_fusion.mine), channel_id=1, source_target_pairs={{0,24},{8,0},{16,8},{24,16},{1,25},{9,1},{17,9},{25,17},{2,26},{10... | collective-permute-start | bytes 393224 | tf_op jit(solution)/shard_map/ppermute | solution.py:42
  18.5 1.4 %collective-permute-start.4 = (f32[64,512]{1,0:T(8,128)S(1)}, f32[64,512]{1,0:T(8,128)S(1)}, u32[]{:S(2)}, u32[]{:S(2)}) collective-permute-start(f32[64,512]{1,0:T(8,128)S(1)} %add_add_fusion.mine), channel_id=1, source_target_pairs={{0,16},{8,24},{16,0},{24,8},{1,17},{9,25},{17,1},{25,9},{2,18},{10... | collective-permute-start | bytes 393224 | tf_op jit(solution)/shard_map/ppermute | solution.py:42
  19.9 0.0 collective-permute-start.10
  19.9 2.7 %collective-permute-done.7.rest_1_ = f32[64,512]{1,0:T(8,128)S(1)} collective-permute-done((f32[64,512]{1,0:T(8,128)S(1)}, f32[64,512]{1,0:T(8,128)S(1)}, u32[]{:S(2)}, u32[]{:S(2)}) %collective-permute-start.7) | collective-permute-done | bytes 131104 | tf_op jit(solution)/shard_map/ppermute | solution.py:42
  22.6 0.0 collective-permute-start.9
  22.6 3.0 %collective-permute-done.6.rest_0_ = f32[64,512]{1,0:T(8,128)S(1)} collective-permute-done((f32[64,512]{1,0:T(8,128)S(1)}, f32[64,512]{1,0:T(8,128)S(1)}, u32[]{:S(2)}, u32[]{:S(2)}) %collective-permute-start.6) | collective-permute-done | bytes 131104 | tf_op jit(solution)/shard_map/ppermute | solution.py:42
  25.6 0.0 collective-permute-start.8
  25.6 0.0 collective-permute-done.4.rest_0_
  25.6 0.5 collective-permute-start.5
  26.1 0.0 collective-permute-done.10.theirs
  26.1 0.0 copy-done
  26.1 3.0 %gram_own.1 = (f32[272,512]{1,0:T(8,128)S(1)}, f32[144,128]{1,0:T(8,128)S(1)}, f32[64,128]{1,0:T(8,128)S(1)}, f32[64,128]{1,0:T(8,128)S(1)}) custom-call(s32[16]{0:T(128)S(1)} %copy-done, bf16[880,256]{1,0:T(8,128)(2,1)S(1)} %get-tuple-element.27.first_pick, bf16[880,256]{1,0:T(8,128)(2,1)S(1)} %get-tuple-element.28.second_pick, ...), custom_call_target="tpu_custom_call" | custom-call | tf_op jit(solution)/shard_map/gram_own/pallas_call | solution.py:322
  29.1 0.0 collective-permute-done.9.rest_3_
  29.1 0.0 collective-permute-done.8.rest_2_
  29.1 5.2 %gram_beside.1 = (f32[272,512]{1,0:T(8,128)S(1)}, f32[144,128]{1,0:T(8,128)S(1)}, f32[64,128]{1,0:T(8,128)S(1)}, f32[64,128]{1,0:T(8,128)S(1)}) custom-call(s32[16]{0:T(128)S(1)} %copy-done, bf16[880,256]{1,0:T(8,128)(2,1)S(1)} %get-tuple-element.27.first_pick, ...), custom_call_target="tpu_custom_call", output_to_operand_aliasing={{0}: (7, {}), {1}: (8, {}), {2}: (9, {}), {3}: (10, {})} | custom-call | tf_op jit(solution)/shard_map/gram_beside/pallas_call | solution.py:323
  34.3 0.0 collective-permute-done.5.rest_1_
  34.3 3.1 %gram_across.1 = (f32[1216,128]{1,0:T(8,128)S(1)}, f32[8,128]{1,0:T(8,128)S(1)}) custom-call(s32[16]{0:T(128)S(1)} %copy-done, bf16[880,256]{1,0:T(8,128)(2,1)S(1)} %get-tuple-element.27.first_pick, bf16[880,256]{1,0:T(8,128)(2,1)S(1)} %get-tuple-element.28.second_pick, f32[64,512]{1,0:T(8,128)S(1)} %collective-permute-done.4.rest_0_, ...), custom_call_target="tpu_custom_call" | custom-call | tf_op jit(solution)/shard_map/gram_across/pallas_call | solution.py:324
  37.4 28.0 %all_to_all.10.parts = f32[8,152,128]{2,1,0:T(8,128)S(1)} all-to-all(f32[8,152,128]{2,1,0:T(8,128)S(1)} %bitcast.3), channel_id=1, replica_groups=mesh['y'=4,'c'=2,'x'=4,'z'=8] {'z'}, dimensions={0} | all-to-all | bytes 1245184 | tf_op jit(solution)/shard_map/all_to_all | solution.py:502
  65.5 21.9 %all_to_all.11.parts = f32[8,160,128]{2,1,0:T(8,128)S(1)} all-to-all(f32[8,160,128]{2,1,0:T(8,128)S(1)} %broadcast_in_dim.2), channel_id=1, replica_groups=mesh['y'=4,'c'=2,'x'=4,'z'=8] {'z'}, dimensions={0} | all-to-all | bytes 1310720 | tf_op jit(solution)/shard_map/all_to_all | solution.py:52
  87.5 1.3 %scale.1 = (f32[616,128]{1,0:T(8,128)S(1)}, f32[616,128]{1,0:T(8,128)S(1)}) custom-call(s32[16]{0:T(128)S(1)} %copy-done, bf16[880,256]{1,0:T(8,128)(2,1)S(1)} %get-tuple-element.27.first_pick, bf16[880,256]{1,0:T(8,128)(2,1)S(1)} %get-tuple-element.28.second_pick, f32[8,160,128]{2,1,0:T(8,128)S(1)} %all_to_all.11.parts), custom_call_target="tpu_custom_call" | custom-call | tf_op jit(solution)/shard_map/scale/pallas_call | solution.py:426
  88.7 2.6 %collective-permute-start.11 = (f32[616,128]{1,0:T(8,128)S(1)}, f32[616,128]{1,0:T(8,128)S(1)}, u32[]{:S(2)}, u32[]{:S(2)}) collective-permute-start(f32[616,128]{1,0:T(8,128)S(1)} %get-tuple-element.40.refs_0_), channel_id=1, source_target_pairs={{0,8},{8,16},{16,24},{24,0},{1,9},{9,17},{17,25},{25,1},{2,10},{10... | collective-permute-start | bytes 946184 | tf_op jit(solution)/shard_map/ppermute | solution.py:42
  91.3 0.0 collective-permute-start.14
  91.3 0.9 collective-permute-start.13
  92.2 2.4 %collective-permute-start.12 = (f32[616,128]{1,0:T(8,128)S(1)}, f32[616,128]{1,0:T(8,128)S(1)}, u32[]{:S(2)}, u32[]{:S(2)}) collective-permute-start(f32[616,128]{1,0:T(8,128)S(1)} %get-tuple-element.41.refs_1_), channel_id=1, source_target_pairs={{0,8},{8,16},{16,24},{24,0},{1,9},{9,17},{17,25},{25,1},{2,10},{10... | collective-permute-start | bytes 946184 | tf_op jit(solution)/shard_map/ppermute | solution.py:42
  94.6 4.6 %collective-permute-done.11.refs_2_ = f32[616,128]{1,0:T(8,128)S(1)} collective-permute-done((f32[616,128]{1,0:T(8,128)S(1)}, f32[616,128]{1,0:T(8,128)S(1)}, u32[]{:S(2)}, u32[]{:S(2)}) %collective-permute-start.11) | collective-permute-done | bytes 315424 | tf_op jit(solution)/shard_map/ppermute | solution.py:42
  99.2 3.7 %collective-permute-start.15 = (f32[616,128]{1,0:T(8,128)S(1)}, f32[616,128]{1,0:T(8,128)S(1)}, u32[]{:S(2)}, u32[]{:S(2)}) collective-permute-start(f32[616,128]{1,0:T(8,128)S(1)} %collective-permute-done.11.refs_2_), channel_id=1, source_target_pairs={{0,8},{8,16},{16,24},{24,0},{1,9},{9,17},{17,25},{25,1},{2,10},{10... | collective-permute-start | bytes 946184 | tf_op jit(solution)/shard_map/ppermute | solution.py:42
  102.9 0.0 collective-permute-done.14.refs_5_
  102.9 0.0 collective-permute-start.16
  102.9 6.8 %collective-permute-done.13.refs_4_ = f32[616,128]{1,0:T(8,128)S(1)} collective-permute-done((f32[616,128]{1,0:T(8,128)S(1)}, f32[616,128]{1,0:T(8,128)S(1)}, u32[]{:S(2)}, u32[]{:S(2)}) %collective-permute-start.13) | collective-permute-done | bytes 315424 | tf_op jit(solution)/shard_map/ppermute | solution.py:42
  109.6 0.0 collective-permute-done.12.refs_3_
  109.6 1.3 %collective-permute-done.15.refs_6_ = f32[616,128]{1,0:T(8,128)S(1)} collective-permute-done((f32[616,128]{1,0:T(8,128)S(1)}, f32[616,128]{1,0:T(8,128)S(1)}, u32[]{:S(2)}, u32[]{:S(2)}) %collective-permute-start.15) | collective-permute-done | bytes 315424 | tf_op jit(solution)/shard_map/ppermute | solution.py:42
  110.9 3.4 %collective-permute-done.16.refs_7_ = f32[616,128]{1,0:T(8,128)S(1)} collective-permute-done((f32[616,128]{1,0:T(8,128)S(1)}, f32[616,128]{1,0:T(8,128)S(1)}, u32[]{:S(2)}, u32[]{:S(2)}) %collective-permute-start.16) | collective-permute-done | bytes 315424 | tf_op jit(solution)/shard_map/ppermute | solution.py:42
  114.4 1.8 %lay.1 = (f32[268,2144]{1,0:T(8,128)}, f32[64,268]{1,0:T(8,128)}) custom-call(f32[616,128]{1,0:T(8,128)S(1)} %get-tuple-element.40.refs_0_, f32[616,128]{1,0:T(8,128)S(1)} %get-tuple-element.41.refs_1_, f32[616,128]{1,0:T(8,128)S(1)} %collective-permute-done.11.refs_2_, f32[616,128]{1,0:T(8,128)S(1)} %collective-permute-done.12.refs_3_, ...), custom_call_target="tpu_custom_call" | custom-call | tf_op jit(solution)/shard_map/lay/pallas_call | solution.py:470
  (4 shorter events, 0.1 us)
Async XLA Ops:
  0.6 25.5 %copy-start = (s32[16]{0:T(128)S(1)}, s32[16]{0:T(128)}, u32[]{:S(2)}) copy-start(s32[16]{0:T(128)} %lengths.7) | copy-start | bytes 196
  2.5 1.4 %collective-permute-start = (f32[64,512]{1,0:T(8,128)S(1)}, f32[64,512]{1,0:T(8,128)S(1)}, u32[]{:S(2)}, u32[]{:S(2)}) collective-permute-start(f32[64,512]{1,0:T(8,128)S(1)} %get-tuple-element.24), channel_id=1, source_target_pairs={{0,32},{32,0},{1,33},{33,1},{2,34},{34,2},{3,35},{35,3},{4,36},{36... | collective-permute-start | bytes 393224 | tf_op jit(solution)/shard_map/ppermute | solution.py:37
  4.0 6.2 %collective-permute-start.3 = (f32[64,512]{1,0:T(8,128)S(1)}, f32[64,512]{1,0:T(8,128)S(1)}, u32[]{:S(2)}, u32[]{:S(2)}) collective-permute-start(f32[64,512]{1,0:T(8,128)S(1)} %add.12), channel_id=1, source_target_pairs={{0,192},{64,0},{128,64},{192,128},{1,193},{65,1},{129,65},{193,129... | collective-permute-start | bytes 393224 | tf_op jit(solution)/shard_map/ppermute | solution.py:42
  7.0 9.3 %collective-permute-start.2 = (f32[64,512]{1,0:T(8,128)S(1)}, f32[64,512]{1,0:T(8,128)S(1)}, u32[]{:S(2)}, u32[]{:S(2)}) collective-permute-start(f32[64,512]{1,0:T(8,128)S(1)} %add.12), channel_id=1, source_target_pairs={{0,64},{64,128},{128,192},{192,0},{1,65},{65,129},{129,193},{193,1... | collective-permute-start | bytes 393224 | tf_op jit(solution)/shard_map/ppermute | solution.py:42
  7.1 9.3 %collective-permute-start.1 = (f32[64,512]{1,0:T(8,128)S(1)}, f32[64,512]{1,0:T(8,128)S(1)}, u32[]{:S(2)}, u32[]{:S(2)}) collective-permute-start(f32[64,512]{1,0:T(8,128)S(1)} %add.12), channel_id=1, source_target_pairs={{0,128},{64,192},{128,0},{192,64},{1,129},{65,193},{129,1},{193,65... | collective-permute-start | bytes 393224 | tf_op jit(solution)/shard_map/ppermute | solution.py:42
  16.4 6.2 %collective-permute-start.7 = (f32[64,512]{1,0:T(8,128)S(1)}, f32[64,512]{1,0:T(8,128)S(1)}, u32[]{:S(2)}, u32[]{:S(2)}) collective-permute-start(f32[64,512]{1,0:T(8,128)S(1)} %add_add_fusion.mine), channel_id=1, source_target_pairs={{0,8},{8,16},{16,24},{24,0},{1,9},{9,17},{17,25},{25,1},{2,10},{10... | collective-permute-start | bytes 393224 | tf_op jit(solution)/shard_map/ppermute | solution.py:42
  16.9 8.7 %collective-permute-start.6 = (f32[64,512]{1,0:T(8,128)S(1)}, f32[64,512]{1,0:T(8,128)S(1)}, u32[]{:S(2)}, u32[]{:S(2)}) collective-permute-start(f32[64,512]{1,0:T(8,128)S(1)} %add_add_fusion.mine), channel_id=1, source_target_pairs={{0,24},{8,0},{16,8},{24,16},{1,25},{9,1},{17,9},{25,17},{2,26},{10... | collective-permute-start | bytes 393224 | tf_op jit(solution)/shard_map/ppermute | solution.py:42
  18.5 7.1 %collective-permute-start.4 = (f32[64,512]{1,0:T(8,128)S(1)}, f32[64,512]{1,0:T(8,128)S(1)}, u32[]{:S(2)}, u32[]{:S(2)}) collective-permute-start(f32[64,512]{1,0:T(8,128)S(1)} %add_add_fusion.mine), channel_id=1, source_target_pairs={{0,16},{8,24},{16,0},{24,8},{1,17},{9,25},{17,1},{25,9},{2,18},{10... | collective-permute-start | bytes 393224 | tf_op jit(solution)/shard_map/ppermute | solution.py:42
  19.9 6.2 %collective-permute-start.10 = (f32[64,512]{1,0:T(8,128)S(1)}, f32[64,512]{1,0:T(8,128)S(1)}, u32[]{:S(2)}, u32[]{:S(2)}) collective-permute-start(f32[64,512]{1,0:T(8,128)S(1)} %add_add_fusion.mine), channel_id=1, source_target_pairs={{0,32},{32,0},{1,33},{33,1},{2,34},{34,2},{3,35},{35,3},{4,36},{36... | collective-permute-start | bytes 393224 | tf_op jit(solution)/shard_map/ppermute | solution.py:37
  22.6 6.5 %collective-permute-start.9 = (f32[64,512]{1,0:T(8,128)S(1)}, f32[64,512]{1,0:T(8,128)S(1)}, u32[]{:S(2)}, u32[]{:S(2)}) collective-permute-start(f32[64,512]{1,0:T(8,128)S(1)} %collective-permute-done.7.rest_1_), channel_id=1, source_target_pairs={{0,32},{32,0},{1,33},{33,1},{2,34},{34,2},{3,35},{35,3},{4,36},{36... | collective-permute-start | bytes 393224 | tf_op jit(solution)/shard_map/ppermute | solution.py:37
  25.6 3.5 %collective-permute-start.8 = (f32[64,512]{1,0:T(8,128)S(1)}, f32[64,512]{1,0:T(8,128)S(1)}, u32[]{:S(2)}, u32[]{:S(2)}) collective-permute-start(f32[64,512]{1,0:T(8,128)S(1)} %collective-permute-done.6.rest_0_), channel_id=1, source_target_pairs={{0,32},{32,0},{1,33},{33,1},{2,34},{34,2},{3,35},{35,3},{4,36},{36... | collective-permute-start | bytes 393224 | tf_op jit(solution)/shard_map/ppermute | solution.py:37
  25.6 8.7 %collective-permute-start.5 = (f32[64,512]{1,0:T(8,128)S(1)}, f32[64,512]{1,0:T(8,128)S(1)}, u32[]{:S(2)}, u32[]{:S(2)}) collective-permute-start(f32[64,512]{1,0:T(8,128)S(1)} %collective-permute-done.4.rest_0_), channel_id=1, source_target_pairs={{0,32},{32,0},{1,33},{33,1},{2,34},{34,2},{3,35},{35,3},{4,36},{36... | collective-permute-start | bytes 393224 | tf_op jit(solution)/shard_map/ppermute | solution.py:37
  88.7 10.4 %collective-permute-start.11 = (f32[616,128]{1,0:T(8,128)S(1)}, f32[616,128]{1,0:T(8,128)S(1)}, u32[]{:S(2)}, u32[]{:S(2)}) collective-permute-start(f32[616,128]{1,0:T(8,128)S(1)} %get-tuple-element.40.refs_0_), channel_id=1, source_target_pairs={{0,8},{8,16},{16,24},{24,0},{1,9},{9,17},{17,25},{25,1},{2,10},{10... | collective-permute-start | bytes 946184 | tf_op jit(solution)/shard_map/ppermute | solution.py:42
  91.3 11.5 %collective-permute-start.14 = (f32[616,128]{1,0:T(8,128)S(1)}, f32[616,128]{1,0:T(8,128)S(1)}, u32[]{:S(2)}, u32[]{:S(2)}) collective-permute-start(f32[616,128]{1,0:T(8,128)S(1)} %get-tuple-element.41.refs_1_), channel_id=1, source_target_pairs={{0,24},{8,0},{16,8},{24,16},{1,25},{9,1},{17,9},{25,17},{2,26},{10... | collective-permute-start | bytes 946184 | tf_op jit(solution)/shard_map/ppermute | solution.py:42
  91.3 18.3 %collective-permute-start.13 = (f32[616,128]{1,0:T(8,128)S(1)}, f32[616,128]{1,0:T(8,128)S(1)}, u32[]{:S(2)}, u32[]{:S(2)}) collective-permute-start(f32[616,128]{1,0:T(8,128)S(1)} %get-tuple-element.40.refs_0_), channel_id=1, source_target_pairs={{0,24},{8,0},{16,8},{24,16},{1,25},{9,1},{17,9},{25,17},{2,26},{10... | collective-permute-start | bytes 946184 | tf_op jit(solution)/shard_map/ppermute | solution.py:42
  92.2 17.4 %collective-permute-start.12 = (f32[616,128]{1,0:T(8,128)S(1)}, f32[616,128]{1,0:T(8,128)S(1)}, u32[]{:S(2)}, u32[]{:S(2)}) collective-permute-start(f32[616,128]{1,0:T(8,128)S(1)} %get-tuple-element.41.refs_1_), channel_id=1, source_target_pairs={{0,8},{8,16},{16,24},{24,0},{1,9},{9,17},{17,25},{25,1},{2,10},{10... | collective-permute-start | bytes 946184 | tf_op jit(solution)/shard_map/ppermute | solution.py:42
  99.2 11.8 %collective-permute-start.15 = (f32[616,128]{1,0:T(8,128)S(1)}, f32[616,128]{1,0:T(8,128)S(1)}, u32[]{:S(2)}, u32[]{:S(2)}) collective-permute-start(f32[616,128]{1,0:T(8,128)S(1)} %collective-permute-done.11.refs_2_), channel_id=1, source_target_pairs={{0,8},{8,16},{16,24},{24,0},{1,9},{9,17},{17,25},{25,1},{2,10},{10... | collective-permute-start | bytes 946184 | tf_op jit(solution)/shard_map/ppermute | solution.py:42
  102.9 11.5 %collective-permute-start.16 = (f32[616,128]{1,0:T(8,128)S(1)}, f32[616,128]{1,0:T(8,128)S(1)}, u32[]{:S(2)}, u32[]{:S(2)}) collective-permute-start(f32[616,128]{1,0:T(8,128)S(1)} %collective-permute-done.14.refs_5_), channel_id=1, source_target_pairs={{0,24},{8,0},{16,8},{24,16},{1,25},{9,1},{17,9},{25,17},{2,26},{10... | collective-permute-start | bytes 946184 | tf_op jit(solution)/shard_map/ppermute | solution.py:42

commit v7 on v6

--- a/solution.py
+++ b/solution.py
@@ -439,43 +439,56 @@
 
 
 def lay_kernel(*refs):
-    pieces, (gram_out, side_out, tails, sides) = refs[:8], refs[8:]
+    pieces, (gram_out, side_out, staged, edge, side, tails, sides, done) = refs[:8], refs[8:]
     x = lax.axis_index("x")
-
-    def put(source, parts):
+    copies = []
+
+    def send(value, target):
+        copies.append(pltpu.make_async_copy(value, target, done.at[len(copies)]))
+        copies[-1].start()
+
+    for index, by in enumerate((0, 3, 1, 2)):
+        source = (x + by) % 4
+        parts = [(pieces[2 * index], 0, OUT_HALF), (pieces[2 * index + 1], OUT_HALF, OUT_ROWS)]
         for k in range(COLS // 128):
             first = k * ROWS_PAD
-            lanes = pl.ds(pl.multiple_of((source * 4 + k) * 128, 128), 128)
             for part, low, high in parts:
                 begin, end = max(first, low), min(first + ROWS, high)
                 if begin < end:
-                    gram_out[begin - first : end - first, lanes] = part[begin - low : end - low, :]
+                    staged[index, begin - first : end - first, k * 128 : (k + 1) * 128] = part[begin - low : end - low, :]
+        send(staged.at[index], gram_out.at[:, pl.ds(pl.multiple_of(source * COLS, COLS), COLS)])
         for part, low, high in parts:
             begin, end = max(OUT_TAIL, low), min(OUT_ROWS, high)
             if begin < end:
                 tails[source, begin - OUT_TAIL : end - OUT_TAIL, :] = part[begin - low : end - low, :]
-
-    for by, top, bottom in zip((0, 3, 1, 2), pieces[::2], pieces[1::2]):
-        put((x + by) % 4, [(top, 0, OUT_HALF), (bottom, OUT_HALF, OUT_ROWS)])
     sides[...] = jnp.zeros_like(sides)
     for x_of, low, high in ((0, 0, 128), (1, 128, ROWS)):
         count = high - low
-        gram_out[low:high, 16 * 128 :] = tails[x_of, :count, :TAIL_QUADS]
+        edge[low:high, :] = tails[x_of, :count, :TAIL_QUADS]
         sides[low:high, :TAIL_SIDES] = tails[x_of, :count, TAIL_QUADS:]
         sides[low:high, TAIL_SIDES:R] = tails[x_of + 2, :count, TAIL_QUADS:]
-    side_out[...] = sides[...].T[:R, :ROWS]
+    send(edge, gram_out.at[:, pl.ds(4 * COLS, TAIL_QUADS)])
+    side[...] = sides[...].T[:R, :ROWS]
+    send(side, side_out)
+    for copy in copies:
+        copy.wait()
 
 
 def lay(*pieces):
+    whole = pl.BlockSpec(memory_space=pltpu.HBM)
     return pl.pallas_call(
         lay_kernel,
-        out_shape=(
-            jax.ShapeDtypeStruct((ROWS, FEAT), jnp.float32),
-            jax.ShapeDtypeStruct((R, ROWS), jnp.float32),
-        ),
+        out_shape=(pltpu.HBM((ROWS, FEAT), jnp.float32), pltpu.HBM((R, ROWS), jnp.float32)),
         in_specs=[VMEM] * 8,
-        out_specs=(VMEM, VMEM),
-        scratch_shapes=[pltpu.VMEM((4, TAIL_ROWS, 128), jnp.float32), pltpu.VMEM((384, 128), jnp.float32)],
+        out_specs=(whole, whole),
+        scratch_shapes=[
+            pltpu.VMEM((4, ROWS, COLS), jnp.float32),
+            pltpu.VMEM((ROWS, TAIL_QUADS), jnp.float32),
+            pltpu.VMEM((R, ROWS), jnp.float32),
+            pltpu.VMEM((4, TAIL_ROWS, 128), jnp.float32),
+            pltpu.VMEM((384, 128), jnp.float32),
+            pltpu.SemaphoreType.DMA((6,)),
+        ],
         compiler_params=ROOM,
         name="lay",
     )(*[near_by(v) for v in pieces])

time: 116 us -> 116 us (level)
  no operation moved by 1% of the time
where the time goes in v7:
time: 116 us
  blocking collectives  50 us (43%)
  waiting for transfers between devices  29.5 us (25%)
  starting transfers between devices  19 us (16%)
  Pallas kernels  16.8 us (14%)
    ppermute x12, waiting for transfers between devices, turn(): lax.ppermute(value, axis, [(i, (i + by) % count) for i in range(count)])  28.1 us
    all_to_all x1, blocking collectives, shards(): lax.all_to_all(block.reshape(8, PIECE, 128), 'z', 0, 0, tiled=True)  28 us
    all_to_all x1, blocking collectives, everyone(): return lax.all_to_all(spread, axis, 0, 0, tiled=True)  21.9 us
    ppermute x12, starting transfers between devices, turn(): lax.ppermute(value, axis, [(i, (i + by) % count) for i in range(count)])  18.4 us
    pallas_call x1, Pallas kernels, gram(): beside(lengths, *kept, *[near_by(v) for v in (mine[1], mine[3], theirs[1]...  5.16 us
    pallas_call x1, Pallas kernels, gram(): across(lengths, *kept, *[near_by(v) for v in (mine[2], theirs[2], *sums)])  3.06 us
    pallas_call x1, Pallas kernels, gram(): sums = own(lengths, *kept, near_by(mine[0]), near_by(theirs[0]))  2.99 us
  transfers between devices with their start and end apart: 17, of which 9 were waited for; matrix products, arithmetic and copies ran while one was open for 0% of the time, Pallas kernels for 8%

profile of v7, /device:TPU:6, one launch (start us, length us, event | category | flops | bytes accessed | tf_op | source)
XLA Modules:
  0.0 116.2 jit_solution(16195170793526929210)
XLA Ops:
  0.6 0.0 copy-start
  0.6 1.9 %project.1 = (f32[64,512]{1,0:T(8,128)S(1)}, f32[64,512]{1,0:T(8,128)S(1)}) custom-call(bf16[64,1024]{1,0:T(8,128)(2,1)} %bitcast.4, bf16[1024,1024]{1,0:T(8,128)(2,1)} %snapshots.1), custom_call_target="tpu_custom_call" | custom-call | tf_op jit(solution)/shard_map/project/pallas_call | solution.py:180
  2.5 0.1 collective-permute-start
  2.6 1.3 %collective-permute-done = f32[64,512]{1,0:T(8,128)S(1)} collective-permute-done((f32[64,512]{1,0:T(8,128)S(1)}, f32[64,512]{1,0:T(8,128)S(1)}, u32[]{:S(2)}, u32[]{:S(2)}) %collective-permute-start) | collective-permute-done | bytes 131104 | tf_op jit(solution)/shard_map/ppermute | solution.py:37
  4.0 3.1 %collective-permute-start.3 = (f32[64,512]{1,0:T(8,128)S(1)}, f32[64,512]{1,0:T(8,128)S(1)}, u32[]{:S(2)}, u32[]{:S(2)}) collective-permute-start(f32[64,512]{1,0:T(8,128)S(1)} %add.12), channel_id=1, source_target_pairs={{0,192},{64,0},{128,64},{192,128},{1,193},{65,1},{129,65},{193,129... | collective-permute-start | bytes 393224 | tf_op jit(solution)/shard_map/ppermute | solution.py:42
  7.0 0.0 collective-permute-start.2
  7.1 2.2 %collective-permute-start.1 = (f32[64,512]{1,0:T(8,128)S(1)}, f32[64,512]{1,0:T(8,128)S(1)}, u32[]{:S(2)}, u32[]{:S(2)}) collective-permute-start(f32[64,512]{1,0:T(8,128)S(1)} %add.12), channel_id=1, source_target_pairs={{0,128},{64,192},{128,0},{192,64},{1,129},{65,193},{129,1},{193,65... | collective-permute-start | bytes 393224 | tf_op jit(solution)/shard_map/ppermute | solution.py:42
  9.3 0.7 picks.1
  10.0 0.2 collective-permute-done.3
  10.1 6.2 %collective-permute-done.2 = f32[64,512]{1,0:T(8,128)S(1)} collective-permute-done((f32[64,512]{1,0:T(8,128)S(1)}, f32[64,512]{1,0:T(8,128)S(1)}, u32[]{:S(2)}, u32[]{:S(2)}) %collective-permute-start.2) | collective-permute-done | bytes 131104 | tf_op jit(solution)/shard_map/ppermute | solution.py:42
  16.3 0.0 collective-permute-done.1
  16.4 0.6 collective-permute-start.7
  16.9 1.5 %collective-permute-start.6 = (f32[64,512]{1,0:T(8,128)S(1)}, f32[64,512]{1,0:T(8,128)S(1)}, u32[]{:S(2)}, u32[]{:S(2)}) collective-permute-start(f32[64,512]{1,0:T(8,128)S(1)} %add_add_fusion.mine), channel_id=1, source_target_pairs={{0,24},{8,0},{16,8},{24,16},{1,25},{9,1},{17,9},{25,17},{2,26},{10... | collective-permute-start | bytes 393224 | tf_op jit(solution)/shard_map/ppermute | solution.py:42
  18.5 1.4 %collective-permute-start.4 = (f32[64,512]{1,0:T(8,128)S(1)}, f32[64,512]{1,0:T(8,128)S(1)}, u32[]{:S(2)}, u32[]{:S(2)}) collective-permute-start(f32[64,512]{1,0:T(8,128)S(1)} %add_add_fusion.mine), channel_id=1, source_target_pairs={{0,16},{8,24},{16,0},{24,8},{1,17},{9,25},{17,1},{25,9},{2,18},{10... | collective-permute-start | bytes 393224 | tf_op jit(solution)/shard_map/ppermute | solution.py:42
  19.9 0.0 collective-permute-start.10
  19.9 2.7 %collective-permute-done.7.rest_1_ = f32[64,512]{1,0:T(8,128)S(1)} collective-permute-done((f32[64,512]{1,0:T(8,128)S(1)}, f32[64,512]{1,0:T(8,128)S(1)}, u32[]{:S(2)}, u32[]{:S(2)}) %collective-permute-start.7) | collective-permute-done | bytes 131104 | tf_op jit(solution)/shard_map/ppermute | solution.py:42
  22.6 0.0 collective-permute-start.9
  22.6 3.0 %collective-permute-done.6.rest_0_ = f32[64,512]{1,0:T(8,128)S(1)} collective-permute-done((f32[64,512]{1,0:T(8,128)S(1)}, f32[64,512]{1,0:T(8,128)S(1)}, u32[]{:S(2)}, u32[]{:S(2)}) %collective-permute-start.6) | collective-permute-done | bytes 131104 | tf_op jit(solution)/shard_map/ppermute | solution.py:42
  25.6 0.0 collective-permute-start.8
  25.6 0.0 collective-permute-done.4.rest_0_
  25.6 0.5 collective-permute-start.5
  26.1 0.0 collective-permute-done.10.theirs
  26.1 0.0 copy-done
  26.1 3.0 %gram_own.1 = (f32[272,512]{1,0:T(8,128)S(1)}, f32[144,128]{1,0:T(8,128)S(1)}, f32[64,128]{1,0:T(8,128)S(1)}, f32[64,128]{1,0:T(8,128)S(1)}) custom-call(s32[16]{0:T(128)S(1)} %copy-done, bf16[880,256]{1,0:T(8,128)(2,1)S(1)} %get-tuple-element.27.first_pick, bf16[880,256]{1,0:T(8,128)(2,1)S(1)} %get-tuple-element.28.second_pick, ...), custom_call_target="tpu_custom_call" | custom-call | tf_op jit(solution)/shard_map/gram_own/pallas_call | solution.py:322
  29.1 0.0 collective-permute-done.9.rest_3_
  29.1 0.0 collective-permute-done.8.rest_2_
  29.1 5.2 %gram_beside.1 = (f32[272,512]{1,0:T(8,128)S(1)}, f32[144,128]{1,0:T(8,128)S(1)}, f32[64,128]{1,0:T(8,128)S(1)}, f32[64,128]{1,0:T(8,128)S(1)}) custom-call(s32[16]{0:T(128)S(1)} %copy-done, bf16[880,256]{1,0:T(8,128)(2,1)S(1)} %get-tuple-element.27.first_pick, ...), custom_call_target="tpu_custom_call", output_to_operand_aliasing={{0}: (7, {}), {1}: (8, {}), {2}: (9, {}), {3}: (10, {})} | custom-call | tf_op jit(solution)/shard_map/gram_beside/pallas_call | solution.py:323
  34.3 0.0 collective-permute-done.5.rest_1_
  34.3 3.1 %gram_across.1 = (f32[1216,128]{1,0:T(8,128)S(1)}, f32[8,128]{1,0:T(8,128)S(1)}) custom-call(s32[16]{0:T(128)S(1)} %copy-done, bf16[880,256]{1,0:T(8,128)(2,1)S(1)} %get-tuple-element.27.first_pick, bf16[880,256]{1,0:T(8,128)(2,1)S(1)} %get-tuple-element.28.second_pick, f32[64,512]{1,0:T(8,128)S(1)} %collective-permute-done.4.rest_0_, ...), custom_call_target="tpu_custom_call" | custom-call | tf_op jit(solution)/shard_map/gram_across/pallas_call | solution.py:324
  37.4 28.0 %all_to_all.10.parts = f32[8,152,128]{2,1,0:T(8,128)S(1)} all-to-all(f32[8,152,128]{2,1,0:T(8,128)S(1)} %bitcast.3), channel_id=1, replica_groups=mesh['y'=4,'c'=2,'x'=4,'z'=8] {'z'}, dimensions={0} | all-to-all | bytes 1245184 | tf_op jit(solution)/shard_map/all_to_all | solution.py:515
  65.5 21.9 %all_to_all.11.parts = f32[8,160,128]{2,1,0:T(8,128)S(1)} all-to-all(f32[8,160,128]{2,1,0:T(8,128)S(1)} %broadcast_in_dim.2), channel_id=1, replica_groups=mesh['y'=4,'c'=2,'x'=4,'z'=8] {'z'}, dimensions={0} | all-to-all | bytes 1310720 | tf_op jit(solution)/shard_map/all_to_all | solution.py:52
  87.5 1.3 %scale.1 = (f32[616,128]{1,0:T(8,128)S(1)}, f32[616,128]{1,0:T(8,128)S(1)}) custom-call(s32[16]{0:T(128)S(1)} %copy-done, bf16[880,256]{1,0:T(8,128)(2,1)S(1)} %get-tuple-element.27.first_pick, bf16[880,256]{1,0:T(8,128)(2,1)S(1)} %get-tuple-element.28.second_pick, f32[8,160,128]{2,1,0:T(8,128)S(1)} %all_to_all.11.parts), custom_call_target="tpu_custom_call" | custom-call | tf_op jit(solution)/shard_map/scale/pallas_call | solution.py:426
  88.7 2.6 %collective-permute-start.11 = (f32[616,128]{1,0:T(8,128)S(1)}, f32[616,128]{1,0:T(8,128)S(1)}, u32[]{:S(2)}, u32[]{:S(2)}) collective-permute-start(f32[616,128]{1,0:T(8,128)S(1)} %get-tuple-element.40.refs_0_), channel_id=1, source_target_pairs={{0,8},{8,16},{16,24},{24,0},{1,9},{9,17},{17,25},{25,1},{2,10},{10... | collective-permute-start | bytes 946184 | tf_op jit(solution)/shard_map/ppermute | solution.py:42
  91.3 0.0 collective-permute-start.14
  91.3 0.9 collective-permute-start.13
  92.2 2.4 %collective-permute-start.12 = (f32[616,128]{1,0:T(8,128)S(1)}, f32[616,128]{1,0:T(8,128)S(1)}, u32[]{:S(2)}, u32[]{:S(2)}) collective-permute-start(f32[616,128]{1,0:T(8,128)S(1)} %get-tuple-element.41.refs_1_), channel_id=1, source_target_pairs={{0,8},{8,16},{16,24},{24,0},{1,9},{9,17},{17,25},{25,1},{2,10},{10... | collective-permute-start | bytes 946184 | tf_op jit(solution)/shard_map/ppermute | solution.py:42
  94.6 4.6 %collective-permute-done.11.refs_2_ = f32[616,128]{1,0:T(8,128)S(1)} collective-permute-done((f32[616,128]{1,0:T(8,128)S(1)}, f32[616,128]{1,0:T(8,128)S(1)}, u32[]{:S(2)}, u32[]{:S(2)}) %collective-permute-start.11) | collective-permute-done | bytes 315424 | tf_op jit(solution)/shard_map/ppermute | solution.py:42
  99.2 3.7 %collective-permute-start.15 = (f32[616,128]{1,0:T(8,128)S(1)}, f32[616,128]{1,0:T(8,128)S(1)}, u32[]{:S(2)}, u32[]{:S(2)}) collective-permute-start(f32[616,128]{1,0:T(8,128)S(1)} %collective-permute-done.11.refs_2_), channel_id=1, source_target_pairs={{0,8},{8,16},{16,24},{24,0},{1,9},{9,17},{17,25},{25,1},{2,10},{10... | collective-permute-start | bytes 946184 | tf_op jit(solution)/shard_map/ppermute | solution.py:42
  102.9 0.0 collective-permute-done.14.refs_5_
  102.9 0.0 collective-permute-start.16
  102.9 6.8 %collective-permute-done.13.refs_4_ = f32[616,128]{1,0:T(8,128)S(1)} collective-permute-done((f32[616,128]{1,0:T(8,128)S(1)}, f32[616,128]{1,0:T(8,128)S(1)}, u32[]{:S(2)}, u32[]{:S(2)}) %collective-permute-start.13) | collective-permute-done | bytes 315424 | tf_op jit(solution)/shard_map/ppermute | solution.py:42
  109.6 0.0 collective-permute-done.12.refs_3_
  109.6 1.3 %collective-permute-done.15.refs_6_ = f32[616,128]{1,0:T(8,128)S(1)} collective-permute-done((f32[616,128]{1,0:T(8,128)S(1)}, f32[616,128]{1,0:T(8,128)S(1)}, u32[]{:S(2)}, u32[]{:S(2)}) %collective-permute-start.15) | collective-permute-done | bytes 315424 | tf_op jit(solution)/shard_map/ppermute | solution.py:42
  110.9 3.4 %collective-permute-done.16.refs_7_ = f32[616,128]{1,0:T(8,128)S(1)} collective-permute-done((f32[616,128]{1,0:T(8,128)S(1)}, f32[616,128]{1,0:T(8,128)S(1)}, u32[]{:S(2)}, u32[]{:S(2)}) %collective-permute-start.16) | collective-permute-done | bytes 315424 | tf_op jit(solution)/shard_map/ppermute | solution.py:42
  114.4 1.7 %lay.1 = (f32[268,2144]{1,0:T(8,128)}, f32[64,268]{1,0:T(8,128)}) custom-call(f32[616,128]{1,0:T(8,128)S(1)} %get-tuple-element.40.refs_0_, f32[616,128]{1,0:T(8,128)S(1)} %get-tuple-element.41.refs_1_, f32[616,128]{1,0:T(8,128)S(1)} %collective-permute-done.11.refs_2_, f32[616,128]{1,0:T(8,128)S(1)} %collective-permute-done.12.refs_3_, ...), custom_call_target="tpu_custom_call" | custom-call | tf_op jit(solution)/shard_map/lay/pallas_call | solution.py:479
  (4 shorter events, 0.1 us)
Async XLA Ops:
  0.6 25.5 %copy-start = (s32[16]{0:T(128)S(1)}, s32[16]{0:T(128)}, u32[]{:S(2)}) copy-start(s32[16]{0:T(128)} %lengths.7) | copy-start | bytes 196
  2.5 1.4 %collective-permute-start = (f32[64,512]{1,0:T(8,128)S(1)}, f32[64,512]{1,0:T(8,128)S(1)}, u32[]{:S(2)}, u32[]{:S(2)}) collective-permute-start(f32[64,512]{1,0:T(8,128)S(1)} %get-tuple-element.24), channel_id=1, source_target_pairs={{0,32},{32,0},{1,33},{33,1},{2,34},{34,2},{3,35},{35,3},{4,36},{36... | collective-permute-start | bytes 393224 | tf_op jit(solution)/shard_map/ppermute | solution.py:37
  4.0 6.2 %collective-permute-start.3 = (f32[64,512]{1,0:T(8,128)S(1)}, f32[64,512]{1,0:T(8,128)S(1)}, u32[]{:S(2)}, u32[]{:S(2)}) collective-permute-start(f32[64,512]{1,0:T(8,128)S(1)} %add.12), channel_id=1, source_target_pairs={{0,192},{64,0},{128,64},{192,128},{1,193},{65,1},{129,65},{193,129... | collective-permute-start | bytes 393224 | tf_op jit(solution)/shard_map/ppermute | solution.py:42
  7.0 9.3 %collective-permute-start.2 = (f32[64,512]{1,0:T(8,128)S(1)}, f32[64,512]{1,0:T(8,128)S(1)}, u32[]{:S(2)}, u32[]{:S(2)}) collective-permute-start(f32[64,512]{1,0:T(8,128)S(1)} %add.12), channel_id=1, source_target_pairs={{0,64},{64,128},{128,192},{192,0},{1,65},{65,129},{129,193},{193,1... | collective-permute-start | bytes 393224 | tf_op jit(solution)/shard_map/ppermute | solution.py:42
  7.1 9.3 %collective-permute-start.1 = (f32[64,512]{1,0:T(8,128)S(1)}, f32[64,512]{1,0:T(8,128)S(1)}, u32[]{:S(2)}, u32[]{:S(2)}) collective-permute-start(f32[64,512]{1,0:T(8,128)S(1)} %add.12), channel_id=1, source_target_pairs={{0,128},{64,192},{128,0},{192,64},{1,129},{65,193},{129,1},{193,65... | collective-permute-start | bytes 393224 | tf_op jit(solution)/shard_map/ppermute | solution.py:42
  16.4 6.2 %collective-permute-start.7 = (f32[64,512]{1,0:T(8,128)S(1)}, f32[64,512]{1,0:T(8,128)S(1)}, u32[]{:S(2)}, u32[]{:S(2)}) collective-permute-start(f32[64,512]{1,0:T(8,128)S(1)} %add_add_fusion.mine), channel_id=1, source_target_pairs={{0,8},{8,16},{16,24},{24,0},{1,9},{9,17},{17,25},{25,1},{2,10},{10... | collective-permute-start | bytes 393224 | tf_op jit(solution)/shard_map/ppermute | solution.py:42
  16.9 8.7 %collective-permute-start.6 = (f32[64,512]{1,0:T(8,128)S(1)}, f32[64,512]{1,0:T(8,128)S(1)}, u32[]{:S(2)}, u32[]{:S(2)}) collective-permute-start(f32[64,512]{1,0:T(8,128)S(1)} %add_add_fusion.mine), channel_id=1, source_target_pairs={{0,24},{8,0},{16,8},{24,16},{1,25},{9,1},{17,9},{25,17},{2,26},{10... | collective-permute-start | bytes 393224 | tf_op jit(solution)/shard_map/ppermute | solution.py:42
  18.5 7.1 %collective-permute-start.4 = (f32[64,512]{1,0:T(8,128)S(1)}, f32[64,512]{1,0:T(8,128)S(1)}, u32[]{:S(2)}, u32[]{:S(2)}) collective-permute-start(f32[64,512]{1,0:T(8,128)S(1)} %add_add_fusion.mine), channel_id=1, source_target_pairs={{0,16},{8,24},{16,0},{24,8},{1,17},{9,25},{17,1},{25,9},{2,18},{10... | collective-permute-start | bytes 393224 | tf_op jit(solution)/shard_map/ppermute | solution.py:42
  19.9 6.2 %collective-permute-start.10 = (f32[64,512]{1,0:T(8,128)S(1)}, f32[64,512]{1,0:T(8,128)S(1)}, u32[]{:S(2)}, u32[]{:S(2)}) collective-permute-start(f32[64,512]{1,0:T(8,128)S(1)} %add_add_fusion.mine), channel_id=1, source_target_pairs={{0,32},{32,0},{1,33},{33,1},{2,34},{34,2},{3,35},{35,3},{4,36},{36... | collective-permute-start | bytes 393224 | tf_op jit(solution)/shard_map/ppermute | solution.py:37
  22.6 6.5 %collective-permute-start.9 = (f32[64,512]{1,0:T(8,128)S(1)}, f32[64,512]{1,0:T(8,128)S(1)}, u32[]{:S(2)}, u32[]{:S(2)}) collective-permute-start(f32[64,512]{1,0:T(8,128)S(1)} %collective-permute-done.7.rest_1_), channel_id=1, source_target_pairs={{0,32},{32,0},{1,33},{33,1},{2,34},{34,2},{3,35},{35,3},{4,36},{36... | collective-permute-start | bytes 393224 | tf_op jit(solution)/shard_map/ppermute | solution.py:37
  25.6 3.5 %collective-permute-start.8 = (f32[64,512]{1,0:T(8,128)S(1)}, f32[64,512]{1,0:T(8,128)S(1)}, u32[]{:S(2)}, u32[]{:S(2)}) collective-permute-start(f32[64,512]{1,0:T(8,128)S(1)} %collective-permute-done.6.rest_0_), channel_id=1, source_target_pairs={{0,32},{32,0},{1,33},{33,1},{2,34},{34,2},{3,35},{35,3},{4,36},{36... | collective-permute-start | bytes 393224 | tf_op jit(solution)/shard_map/ppermute | solution.py:37
  25.6 8.7 %collective-permute-start.5 = (f32[64,512]{1,0:T(8,128)S(1)}, f32[64,512]{1,0:T(8,128)S(1)}, u32[]{:S(2)}, u32[]{:S(2)}) collective-permute-start(f32[64,512]{1,0:T(8,128)S(1)} %collective-permute-done.4.rest_0_), channel_id=1, source_target_pairs={{0,32},{32,0},{1,33},{33,1},{2,34},{34,2},{3,35},{35,3},{4,36},{36... | collective-permute-start | bytes 393224 | tf_op jit(solution)/shard_map/ppermute | solution.py:37
  88.7 10.4 %collective-permute-start.11 = (f32[616,128]{1,0:T(8,128)S(1)}, f32[616,128]{1,0:T(8,128)S(1)}, u32[]{:S(2)}, u32[]{:S(2)}) collective-permute-start(f32[616,128]{1,0:T(8,128)S(1)} %get-tuple-element.40.refs_0_), channel_id=1, source_target_pairs={{0,8},{8,16},{16,24},{24,0},{1,9},{9,17},{17,25},{25,1},{2,10},{10... | collective-permute-start | bytes 946184 | tf_op jit(solution)/shard_map/ppermute | solution.py:42
  91.3 11.5 %collective-permute-start.14 = (f32[616,128]{1,0:T(8,128)S(1)}, f32[616,128]{1,0:T(8,128)S(1)}, u32[]{:S(2)}, u32[]{:S(2)}) collective-permute-start(f32[616,128]{1,0:T(8,128)S(1)} %get-tuple-element.41.refs_1_), channel_id=1, source_target_pairs={{0,24},{8,0},{16,8},{24,16},{1,25},{9,1},{17,9},{25,17},{2,26},{10... | collective-permute-start | bytes 946184 | tf_op jit(solution)/shard_map/ppermute | solution.py:42
  91.3 18.3 %collective-permute-start.13 = (f32[616,128]{1,0:T(8,128)S(1)}, f32[616,128]{1,0:T(8,128)S(1)}, u32[]{:S(2)}, u32[]{:S(2)}) collective-permute-start(f32[616,128]{1,0:T(8,128)S(1)} %get-tuple-element.40.refs_0_), channel_id=1, source_target_pairs={{0,24},{8,0},{16,8},{24,16},{1,25},{9,1},{17,9},{25,17},{2,26},{10... | collective-permute-start | bytes 946184 | tf_op jit(solution)/shard_map/ppermute | solution.py:42
  92.2 17.4 %collective-permute-start.12 = (f32[616,128]{1,0:T(8,128)S(1)}, f32[616,128]{1,0:T(8,128)S(1)}, u32[]{:S(2)}, u32[]{:S(2)}) collective-permute-start(f32[616,128]{1,0:T(8,128)S(1)} %get-tuple-element.41.refs_1_), channel_id=1, source_target_pairs={{0,8},{8,16},{16,24},{24,0},{1,9},{9,17},{17,25},{25,1},{2,10},{10... | collective-permute-start | bytes 946184 | tf_op jit(solution)/shard_map/ppermute | solution.py:42
  99.2 11.8 %collective-permute-start.15 = (f32[616,128]{1,0:T(8,128)S(1)}, f32[616,128]{1,0:T(8,128)S(1)}, u32[]{:S(2)}, u32[]{:S(2)}) collective-permute-start(f32[616,128]{1,0:T(8,128)S(1)} %collective-permute-done.11.refs_2_), channel_id=1, source_target_pairs={{0,8},{8,16},{16,24},{24,0},{1,9},{9,17},{17,25},{25,1},{2,10},{10... | collective-permute-start | bytes 946184 | tf_op jit(solution)/shard_map/ppermute | solution.py:42
  102.9 11.5 %collective-permute-start.16 = (f32[616,128]{1,0:T(8,128)S(1)}, f32[616,128]{1,0:T(8,128)S(1)}, u32[]{:S(2)}, u32[]{:S(2)}) collective-permute-start(f32[616,128]{1,0:T(8,128)S(1)} %collective-permute-done.14.refs_5_), channel_id=1, source_target_pairs={{0,24},{8,0},{16,8},{24,16},{1,25},{9,1},{17,9},{25,17},{2,26},{10... | collective-permute-start | bytes 946184 | tf_op jit(solution)/shard_map/ppermute | solution.py:42
